TPU v7x, 32 devices: a whole 2x2x4 slice. The times are simulated.
32 devices in a mesh: batch: 8 (over z, x), blk: 4 (over y, core).
Axes of the slice: x: 2, y: 2, z: 4, core: 2. Of those that a mesh axis runs over, the one named last changes fastest.
Arguments:
- inputs: bfloat16 [8, 2048, 1024], P('batch', 'blk'), may hold values from -6 to 6
- ln1_gain: float32 [1024], replicated, may hold values from 0.1 to 1.9
- ln1_bias: float32 [1024], replicated, may hold values from -1 to 1
- w_qkv: bfloat16 [1024, 3072], replicated, may hold values from -0.1875 to 0.1875
- bias_q: float32 [1024], replicated, may hold values from -1.5 to 1.5
- bias_v: float32 [1024], replicated, may hold values from -0.25 to 0.25
- w_out: bfloat16 [1024, 1024], replicated, may hold values from -2 to 2
- bias_out: float32 [1024], replicated, may hold values from -1 to 1
- ln2_gain: float32 [1024], replicated, may hold values from 0.1 to 1.9
- ln2_bias: float32 [1024], replicated, may hold values from -1 to 1
- w_up: bfloat16 [1024, 4096], replicated, may hold values from -0.1875 to 0.1875
- bias_up: float32 [4096], replicated, may hold values from -1.5 to 1.5
- w_down: bfloat16 [4096, 1024], replicated, may hold values from -0.09375 to 0.09375
- bias_down: float32 [1024], replicated, may hold values from -2.5 to 2.5
- lengths: int32 [8, 2, 3], P('batch'), may hold values from 1 to 640, as said below
- cotangent: bfloat16 [8, 2048, 1024], P('batch', 'blk'), may hold values from -6 to 6
Outputs:
- result: bfloat16 [8, 2048, 1024], P('batch', 'blk')
- grad_inputs: float32 [8, 2048, 1024], P('batch', 'blk')
- grad_ln1_gain: float32 [1024], P('batch')
- grad_ln1_bias: float32 [1024], P('batch')
- grad_w_qkv: float32 [1024, 3072], P('batch')
- grad_bias_q: float32 [1024], P('batch')
- grad_bias_v: float32 [1024], P('batch')
- grad_w_out: float32 [1024, 1024], P('batch')
- grad_bias_out: float32 [1024], P('batch')
- grad_ln2_gain: float32 [1024], P('batch')
- grad_ln2_bias: float32 [1024], P('batch')
- grad_w_up: float32 [1024, 4096], P('batch')
- grad_bias_up: float32 [4096], P('batch')
- grad_w_down: float32 [4096, 1024], P('batch')
- grad_bias_down: float32 [1024], P('batch')
Inputs may be any that keep to these rules, and one draw needn't show every extreme that they name: lengths[r, u] gives utterance u of row r as (phonemes, prompt frames, target frames), packed in order from slot 0; phonemes number 1 to 128, prompt frames 1 to 256, target frames 1 to 640; slots after a row's last utterance are padding.
All inputs are finite; a program needn't handle non-finite values.
Results may differ from a plain program's by a relative error of at most 0.018.
Values may be sent and summed in bfloat16 or wider, within the bound.
No kernel may reach another device: no remote copies, remote signals or barrier semaphores. Data moves between devices by JAX's collectives and lax.ppermute only.
A program may use at most 192 MiB of HBM per device.

v0:
```python
import functools

import jax
import jax.numpy as jnp
from jax import lax
from jax.experimental import pallas as pl
from jax.experimental.pallas import tpu as pltpu
from jax.sharding import Mesh
from jax.sharding import PartitionSpec as P

D = 1024
H = 16
HD = 64
EPS = 1e-05
NEG = -1e30
VM = 20
AV = 28
BF = jnp.bfloat16
F32 = jnp.float32


def layer_norm(values, gain_vec, shift_vec):
    center = values - jnp.mean(values, axis=-1, keepdims=True)
    spread = jnp.mean(center * center, axis=-1, keepdims=True)
    return center * lax.rsqrt(spread + EPS) * gain_vec + shift_vec


def dot(a, b):
    return jnp.dot(a, b, preferred_element_type=F32)


def dot_tn(a, b):
    return lax.dot_general(a, b, (((0,), (0,)), ((), ())), preferred_element_type=F32)


def dot_nt(a, b):
    return lax.dot_general(a, b, (((1,), (1,)), ((), ())), preferred_element_type=F32)


def half(a, h):
    a = a[:, (h // 2) * 2 * HD : (h // 2 + 1) * 2 * HD]
    lane = lax.broadcasted_iota(jnp.int32, a.shape, 1)
    zero = jnp.zeros_like(a)
    return jnp.where(lane < HD, a, zero) if h % 2 == 0 else jnp.where(lane < HD, zero, a)


def pair(a, h):
    return a[:, (h // 2) * 2 * HD : (h // 2 + 1) * 2 * HD]


def fwd_kernel(T, HG, lst, cnt, base, q_ref, k_ref, v_ref, lo_ref, hi_ref, ctx_ref, lse_ref):
    nq = q_ref.shape[0] // T
    row = lax.broadcasted_iota(jnp.int32, (T, T), 0)

    @pl.loop(0, nq)
    def _(qt):
        at = pl.ds(pl.multiple_of(qt * T, T), T)
        q = q_ref[at, :]
        qh = [half(q, h) for h in range(HG)]
        lo, hi = lo_ref[:, at], hi_ref[:, at]

        def body(n, carry):
            t = lst[qt, n]
            ks = pl.ds(pl.multiple_of(t * T, T), T)
            k, v = k_ref[ks, :], v_ref[ks, :].T
            vis = (row >= lo - base[t]) & (row < hi - base[t])
            raw = [dot_nt(pair(k, h), qh[h]) for h in range(HG)]
            out = []
            for h in range(HG):
                m, l, acc = carry[h]
                s = jnp.where(vis, raw[h], NEG)
                mn = jnp.maximum(m, jnp.max(s, axis=0, keepdims=True))
                a = jnp.exp(m - mn)
                p = jnp.exp(s - mn)
                l = a * l + jnp.sum(p, axis=0, keepdims=True)
                acc = acc * a + dot(v[h * HD : (h + 1) * HD, :], p.astype(BF))
                out.append((mn, l, acc))
            return tuple(out)

        one = (jnp.full((1, T), NEG, F32), jnp.zeros((1, T), F32), jnp.zeros((HD, T), F32))
        res = lax.fori_loop(0, cnt[qt], body, (one,) * HG)
        ctx_ref[at, :] = jnp.concatenate([r[2] / r[1] for r in res], axis=0).T.astype(BF)
        lse_ref[:, at] = jnp.concatenate([r[0] + jnp.log(r[1]) for r in res], axis=0)


def bwd_kernel(T, HG, lst, cnt, base, q_ref, k_ref, v_ref, ctx_ref, do_ref, lse_ref, lo_ref, hi_ref, out_ref, dqt, dl):
    n_tiles = q_ref.shape[0] // T
    W = HG * HD
    row = lax.broadcasted_iota(jnp.int32, (T, T), 0)
    lane = lax.broadcasted_iota(jnp.int32, (T, 2 * HD), 1)
    dqt[...] = jnp.zeros_like(dqt)

    @pl.loop(0, n_tiles)
    def _(t):
        at = pl.ds(pl.multiple_of(t * T, T), T)
        prod = (do_ref[at, :].astype(F32) * ctx_ref[at, :].astype(F32)).T
        dl[:, at] = jnp.concatenate([jnp.sum(prod[h * HD : (h + 1) * HD], axis=0, keepdims=True) for h in range(HG)], axis=0)

    @pl.loop(0, n_tiles)
    def _(kt):
        ks = pl.ds(pl.multiple_of(kt * T, T), T)
        k, v = k_ref[ks, :], v_ref[ks, :]
        kT = k.T
        kh, vh = [half(k, h) for h in range(HG)], [half(v, h) for h in range(HG)]

        def body(n, carry):
            at = pl.ds(pl.multiple_of(lst[kt, n] * T, T), T)
            q, do = q_ref[at, :], do_ref[at, :]
            vis = (row >= lo_ref[:, at] - base[kt]) & (row < hi_ref[:, at] - base[kt])
            raw = [dot_nt(kh[h], pair(q, h)) for h in range(HG)]
            dps = [dot_nt(vh[h], pair(do, h)) for h in range(HG)]
            out = []
            for h in range(HG):
                p = jnp.exp(jnp.where(vis, raw[h], NEG) - lse_ref[h : h + 1, at])
                ds = (p * (dps[h] - dl[h : h + 1, at])).astype(BF)
                out.append((carry[h][0] + dot(ds, pair(q, h)), carry[h][1] + dot(p.astype(BF), pair(do, h))))
                dqt[h * HD : (h + 1) * HD, at] += dot(kT[h * HD : (h + 1) * HD, :], ds)
            return tuple(out)

        one = (jnp.zeros((T, 2 * HD), F32), jnp.zeros((T, 2 * HD), F32))
        res = lax.fori_loop(0, cnt[kt], body, (one,) * HG)
        for p in range(HG // 2):
            cols = slice(p * 2 * HD, (p + 1) * 2 * HD)
            a, b = res[2 * p], res[2 * p + 1]
            out_ref[ks, W + cols.start : W + cols.stop] = jnp.where(lane < HD, a[0], b[0]).astype(BF)
            out_ref[ks, 2 * W + cols.start : 2 * W + cols.stop] = jnp.where(lane < HD, a[1], b[1]).astype(BF)

    @pl.loop(0, n_tiles)
    def _(t):
        at = pl.ds(pl.multiple_of(t * T, T), T)
        out_ref[at, :W] = (dqt[:, at].T * HD**-0.5).astype(BF)


def attend(kernel, scalars, ins, outs, scratch, flops):
    def spec(shape, cols):
        if cols is None:
            return pl.BlockSpec(shape, lambda i, *_: (0,) * len(shape))
        return pl.BlockSpec((shape[0], cols[0]), lambda i, *_: (0, cols[1]))

    size = sum(a.size * a.dtype.itemsize for a, _ in ins) + sum(o.size * o.dtype.itemsize for o in outs)
    return pl.pallas_call(
        kernel,
        out_shape=outs,
        grid_spec=pltpu.PrefetchScalarGridSpec(
            num_scalar_prefetch=len(scalars),
            grid=(1,),
            in_specs=[spec(a.shape, cols) for a, cols in ins],
            out_specs=[spec(o.shape, None) for o in outs],
            scratch_shapes=scratch,
        ),
        compiler_params=pltpu.CompilerParams(vmem_limit_bytes=AV << 20),
        cost_estimate=pl.CostEstimate(flops=flops, bytes_accessed=size, transcendentals=0),
    )(*scalars, *[a for a, _ in ins])


def grid_call(kernel, grid, scalars, ins, outs, flops, scratch=(), aliases=None, vmem=VM, light=1):
    def spec(block, index):
        return pl.BlockSpec(memory_space=pl.ANY) if block is None else pl.BlockSpec(block, index)

    size = sum(a.size * a.dtype.itemsize for a, b, _ in ins if b is not None)
    size += sum(o.size * o.dtype.itemsize for o, _, _ in outs)
    return pl.pallas_call(
        kernel,
        out_shape=[o for o, _, _ in outs],
        grid_spec=pltpu.PrefetchScalarGridSpec(
            num_scalar_prefetch=len(scalars),
            grid=grid,
            in_specs=[spec(b, m) for _, b, m in ins],
            out_specs=[spec(b, m) for _, b, m in outs],
            scratch_shapes=list(scratch),
        ),
        input_output_aliases=aliases or {},
        compiler_params=pltpu.CompilerParams(vmem_limit_bytes=vmem << 20),
        cost_estimate=pl.CostEstimate(flops=flops // light, bytes_accessed=size // light, transcendentals=0),
    )(*scalars, *[a for a, _, _ in ins])


def whole(a):
    return a.shape, lambda *_: (0,) * len(a.shape)


def centred(x):
    x = x.astype(F32)
    center = x - jnp.mean(x, axis=-1, keepdims=True)
    spread = jnp.mean(center * center, axis=-1, keepdims=True)
    return center * lax.rsqrt(spread + EPS)


def qkv_kernel(x_ref, g_ref, b_ref, w_ref, bias_ref, sc_ref, *refs):
    h_ref, o_ref = refs[-2:]
    h = (centred(x_ref[...]) * g_ref[...] + b_ref[...]).astype(BF)
    h_ref[...] = h
    o = (dot(h, w_ref[...]) + bias_ref[...]).astype(BF)
    o_ref[...] = (o.astype(F32) * sc_ref[...]).astype(BF)


def qkv_call(x, g, b, w, bias, sc, r, blocks, held):
    F, n = x.shape[0], w.shape[1]
    TR = min(256, F)
    per = F // TR
    row = lambda i: (i, 0)
    to = lambda i: (r * per + i, 0)
    ins = [(x, (TR, D), row)] + [(v, *whole(v)) for v in (g, b, w, bias, sc)]
    shapes = [jax.ShapeDtypeStruct((blocks * F, D), BF), jax.ShapeDtypeStruct((blocks * F, n), BF)]
    aliases = {}
    if held is not None:
        ins += [(held[0], None, None), (held[1], None, None)]
        aliases = {6: 0, 7: 1}
    return grid_call(qkv_kernel, (per,), (), ins, [(shapes[0], (TR, D), to), (shapes[1], (TR, n), to)],
                     2 * F * D * n, aliases=aliases)


def out_kernel(n, group_ref, *refs):
    x_ref, bias_ref, g_ref, b_ref, mid_ref, h_ref = refs[2 * n :]
    mid = sum(dot(refs[i][...], refs[n + i][...]) for i in range(n)) + bias_ref[...]
    mid = x_ref[...].astype(F32) + mid
    mid_ref[...] = mid
    h_ref[...] = (centred(mid) * g_ref[...] + b_ref[...]).astype(BF)


def out_call(mine, groups, w_out, x, bias, g, b):
    F, n = x.shape[0], len(mine)
    W = mine[0].shape[1]
    TR = min(256, F)
    row = lambda i, gr: (i, 0)
    ins = [(m, (TR, W), row) for m in mine]
    ins += [(w_out, (W, D), lambda i, gr, r=r: (gr[r], 0)) for r in range(n)]
    ins += [(x, (TR, D), row)] + [(v, *whole(v)) for v in (bias, g, b)]
    return grid_call(functools.partial(out_kernel, n), (F // TR,), (groups,), ins,
                     [(jax.ShapeDtypeStruct((F, D), F32), (TR, D), row), (jax.ShapeDtypeStruct((F, D), BF), (TR, D), row)],
                     2 * F * D * D)


def ln2_kernel(dh_ref, mid_ref, up_ref, g_ref, w_ref, dy_ref, da_ref, dctx_ref, sum_ref):
    @pl.when(pl.program_id(0) == 0)
    def _():
        sum_ref[...] = jnp.zeros_like(sum_ref)

    mid, dh, up = mid_ref[...], dh_ref[...], up_ref[...].astype(F32)
    center = mid - jnp.mean(mid, axis=-1, keepdims=True)
    rstd = lax.rsqrt(jnp.mean(center * center, axis=-1, keepdims=True) + EPS)
    xh = center * rstd
    t = dh * g_ref[...]
    d = rstd * (t - jnp.mean(t, axis=-1, keepdims=True) - xh * jnp.mean(t * xh, axis=-1, keepdims=True))
    dy = up + d
    dy_ref[...] = dy
    da = dy.astype(BF)
    da_ref[...] = da
    dctx_ref[...] = dot_nt(da, w_ref[...]).astype(BF)
    for k, v in enumerate((dh * xh, dh, da.astype(F32), up)):
        sum_ref[k : k + 1, :] += jnp.sum(v, axis=0, keepdims=True)


def ln2_call(dh2, middle, up, g, w_out):
    F = up.shape[0]
    TR = min(256, F)
    row = lambda i: (i, 0)
    sds = jax.ShapeDtypeStruct
    return grid_call(
        ln2_kernel, (F // TR,), (),
        [(dh2, (TR, D), row), (middle, (TR, D), row), (up, (TR, D), row), (g, *whole(g)), (w_out, *whole(w_out))],
        [(sds((F, D), F32), (TR, D), row), (sds((F, D), BF), (TR, D), row), (sds((F, D), BF), (TR, D), row),
         (sds((4, D), F32), (4, D), lambda i: (0, 0))], 2 * F * D * D)


def mlp_kernel(sub, h_ref, w_ref, b_ref, dg_ref, act_ref, du_ref, dh_ref, bu_ref):
    rows = h_ref.shape[0]

    @pl.when(pl.program_id(0) == 0)
    def _():
        dh_ref[...] = jnp.zeros_like(dh_ref)

    bu = jnp.zeros(bu_ref.shape, F32)
    for r in range(0, rows, sub):
        at = slice(r, r + sub)
        u = dot(h_ref[at, :], w_ref[...]) + b_ref[...]
        cdf = 0.5 + 0.5 * lax.erf(u * 0.7071067811865476)
        pdf = jnp.exp(-0.5 * u * u) * 0.3989422804014327
        act_ref[at, :] = (u * cdf).astype(BF)
        du = (dg_ref[at, :].astype(F32) * (cdf + u * pdf)).astype(BF)
        du_ref[at, :] = du
        bu = bu + jnp.sum(du.astype(F32), axis=0, keepdims=True)
        dh_ref[at, :] += dot_nt(du, w_ref[...])
    bu_ref[...] = bu


def dg_kernel(c_ref, w_ref, o_ref):
    o_ref[...] = dot_nt(c_ref[...], w_ref[...]).astype(BF)


def dg_call(c, w_down):
    F, FF = c.shape[0], w_down.shape[0]
    N = 512
    (out,) = grid_call(dg_kernel, (FF // N,), (), [(c, *whole(c)), (w_down, (N, D), lambda i: (i, 0))],
                       [(jax.ShapeDtypeStruct((F, FF), BF), (F, N), lambda i: (0, i))], 2 * F * D * FF)
    return out


def down_kernel(a_ref, w_ref, mid_ref, bias_ref, o_ref, acc):
    k = pl.program_id(0)

    @pl.when(k == 0)
    def _():
        acc[...] = mid_ref[...] + bias_ref[...]

    acc[...] += dot(a_ref[...], w_ref[...])

    @pl.when(k == pl.num_programs(0) - 1)
    def _():
        o_ref[...] = acc[...].astype(BF)


def down_call(act, w_down, middle, bias):
    F, FF = act.shape
    N = 1024
    (out,) = grid_call(
        down_kernel, (FF // N,), (),
        [(act, (F, N), lambda k: (0, k)), (w_down, (N, D), lambda k: (k, 0)), (middle, *whole(middle)), (bias, *whole(bias))],
        [(jax.ShapeDtypeStruct((F, D), BF), (F, D), lambda k: (0, 0))], 2 * F * D * FF,
        scratch=[pltpu.VMEM((F, D), F32)], light=8)
    return out


def mlp_call(h2, w_up, bias_up, dg):
    F, FF = dg.shape
    N = 1024
    sds = jax.ShapeDtypeStruct
    col = lambda i: (0, i)
    return grid_call(
        functools.partial(mlp_kernel, min(256, F)), (FF // N,), (),
        [(h2, *whole(h2)), (w_up, (D, N), col), (bias_up, (1, N), col), (dg, (F, N), col)],
        [(sds((F, FF), BF), (F, N), col), (sds((F, FF), BF), (F, N), col), (sds((F, D), F32), (F, D), lambda i: (0, 0)),
         (sds((1, FF), F32), (1, N), col)], 4 * F * D * FF, vmem=28)


def wgrad_kernel(put, n, half_ref, *refs):
    put([dot_tn(refs[2 * i][...], refs[2 * i + 1][...]) for i in range(n)], refs[2 * n :])


def wgrad_rows(a, b, side, Y, B, add=None, splits=()):
    k, M = a.shape
    N = b.shape[1] // 2
    W, R = N // Y, M // B
    per = min(B, max(1, 1024 // R))
    idx = lambda i, h: (i, 0, 0, 0)
    ends = list(splits) + [R]

    def put(prods, refs):
        (o,) = prods
        for p in range(per):
            for q in range(Y):
                v = o[p * R : (p + 1) * R, q * W : (q + 1) * W]
                if add is not None:
                    v = v + refs[0][p, q].astype(F32)
                v = v.astype(BF)
                for ref, lo, hi in zip(refs[-len(ends) :], [0] + ends, ends):
                    ref[p, q] = v[lo:hi]

    ins = [(a, (k, per * R), lambda i, h: (0, i)), (b, (k, N), lambda i, h: (0, h[0]))]
    if add is not None:
        ins.append((add, (per, Y, R, W), idx))
    sizes = [hi - lo for lo, hi in zip([0] + ends, ends)]
    return grid_call(functools.partial(wgrad_kernel, put, 1), (B // per,), (side.reshape(1),), ins,
                     [(jax.ShapeDtypeStruct((B, Y, r, W), BF), (per, Y, r, W), idx) for r in sizes], 2 * k * M * N)


def wgrad_cols(a, b, side, Y, B, W, add=None, splits=(), lead=None):
    k, M = a.shape
    R, cut = M // B, b.shape[1] // (2 * Y * W)
    before = 0 if lead is None else lead.shape[2]
    rows = R * cut
    idx = lambda j, h: (0, j, 0, 0)
    ends = [before + e for e in splits] + [before + rows]

    def put(prods, refs):
        (o,) = prods
        if lead is not None:
            refs[-1][:, 0, :before] = refs[-2][:, 0]
        for p in range(cut):
            v = o[:, p * W : (p + 1) * W].reshape(B, R, W)
            if add is not None:
                v = v + refs[0][:, 0, p * R : (p + 1) * R].astype(F32)
            v = v.astype(BF)
            for ref, lo, hi in zip(refs[-len(ends) :], [0] + ends, ends):
                a0, a1 = max(lo, before + p * R), min(hi, before + (p + 1) * R)
                if a0 < a1:
                    ref[:, 0, a0 - lo : a1 - lo] = v[:, a0 - before - p * R : a1 - before - p * R]

    ins = [(a, *whole(a)), (b, (k, cut * W), lambda j, h: (0, h[0] * Y + j))]
    if add is not None:
        ins.append((add, (B, 1, rows, W), idx))
    if lead is not None:
        ins.append((lead, (B, 1, before, W), idx))
    sizes = [hi - lo for lo, hi in zip([0] + ends, ends)]
    return grid_call(functools.partial(wgrad_kernel, put, 1), (Y,), (side.reshape(1),), ins,
                     [(jax.ShapeDtypeStruct((B, Y, r, W), BF), (B, 1, r, W), idx) for r in sizes],
                     2 * k * M * b.shape[1] // 2)


def qgrad_kernel(a_ref, b_ref, o_ref):
    o_ref[...] = dot_tn(a_ref[...], b_ref[...]).reshape(o_ref.shape).astype(BF)


def qgrad(h_all, dqkv, B):
    S, n = dqkv.shape
    W = n // 3
    (out,) = grid_call(
        qgrad_kernel, (3,), (), [(h_all, *whole(h_all)), (dqkv, (S, W), lambda p: (0, p))],
        [(jax.ShapeDtypeStruct((B, 3 * D // B, W), BF), (B, D // B, W), lambda p: (0, p, 0))], 2 * S * D * n, light=8)
    return out


def dh_kernel(n_far, dq_ref, got_ref, w_ref, wm_ref, x_ref, far_ref, own_ref, sum_ref):
    i = pl.program_id(0)

    @pl.when(i == 0)
    def _():
        sum_ref[...] = jnp.zeros_like(sum_ref)

    part = dot_nt(dq_ref[...], w_ref[...]) + dot_nt(got_ref[...], wm_ref[...])
    low = part.astype(BF)

    @pl.when(i < n_far)
    def _():
        far_ref[...] = low

    @pl.when(i >= n_far)
    def _():
        own_ref[...] = low

    sum_ref[0:1, :] += jnp.sum(part * centred(x_ref[...]), axis=0, keepdims=True)
    sum_ref[1:2, :] += jnp.sum(part, axis=0, keepdims=True)


def dh_call(dqkv, got, w_g, w_m, x_all, Y):
    S, n = dqkv.shape
    F = S // (2 * Y)
    TR = min(256, F)
    per = F // TR
    n_far = (Y - 1) * per
    block = lambda i: (i // per + 1) % Y
    full = lambda i: (2 * block(i) * per + i % per, 0)
    sds = jax.ShapeDtypeStruct
    return grid_call(
        functools.partial(dh_kernel, n_far), (Y * per,), (),
        [(dqkv, (TR, n), full), (got, (TR, n), lambda i: (block(i) * per + i % per, 0)), (w_g, *whole(w_g)),
         (w_m, *whole(w_m)), (x_all, (TR, D), full)],
        [(sds(((Y - 1) * F, D), BF), (TR, D), lambda i: (jnp.minimum(i, n_far - 1), 0)),
         (sds((F, D), BF), (TR, D), lambda i: (jnp.maximum(i - n_far, 0), 0)),
         (sds((2, D), F32), (2, D), lambda i: (0, 0))],
        2 * S * D * n, light=8)


def tile_list(active):
    m = active.shape[1]
    hit = active.astype(jnp.int32)
    upto = jnp.tril(jnp.ones((m, m), jnp.int32))
    rank = jnp.sum(hit[:, None, :] * upto[None], axis=2) - 1
    ids = jnp.arange(m, dtype=jnp.int32)
    here = (rank[:, :, None] == ids[None, None, :]) & active[:, :, None]
    return jnp.sum(jnp.where(here, ids[None, :, None], 0), axis=1), jnp.sum(hit, axis=1)


def after(vals, deps):
    return lax.optimization_barrier((vals, deps))[0]


def shards(Z, X, Y, inputs, ln1_gain, ln1_bias, w_qkv, bias_q, bias_v, w_out, bias_out, ln2_gain, ln2_bias,
           w_up, bias_up, w_down, bias_down, lengths, cotangent):
    F = inputs.shape[1]
    K = 2 * Y
    S = F * K
    T = min(256, F)
    W = D // K
    HG = H // K
    B = Z * X
    zi, xi, y, c = (lax.axis_index(n) for n in ("z", "x", "y", "c"))
    group = y * 2 + c
    sds = jax.ShapeDtypeStruct

    def shift(v, axis, n, s):
        return lax.ppermute(v, axis, [(i, (i + s) % n) for i in range(n)])

    def mate(v):
        return lax.ppermute(v, "c", [(0, 1), (1, 0)])

    rel = [(s, d) for s in range(Y) for d in range(2)]

    def hop(v, s, d):
        pairs = [(yy * 2 + cc, ((yy + s) % Y) * 2 + (cc ^ d)) for yy in range(Y) for cc in range(2)]
        return lax.ppermute(v, ("y", "c"), pairs)

    def flip(d):
        return c if d == 0 else 1 - c

    blocks = jnp.stack([((y - s) % Y) * 2 + flip(d) for s, d in rel])
    ends = jnp.cumsum(lengths.reshape(-1))
    pos = (blocks[:, None] * F + jnp.arange(F, dtype=jnp.int32)[None]).reshape(1, S)
    piece = jnp.sum((pos >= ends[:, None]).astype(jnp.int32), axis=0, keepdims=True)
    pieces = ends.shape[0]
    starts = jnp.concatenate([jnp.zeros((1,), ends.dtype), ends[:-1]])

    def look(table, idx):
        return jnp.sum(jnp.where(idx == jnp.arange(pieces)[:, None], table[:, None], 0), axis=0, keepdims=True)

    pad = piece >= pieces
    lo = jnp.where(pad, pos, look(starts, (piece // 3) * 3)).astype(jnp.int32)
    hi = jnp.where(pad | (piece % 3 == 2), pos + 1, look(ends, piece)).astype(jnp.int32)
    base = pos[0, ::T].astype(jnp.int32)
    qlo = jnp.min(lo.reshape(S // T, T), axis=1)
    qhi = jnp.max(hi.reshape(S // T, T), axis=1)
    active = (base[None, :] < qhi[:, None]) & (base[None, :] + T > qlo[:, None])
    lst_q, cnt_q = tile_list(active)
    lst_k, cnt_k = tile_list(active.T)

    x_own = inputs.reshape(F, D)
    up = cotangent.reshape(F, D)
    flat_in = x_own.astype(F32)

    def cols_of(w, g):
        return [lax.dynamic_slice_in_dim(w, part * D + g * W, W, w.ndim - 1) for part in range(3)]

    far = [shift(x_own, "y", Y, s) for s in range(1, Y)]
    near = mate(x_own)
    w_g = jnp.concatenate(cols_of(w_qkv, group), axis=1)
    w_m = jnp.concatenate(cols_of(w_qkv, y * 2 + 1 - c), axis=1)
    b_g = jnp.concatenate([lax.dynamic_slice_in_dim(bias_q, group * W, W, 0), jnp.zeros((W,), F32),
                           lax.dynamic_slice_in_dim(bias_v, group * W, W, 0)])[None]
    sc_g = jnp.where(jnp.arange(3 * W) < W, HD**-0.5, 1.0).astype(F32)[None]
    ln1 = (ln1_gain[None], ln1_bias[None])
    held = qkv_call(x_own, *ln1, w_g, b_g, sc_g, 0, K, None)
    held = qkv_call(near, *ln1, w_g, b_g, sc_g, 1, K, held)
    dg = dg_call(after(up, held[1]), w_down)
    xs = [x_own, near]
    for i, r in enumerate(far):
        r = after(r, dg) if i == 0 else r
        xs += [r, mate(r)]
        held = qkv_call(xs[-2], *ln1, w_g, b_g, sc_g, 2 * i + 2, K, held)
        held = qkv_call(xs[-1], *ln1, w_g, b_g, sc_g, 2 * i + 3, K, held)
    h_all, qkv = held
    lse_shape = sds((HG, S), F32)
    ctx_g, lse = attend(
        functools.partial(fwd_kernel, T, HG), (lst_q, cnt_q, base),
        [(qkv, (W, 0)), (qkv, (W, 1)), (qkv, (W, 2)), (lo, None), (hi, None)],
        [sds((S, W), BF), lse_shape], [], 12 * 10**9)

    mine = [ctx_g[:F]] + [hop(ctx_g[(2 * s + d) * F : (2 * s + d + 1) * F], -s, d) for s, d in rel[1:]]
    x_all = jnp.concatenate(after(xs, ctx_g), axis=0)
    mine[1:] = after(mine[1:], x_all)
    groups = jnp.stack([((y + s) % Y) * 2 + flip(d) for s, d in rel]).astype(jnp.int32)
    middle, h2 = out_call([ctx_g] + mine[1:], groups, w_out, x_own, bias_out[None], ln2_gain[None], ln2_bias[None])
    act, du, dh2, g_bu = mlp_call(h2, w_up, bias_up[None], dg)
    mine = jnp.stack(after(mine, dh2))
    ctx = jnp.concatenate(
        [lax.dynamic_index_in_dim(mine, ((yy - y) % Y) * 2 + (cc ^ c), 0, keepdims=False)
         for yy in range(Y) for cc in range(2)], axis=1)

    def shaped(g):
        return g.reshape(Z, X, Y, g.shape[2], W)

    def begin(items, n, me, send, dep=None):
        def cut(g, axis, i):
            return lax.dynamic_index_in_dim(g, i, axis, keepdims=False)

        def piece(terms, axis, i):
            return settle([cut(g, axis, i) for g in terms]).reshape(-1, W)

        bufs = [jnp.concatenate([piece(g, ax, (me + s) % n) for g, ax in items]) for s in range(1, n)]
        if dep is not None:
            bufs = after(bufs, dep)
        return [[cut(g, ax, me) for g in terms] for terms, ax in items], [send(b, s + 1) for s, b in enumerate(bufs)], bufs

    def settle(terms):
        return sum((g.astype(F32) for g in terms[1:]), terms[0].astype(F32)).astype(BF)

    def finish(state):
        own, sent, _ = state
        out, at = [], 0
        for terms in own:
            rows = terms[0].size // W
            out.append(terms + [r[at : at + rows].reshape(terms[0].shape) for r in sent])
            at += rows
        return out

    def hold(states, others):
        sent, others = lax.optimization_barrier(([st[1] for st in states], others))
        return [(st[0], r, st[2]) for st, r in zip(states, sent)], others

    def head(terms):
        return [g[0] for g in terms]

    def over_y(items):
        return begin(items, Y, y, lambda v, s: shift(v, "y", Y, s))

    def over_x(items):
        return begin(items, X, xi, lambda v, s: shift(v, "x", X, s))

    def over_z(items, bit, dep=None):
        bits = [([g.reshape((g.shape[0] // 2, 2) + g.shape[1:]) for g in terms], 1) for terms in items]
        return begin(bits, 2, (zi // bit) % 2, lambda v, s: lax.ppermute(v, "z", [(i, i ^ bit) for i in range(Z)]), dep)

    assert Z & (Z - 1) == 0
    zbits = [1 << i for i in range(Z.bit_length() - 1)]

    def total(v):
        return jnp.sum(v.astype(F32), axis=0)

    def rows_of(vecs):
        return jnp.concatenate([v.reshape(B, -1) for v in vecs], axis=1).astype(BF).reshape(B, -1, W)

    hr = w_down.shape[0] // B // 2
    n_ot = D // B
    ur = hr + n_ot // 2

    (dn_give,) = wgrad_rows(act, up, 1 - c, Y, B)
    dn_got = mate(dn_give)
    (up_give,) = wgrad_cols(h2, after(du, dn_give), 1 - c, Y, B, W)
    up_got = mate(up_give)
    dy1, da, dctx, sums = ln2_call(after(dh2, up_give), middle, up, ln2_gain[None], w_out)

    def heads_of(s, d):
        return lax.dynamic_slice_in_dim(dctx, (((y + s) % Y) * 2 + flip(d)) * W, W, 1)

    def both(s):
        return jnp.concatenate([heads_of(s, 0), heads_of(s, 1)])

    do_y = [both(0)] + [shift(both(s), "y", Y, s) for s in range(1, Y)]

    dnP, dnQ = wgrad_rows(act, after(up, do_y[0]), c, Y, B, dn_got, (hr,))
    t_y, t_x = over_y([([shaped(dnP)], 2)]), over_x([([shaped(dnQ)], 1)])
    ctx_, da_ = after((ctx, da), (t_y[2], t_x[2]))
    (ot_give,) = wgrad_cols(ctx_, da_, 1 - c, Y, B, W)
    ot_got = mate(ot_give)
    upQ, upP = wgrad_cols(h2, after(du, ot_give), c, Y, B, W, up_got, (ur,))
    do_y = after(do_y, ot_give)
    do_c = mate(jnp.concatenate([v[F:] for v in do_y]))
    do_g = jnp.concatenate([b for s in range(Y) for b in (do_y[s][:F], do_c[s * F : (s + 1) * F])])
    (upP,) = wgrad_cols(ctx_, da_, c, Y, B, W, ot_got, (), upP)
    n_y, n_x = over_y([([shaped(upP)], 2)]), over_x([([shaped(upQ)], 1)])
    (t_y, t_x), (n_bufs, do_g) = hold([t_y, t_x], ((n_y[2], n_x[2]), do_g))
    (dnP,), (dnQ,) = finish(t_y), finish(t_x)

    t_y, t_x, t_z = n_y, n_x, over_z([dnQ], 1)
    dnP = settle(dnP)
    early = rows_of([sums[2], sums[0], sums[1], sums[3], g_bu[0]])
    do_g = after(do_g, (n_bufs, t_z[2], early, dnP))
    (dqkv,) = attend(
        functools.partial(bwd_kernel, T, HG), (lst_k, cnt_k, base),
        [(qkv, (W, 0)), (qkv, (W, 1)), (qkv, (W, 2)), (ctx_g, None), (do_g, None), (lse, None), (lo, None), (hi, None)],
        [sds((S, 3 * W), BF)], [pltpu.VMEM((W, S), F32), pltpu.VMEM((HG, S), F32)], 20 * 10**9)
    (t_y, t_x, t_z), (dqkv, dnP) = hold([t_y, t_x, t_z], (dqkv, dnP))
    (upP,), (upQ,), (dnQ,) = finish(t_y), finish(t_x), finish(t_z)

    def of_x(i):
        return jnp.concatenate([settle([lax.dynamic_index_in_dim(g, i, 1, keepdims=False) for g in terms])
                                for terms in ([dnP], upP)], axis=1)

    p_bufs, p_own = [of_x((xi + s) % X) for s in range(1, X)], of_x(xi)
    t_x = ([[p_own]], [shift(b, "x", X, s + 1) for s, b in enumerate(p_bufs)], p_bufs)
    t_a, t_b = over_z([upQ], 1), over_z([dnQ], zbits[1])
    dq_got = mate(dqkv.reshape(Y, 2, F, 3 * W)[:, 1].reshape(Y * F, 3 * W))
    qv = qgrad(h_all, after(dqkv, (p_bufs, t_a[2])), B)
    dh_far, dh_own, g_ln1 = dh_call(dqkv, after(dq_got, qv), w_g, w_m, x_all, Y)
    far = [shift(dh_far[s * F : (s + 1) * F], "y", Y, -s - 1) for s in range(Y - 1)]
    cols = total(dqkv)
    mine_only = jnp.arange(D) // W == group
    late = rows_of([g_ln1[0], g_ln1[1]] + [jnp.where(mine_only, jnp.tile(v, K), 0.0) for v in (cols[:W], cols[2 * W :])])
    vec = jnp.concatenate([late, early], axis=1)
    vec = jnp.pad(vec, ((0, 0), (0, -vec.shape[1] % 16), (0, 0)))
    qv = jnp.concatenate([qv, vec], axis=1).reshape(Z, X, -1, W)
    n_x = over_x([([qv], 1)])
    (t_x, t_a, t_b), n_bufs = hold([t_x, t_a, t_b], n_x[2])
    parts, upQ, dnQ = [p_own] + t_x[1], finish(t_a)[0], finish(t_b)[0]

    t_x = n_x
    t_a, t_b = over_z([parts], 1), over_z([upQ], zbits[1])
    result = down_call(after(act, (n_bufs, t_a[2], t_b[2])), w_down, middle, bias_down[None])
    (t_x, t_a, t_b), (far, result) = hold([t_x, t_a, t_b], (far, result))

    def rest(items, k):
        for bit in zbits[k:]:
            items = finish(over_z(items, bit))
        return items

    (qv,), (parts,), (upQ,), (dnQ,) = finish(t_x), finish(t_a), rest(finish(t_b), 2), rest([dnQ], 2)

    t_a, t_b = over_z([qv], 1), over_z([parts], zbits[1])
    t_y = over_y([(head(dnQ), 0), (head(upQ), 0)])
    far, dh_own = after((far, dh_own), (t_a[2], t_b[2], t_y[2]))
    dh1 = sum((r.astype(F32) for r in far), dh_own.astype(F32))
    _, norm_back_one = jax.vjp(lambda v: layer_norm(v, ln1_gain, ln1_bias), flat_in)
    (dx,) = norm_back_one(dh1)
    grad_inputs = (dy1 + dx).reshape(1, F, D)
    (t_a, t_b, t_y), grad_inputs = hold([t_a, t_b, t_y], grad_inputs)
    (qv,), (parts,), (dnQ, upQ) = finish(t_a), rest(finish(t_b), 2), finish(t_y)

    parts = settle(head(parts))
    first = jnp.concatenate([parts[:hr], settle(dnQ), settle(upQ), parts[hr:]])

    def share_y(g):
        return [g] + [shift(g, "y", Y, s) for s in range(1, Y)]

    t_b = over_z([qv], zbits[1])
    first_y = share_y(first)
    (t_b,), first_y = hold([t_b], first_y)
    (qv,) = rest(finish(t_b), 2)
    tail_y = share_y(settle(head(qv)))

    def share_c(got):
        got = jnp.stack(got)
        other = mate(got)

        def piece(yy, cc):
            i = (y - yy) % Y
            return jnp.where(cc == c, lax.dynamic_index_in_dim(got, i, 0, keepdims=False),
                             lax.dynamic_index_in_dim(other, i, 0, keepdims=False))

        return [[piece(yy, cc) for cc in range(2)] for yy in range(Y)]

    def by_columns(e, at, rows, chunks):
        return jnp.concatenate([e[yy][cc][at + k * rows : at + (k + 1) * rows] for cc in range(2) for yy in range(Y)
                                for k in range(chunks)], axis=1).astype(F32)

    first_e = share_c(first_y)
    n_dn = 2 * hr
    g_w_down = by_columns(first_e, 0, n_dn, 1)
    g_w_up = by_columns(first_e, n_dn, n_ot, 2 * ur // n_ot - 1)
    g_w_out = by_columns(first_e, n_dn + 2 * ur - n_ot, n_ot, 1)
    tail_y, g_w_down, g_w_up, g_w_out = lax.optimization_barrier((tail_y, g_w_down, g_w_up, g_w_out))
    tail_e = share_c(tail_y)
    g_w_qkv = jnp.concatenate([tail_e[yy][cc][p * n_ot : (p + 1) * n_ot] for p in range(3) for yy in range(Y)
                               for cc in range(2)], axis=1).astype(F32)
    at = 3 * n_ot
    flat = sum(tail_e[yy][cc][at:].astype(F32) for yy in range(Y) for cc in range(2)).reshape(-1)
    out, at = [], 0
    for n in (D, D, D, D, D, D, D, D, w_up.shape[1]):
        out.append(flat[at : at + n // B])
        at += n // B
    g_ln1g, g_ln1b, g_bq, g_bv, g_bo, g_ln2g, g_ln2b, g_bd, g_bu = out
    return (result.reshape(1, F, D), grad_inputs, g_ln1g, g_ln1b, g_w_qkv, g_bq, g_bv, g_w_out, g_bo, g_ln2g, g_ln2b,
            g_w_up, g_bu, g_w_down, g_bd)


def solution(mesh):
    batch, blk = mesh.shape["batch"], mesh.shape["blk"]
    Y = blk // 2
    X = Y if batch % Y == 0 else 1
    Z = batch // X
    fine = Mesh(mesh.devices.reshape(Z, X, Y, 2), ("z", "x", "y", "c"))
    rows, slots = ("z", "x"), ("y", "c")
    act = P(rows, slots, None)
    flat, mat = P(rows), P(rows, None)
    return jax.shard_map(
        functools.partial(shards, Z, X, Y),
        mesh=fine,
        in_specs=(act,) + (P(),) * 13 + (P(rows, None, None), act),
        out_specs=(act, act, flat, flat, mat, flat, flat, mat, flat, flat, flat, mat, flat, mat, flat),
        check_vma=False,
    )
```

profile of v0, /device:TPU:0, one launch (start us, length us, event | category | flops | bytes accessed | tf_op | source)
XLA Modules:
  0.0 280.0 jit_solution(5156379366219146128)
XLA Ops:
  1.2 2.6 collective-permute-start
  7.6 3.2 %constant_dynamic-slice_fusion.7 = (bf16[1024,256]{1,0:T(8,128)(2,1)}, bf16[1024,256]{1,0:T(8,128)(2,1)S(1)}, bf16[1024,256]{1,0:T(8,128)(2,1)S(1)}, bf16[1024,2...) fusion(bf16[1024,3072]{1,0:T(8,128)(2,1)} %param.19, s32[]{:T(128)S(6)} %select_n.505, ...), kind=kLoop, calls=%fused_computation.192 | loop fusion | bytes 6291480 | tf_op jit(solution)/shard_map/dynamic_slice | solution.py:521
  11.0 1.5 copy-done.8
  12.5 1.8 shard_map.271
  14.3 1.8 shard_map.272
  16.2 6.2 %shard_map.273.dg_ref = bf16[512,4096]{1,0:T(8,128)(2,1)S(1)} custom-call(bf16[512,1024]{1,0:T(8,128)(2,1)S(1)} %bitcast.306, bf16[4096,1024]{1,0:T(8,128)(2,1)S(1)} %bitcast.311), custom_call_target="tpu_custom_call" | custom-call | flops 4294967296 | bytes 13631488 | tf_op jit(solution)/shard_map/pallas_call | solution.py:162
  22.4 5.3 %collective-permute-done.x_ref = bf16[512,1024]{1,0:T(8,128)(2,1)S(1)} collective-permute-done((bf16[512,1024]{1,0:T(8,128)(2,1)}, bf16[512,1024]{1,0:T(8,128)(2,1)S(1)}, u32[]{:S(2)}, u32[]{:S(2)}) %collective-permute-start) | collective-permute-done | bytes 1048608 | tf_op jit(solution)/shard_map/ppermute | solution.py:482
  28.3 1.8 shard_map.274
  30.4 1.8 shard_map.275
  32.2 13.9 %shard_map.276 = (bf16[2048,256]{1,0:T(8,128)(2,1)S(1)}, f32[4,2048]{1,0:T(4,128)S(1)}) custom-call(s32[8,8]{1,0:T(8,128)S(1)} %select_reduce_fusion.3.lst, s32[8]{0:T(128)S(1)} %get-tuple-element.193.cnt, s32[8]{0:T(128)S(1)} %bitcast.333, bf16[2048,768]{1,0:T(8,128)(2,1)S(1)} %get-tuple-element.106.q_ref.k_ref.v_ref, ...), custom_call_target="tpu_custom_call" | custom-call | flops 12000000000 | bytes 10534912 | tf_op jit(solution)/shard_map/pallas_call | solution.py:141
  47.0 1.7 collective-permute-start.5
  50.4 4.9 %collective-permute-done.5.refs_3_ = bf16[512,256]{1,0:T(8,128)(2,1)S(1)} collective-permute-done((bf16[512,256]{1,0:T(8,128)(2,1)S(1)}, bf16[512,256]{1,0:T(8,128)(2,1)S(1)}, u32[]{:S(2)}, u32[]{:S(2)}) %collective-permute-start.5) | collective-permute-done | bytes 262176 | tf_op jit(solution)/shard_map/ppermute | solution.py:491
  55.3 5.9 %collective-permute-done.4.refs_2_ = bf16[512,256]{1,0:T(8,128)(2,1)S(1)} collective-permute-done((bf16[512,256]{1,0:T(8,128)(2,1)S(1)}, bf16[512,256]{1,0:T(8,128)(2,1)S(1)}, u32[]{:S(2)}, u32[]{:S(2)}) %collective-permute-start.4) | collective-permute-done | bytes 262176 | tf_op jit(solution)/shard_map/ppermute | solution.py:491
  61.3 2.6 shard_map.277
  63.9 1.3 copy-done.15
  65.3 14.4 %shard_map.278 = (bf16[512,4096]{1,0:T(8,128)(2,1)S(1)}, bf16[512,4096]{1,0:T(8,128)(2,1)S(1)}, f32[512,1024]{1,0:T(8,128)S(1)}, f32[1,4096]{1,0:T(1,128)S(1)}) custom-call(bf16[512,1024]{1,0:T(8,128)(2,1)S(1)} %get-tuple-element.115.h_ref.refs_0_, bf16[1024,4096]{1,0:T(8,128)(2,1)S(1)} %bitcast.336, f32[1,4096]{1,0:T(1,128)S(1)} %bitcast.337, ...), custom_call_target="tpu_custom_call" | custom-call | flops 8589934592 | bytes 24150016 | tf_op jit(solution)/shard_map/pallas_call | solution.py:162
  81.0 5.1 %shard_map.279 = bf16[8,2,512,256]{3,2,1,0:T(8,128)(2,1)} custom-call(s32[1]{0:T(128)} %bitcast.30.half_ref, bf16[512,4096]{1,0:T(8,128)(2,1)S(1)} %get-tuple-element.156.refs_0_.a_ref, bf16[512,1024]{1,0:T(8,128)(2,1)S(1)} %bitcast.307), custom_call_target="tpu_custom_call" | custom-call | flops 2147483648 | bytes 9437184 | tf_op jit(solution)/shard_map/pallas_call | solution.py:162
  86.0 4.1 %shard_map.280 = bf16[8,2,512,256]{3,2,1,0:T(8,128)(2,1)} custom-call(s32[1]{0:T(128)} %bitcast.30.half_ref, bf16[512,1024]{1,0:T(8,128)(2,1)S(1)} %get-tuple-element.115.h_ref.refs_0_, bf16[512,4096]{1,0:T(8,128)(2,1)S(1)} %get-tuple-element.133.refs_1_), custom_call_target="tpu_custom_call" | custom-call | flops 2147483648 | bytes 9437184 | tf_op jit(solution)/shard_map/pallas_call | solution.py:162
  90.8 2.8 pad_maximum_fusion.2.wm_ref
  93.5 1.6 copy-done.32
  95.1 3.1 %shard_map.281 = (f32[512,1024]{1,0:T(8,128)S(1)}, bf16[512,1024]{1,0:T(8,128)(2,1)S(1)}, bf16[512,1024]{1,0:T(8,128)(2,1)S(1)}, f32[4,1024]{1,0:T(4,128)S(1)}) custom-call(f32[512,1024]{1,0:T(8,128)S(1)} %copy-done.32, f32[512,1024]{1,0:T(8,128)S(1)} %copy-done.16, bf16[512,1024]{1,0:T(8,128)(2,1)S(1)} %bitcast.308, f32[1,1024]{1,0:T(1,128)S(1)} %bitcast.328, ...), custom_call_target="tpu_custom_call" | custom-call | flops 1073741824 | bytes 11554816 | tf_op jit(solution)/shard_map/pallas_call | solution.py:162
  99.5 1.8 collective-permute-start.13
  101.8 1.9 copy-done.6
  103.7 5.0 %shard_map.282 = (bf16[8,2,256,256]{3,2,1,0:T(8,128)(2,1)S(1)}, bf16[8,2,256,256]{3,2,1,0:T(8,128)(2,1)S(1)}) custom-call(s32[1]{0:T(128)} %bitcast.4.half_ref, bf16[512,4096]{1,0:T(8,128)(2,1)S(1)} %copy-done.6, bf16[512,1024]{1,0:T(8,128)(2,1)S(1)} %bitcast.309, bf16[8,2,512,256]{3,2,1,0:T(8,128)(2,1)} %collective-permute-done.6.refs_2_), custom_call_target="tpu_custom_call" | custom-call | flops 2147483648 | bytes 13631488 | tf_op jit(solution)/shard_map/pallas_call | solution.py:162
  109.9 1.5 constant_dynamic-slice_fusion.11
  111.4 2.0 shard_map.283
  116.3 1.3 collective-permute-start.11
  117.7 2.2 collective-permute-start.12
  119.8 2.2 copy-done.12
  122.0 4.6 %shard_map.284 = (bf16[8,2,320,256]{3,2,1,0:T(8,128)(2,1)S(1)}, bf16[8,2,192,256]{3,2,1,0:T(8,128)(2,1)S(1)}) custom-call(s32[1]{0:T(128)} %bitcast.4.half_ref, bf16[512,1024]{1,0:T(8,128)(2,1)S(1)} %copy-done.24, bf16[512,4096]{1,0:T(8,128)(2,1)S(1)} %copy-done.12, bf16[8,2,512,256]{3,2,1,0:T(8,128)(2,1)} %collective-permute-done.8.refs_2_), custom_call_target="tpu_custom_call" | custom-call | flops 2147483648 | bytes 13631488 | tf_op jit(solution)/shard_map/pallas_call | solution.py:162
  127.0 1.6 fusion.46
  128.8 2.4 shard_map.285
  132.1 10.5 %collective-permute-done.11 = bf16[2048,256]{1,0:T(8,128)(2,1)S(1)} collective-permute-done((bf16[2048,256]{1,0:T(8,128)(2,1)}, bf16[2048,256]{1,0:T(8,128)(2,1)S(1)}, u32[]{:S(2)}, u32[]{:S(2)}) %collective-permute-start.11) | collective-permute-done | bytes 1048608 | tf_op jit(solution)/shard_map/ppermute | solution.py:482
  142.6 1.3 collective-permute-done.12
  144.5 1.6 collective-permute-start.15
  146.5 22.1 %shard_map.286.b_ref.dq_ref = bf16[2048,768]{1,0:T(8,128)(2,1)S(1)} custom-call(s32[8,8]{1,0:T(8,128)S(1)} %select_reduce_fusion.2.lst, s32[8]{0:T(128)S(1)} %get-tuple-element.251.cnt, s32[8]{0:T(128)S(1)} %bitcast.334, bf16[2048,768]{1,0:T(8,128)(2,1)S(1)} %copy-done.10, bf16[2048,768]{1,0:T(8,128)(2,1)S(1)} %copy-done.10, ...), custom_call_target="tpu_custom_call" | custom-call | flops 20000000000 | bytes 14729216 | tf_op jit(solution)/shard_map/pallas_call | solution.py:141
  168.7 3.0 %collective-permute-done.10 = bf16[2560,256]{1,0:T(8,128)(2,1)S(1)} collective-permute-done((bf16[2560,256]{1,0:T(8,128)(2,1)S(1)}, bf16[2560,256]{1,0:T(8,128)(2,1)S(1)}, u32[]{:S(2)}, u32[]{:S(2)}) %collective-permute-start.10) | collective-permute-done | bytes 1310752 | tf_op jit(solution)/shard_map/ppermute | solution.py:482
  174.0 1.6 collective-permute-start.19
  177.7 1.7 collective-permute-start.18
  180.2 4.7 %shard_map.287 = bf16[8,384,256]{2,1,0:T(8,128)(2,1)S(1)} custom-call(bf16[2048,1024]{1,0:T(8,128)(2,1)S(1)} %copy-done.1, bf16[2048,768]{1,0:T(8,128)(2,1)S(1)} %shard_map.286.b_ref.dq_ref), custom_call_target="tpu_custom_call" | custom-call | flops 402653184 | bytes 1114112 | tf_op jit(solution)/shard_map/pallas_call | solution.py:162
  188.2 6.0 %shard_map.288 = (bf16[512,1024]{1,0:T(8,128)(2,1)S(1)}, bf16[512,1024]{1,0:T(8,128)(2,1)S(1)}, f32[2,1024]{1,0:T(2,128)S(1)}) custom-call(bf16[2048,768]{1,0:T(8,128)(2,1)S(1)} %shard_map.286.b_ref.dq_ref, bf16[1024,768]{1,0:T(8,128)(2,1)S(1)} %collective-permute-done.16.got_ref, bf16[1024,768]{1,0:T(8,128)(2,1)S(1)} %copy-done.4, ...), custom_call_target="tpu_custom_call" | custom-call | flops 402653184 | bytes 1770496 | tf_op jit(solution)/shard_map/pallas_call | solution.py:162
  194.2 1.5 pad_maximum_fusion
  198.4 8.5 %collective-permute-done.18 = bf16[4,576,256]{2,1,0:T(8,128)(2,1)} collective-permute-done((bf16[4,576,256]{2,1,0:T(8,128)(2,1)}, bf16[4,576,256]{2,1,0:T(8,128)(2,1)}, u32[]{:S(2)}, u32[]{:S(2)}) %collective-permute-start.18) | collective-permute-done | bytes 1179680 | tf_op jit(solution)/shard_map/ppermute | solution.py:482
  206.9 2.0 add_convert_fusion.1
  212.2 2.2 copy-done.7
  214.4 1.6 copy-done.17
  216.0 3.4 %copy-done.18 = bf16[4096,1024]{1,0:T(8,128)(2,1)S(1)} copy-done((bf16[4096,1024]{1,0:T(8,128)(2,1)S(1)}, bf16[4096,1024]{1,0:T(8,128)(2,1)}, u32[]{:S(2)}) %copy-start.18) | copy-done | bytes 8388632
  219.4 6.6 %shard_map.289 = bf16[512,1024]{1,0:T(8,128)(2,1)} custom-call(bf16[512,4096]{1,0:T(8,128)(2,1)S(1)} %copy-done.7, bf16[4096,1024]{1,0:T(8,128)(2,1)S(1)} %copy-done.18, f32[512,1024]{1,0:T(8,128)S(1)} %copy-done.17, f32[1,1024]{1,0:T(1,128)S(1)} %bitcast.331), custom_call_target="tpu_custom_call" | custom-call | flops 536870912 | bytes 1966592 | tf_op jit(solution)/shard_map/pallas_call | solution.py:162
  227.5 2.1 collective-permute-done.21
  232.0 1.3 collective-permute-start.25
  235.5 2.1 fusion.3
  237.7 2.3 fusion.43
  240.0 3.4 %add_bitcast_fusion = f32[1,512,1024]{2,1,0:T(8,128)} fusion(f32[512,1024]{1,0:T(8,128)S(1)} %copy-done.36, f32[512]{0:T(512)S(1)} %negate_multiply_fusion, f32[512]{0:T(512)S(1)} %get-tuple-element.248, f32[512]{0:T(512)S(1)} %broadcast_multiply_fusion, bf16[1,512,1024]{2,1,0:T(8,128)(2,1)S(1)} %copy-done.8, f32[512]{0:T(512)S(1)} %get-tuple-element.247, ...), kind=kLoop, calls=%fused_computation.11 | loop fusion | flops 6291456 | bytes 7352320 | tf_op jit(solution)/shard_map/reshape | solution.py:693
  243.4 2.0 collective-permute-done.25
  245.4 4.0 %collective-permute-done.24 = bf16[800,256]{1,0:T(8,128)(2,1)S(1)} collective-permute-done((bf16[800,256]{1,0:T(8,128)(2,1)S(1)}, bf16[800,256]{1,0:T(8,128)(2,1)S(1)}, u32[]{:S(2)}, u32[]{:S(2)}) %collective-permute-start.24) | collective-permute-done | bytes 409632 | tf_op jit(solution)/shard_map/ppermute | solution.py:600
  249.4 1.3 fusion.14
  253.2 1.6 collective-permute-start.28
  255.9 8.7 %collective-permute-done.27 = bf16[400,256]{1,0:T(8,128)(2,1)S(1)} collective-permute-done((bf16[400,256]{1,0:T(8,128)(2,1)S(1)}, bf16[400,256]{1,0:T(8,128)(2,1)S(1)}, u32[]{:S(2)}, u32[]{:S(2)}) %collective-permute-start.27) | collective-permute-done | bytes 204832 | tf_op jit(solution)/shard_map/ppermute | solution.py:600
  264.6 1.4 collective-permute-done.28
  267.4 1.8 collective-permute-start.29
  269.2 1.8 broadcast_select_fusion.3
  272.2 1.5 convert_element_type.544
  273.7 1.6 maximum_convert_fusion
  275.6 1.6 collective-permute-done.31
  (330 shorter events, 47.0 us)
Async XLA Ops:
  0.6 13.7 %collective-permute-start.1 = (bf16[512,1024]{1,0:T(8,128)(2,1)}, bf16[512,1024]{1,0:T(8,128)(2,1)S(1)}, u32[]{:S(2)}, u32[]{:S(2)}) collective-permute-start(bf16[512,1024]{1,0:T(8,128)(2,1)} %bitcast.298), channel_id=1, source_target_pairs={{0,1},{1,0},{2,3},{3,2},{4,5},{5,4},{6,7},{7,6},{8,9},{9,8},{10,11... | collective-permute-start | bytes 3145736 | tf_op jit(solution)/shard_map/ppermute | solution.py:485
  1.2 26.6 %collective-permute-start = (bf16[512,1024]{1,0:T(8,128)(2,1)}, bf16[512,1024]{1,0:T(8,128)(2,1)S(1)}, u32[]{:S(2)}, u32[]{:S(2)}) collective-permute-start(bf16[512,1024]{1,0:T(8,128)(2,1)} %bitcast.299), channel_id=1, source_target_pairs={{0,2},{2,0},{1,3},{3,1},{4,6},{6,4},{5,7},{7,5},{8,10},{10,8},{9,1... | collective-permute-start | bytes 3145736 | tf_op jit(solution)/shard_map/ppermute | solution.py:482
  7.6 8.5 %slice-start = ((s8[8388608]{0:T(1024)(128)(4,1)}), s8[4194304]{0:T(1024)(128)(4,1)S(1)}, s32[]{:S(2)}) async-start(s8[8388608]{0:T(1024)(128)(4,1)} %bitcast.310), calls=%async_computation | async-start | bytes 8388608
  11.0 19.4 %copy-start.3 = (bf16[1024,768]{1,0:T(8,128)(2,1)}, bf16[1024,768]{1,0:T(8,128)(2,1)S(1)}, u32[]{:S(2)}) copy-start(bf16[1024,768]{1,0:T(8,128)(2,1)S(1)} %pad_maximum_fusion.1.w_ref) | copy-start | bytes 4718596
  27.7 2.7 collective-permute-start.2
  30.4 34.9 %slice-start.2 = ((s8[8388608]{0:T(1024)(128)(4,1)}), s8[4194304]{0:T(1024)(128)(4,1)S(1)}, s32[]{:S(2)}) async-start(s8[8388608]{0:T(1024)(128)(4,1)} %bitcast.335), calls=%async_computation.2 | async-start | bytes 8388608
  32.2 14.0 %copy-start = (bf16[2048,1024]{1,0:T(8,128)(2,1)}, bf16[2048,1024]{1,0:T(8,128)(2,1)S(1)}, u32[]{:S(2)}) copy-start(bf16[2048,1024]{1,0:T(8,128)(2,1)S(1)} %get-tuple-element.105.a_ref) | copy-start | bytes 12582916
  32.2 14.0 %copy-start.9 = (bf16[2048,768]{1,0:T(8,128)(2,1)}, bf16[2048,768]{1,0:T(8,128)(2,1)S(1)}, u32[]{:S(2)}) copy-start(bf16[2048,768]{1,0:T(8,128)(2,1)S(1)} %get-tuple-element.106.q_ref.k_ref.v_ref) | copy-start | bytes 9437188
  32.2 33.1 %slice-start.3 = ((s8[8388608]{0:T(1024)(128)(4,1)}), s8[4194304]{0:T(1024)(128)(4,1)S(1)}, s32[]{:S(2)}) async-start(s8[8388608]{0:T(1024)(128)(4,1)} %bitcast.335), calls=%async_computation.3 | async-start | bytes 8388608
  46.2 15.1 %copy-start.25 = (bf16[2048,256]{1,0:T(8,128)(2,1)}, bf16[2048,256]{1,0:T(8,128)(2,1)S(1)}, u32[]{:S(2)}) copy-start(bf16[2048,256]{1,0:T(8,128)(2,1)S(1)} %get-tuple-element.107.refs_0_.ctx_ref) | copy-start | bytes 3145732
  47.0 8.3 %collective-permute-start.5 = (bf16[512,256]{1,0:T(8,128)(2,1)S(1)}, bf16[512,256]{1,0:T(8,128)(2,1)S(1)}, u32[]{:S(2)}, u32[]{:S(2)}) collective-permute-start(bf16[512,256]{1,0:T(8,128)(2,1)S(1)} %get-tuple-element.222), channel_id=1, source_target_pairs={{0,3},{1,2},{2,1},{3,0},{4,7},{5,6},{6,5},{7,4},{8,11},{9,10},{10,... | collective-permute-start | bytes 786440 | tf_op jit(solution)/shard_map/ppermute | solution.py:491
  48.7 12.6 %collective-permute-start.4 = (bf16[512,256]{1,0:T(8,128)(2,1)S(1)}, bf16[512,256]{1,0:T(8,128)(2,1)S(1)}, u32[]{:S(2)}, u32[]{:S(2)}) collective-permute-start(bf16[512,256]{1,0:T(8,128)(2,1)S(1)} %get-tuple-element.223), channel_id=1, source_target_pairs={{0,2},{1,3},{2,0},{3,1},{4,6},{5,7},{6,4},{7,5},{8,10},{9,11},{10,... | collective-permute-start | bytes 786440 | tf_op jit(solution)/shard_map/ppermute | solution.py:491
  49.0 12.3 %collective-permute-start.3 = (bf16[512,256]{1,0:T(8,128)(2,1)S(1)}, bf16[512,256]{1,0:T(8,128)(2,1)S(1)}, u32[]{:S(2)}, u32[]{:S(2)}) collective-permute-start(bf16[512,256]{1,0:T(8,128)(2,1)S(1)} %get-tuple-element.224), channel_id=1, source_target_pairs={{0,1},{1,0},{2,3},{3,2},{4,5},{5,4},{6,7},{7,6},{8,9},{9,8},{10,11... | collective-permute-start | bytes 786440 | tf_op jit(solution)/shard_map/ppermute | solution.py:491
  50.2 11.1 %copy-start.2 = (bf16[1024,1024]{1,0:T(8,128)(2,1)S(1)}, bf16[1024,1024]{1,0:T(8,128)(2,1)}, u32[]{:S(2)}) copy-start(bf16[1024,1024]{1,0:T(8,128)(2,1)} %w_ref.6) | copy-start | bytes 6291460
  50.2 11.1 %copy-start.43 = (f32[1024]{0:T(1024)S(1)}, f32[1024]{0:T(1024)}, u32[]{:S(2)}) copy-start(f32[1024]{0:T(1024)} %param.24) | copy-start | bytes 12292
  50.2 11.1 %copy-start.44 = (f32[1024]{0:T(1024)S(1)}, f32[1024]{0:T(1024)}, u32[]{:S(2)}) copy-start(f32[1024]{0:T(1024)} %param.23) | copy-start | bytes 12292
  50.2 11.1 %copy-start.45 = (f32[1024]{0:T(1024)S(1)}, f32[1024]{0:T(1024)}, u32[]{:S(2)}) copy-start(f32[1024]{0:T(1024)} %param.25) | copy-start | bytes 12292
  50.3 13.6 %copy-start.19 = (bf16[2048,1024]{1,0:T(8,128)(2,1)}, bf16[2048,1024]{1,0:T(8,128)(2,1)S(1)}, u32[]{:S(2)}) copy-start(bf16[2048,1024]{1,0:T(8,128)(2,1)S(1)} %constant_dynamic-update-slice_fusion.x_ref) | copy-start | bytes 12582916
  65.3 20.8 %copy-start.23 = (bf16[512,1024]{1,0:T(8,128)(2,1)}, bf16[512,1024]{1,0:T(8,128)(2,1)S(1)}, u32[]{:S(2)}) copy-start(bf16[512,1024]{1,0:T(8,128)(2,1)S(1)} %get-tuple-element.115.h_ref.refs_0_) | copy-start | bytes 3145732
  81.0 5.1 %copy-start.5 = (bf16[512,4096]{1,0:T(8,128)(2,1)}, bf16[512,4096]{1,0:T(8,128)(2,1)S(1)}, u32[]{:S(2)}) copy-start(bf16[512,4096]{1,0:T(8,128)(2,1)S(1)} %get-tuple-element.156.refs_0_.a_ref) | copy-start | bytes 12582916
  81.0 5.1 %copy-start.11 = (bf16[512,4096]{1,0:T(8,128)(2,1)}, bf16[512,4096]{1,0:T(8,128)(2,1)S(1)}, u32[]{:S(2)}) copy-start(bf16[512,4096]{1,0:T(8,128)(2,1)S(1)} %get-tuple-element.133.refs_1_) | copy-start | bytes 12582916
  86.0 15.8 %collective-permute-start.6 = (bf16[8,2,512,256]{3,2,1,0:T(8,128)(2,1)}, bf16[8,2,512,256]{3,2,1,0:T(8,128)(2,1)}, u32[]{:S(2)}, u32[]{:S(2)}) collective-permute-start(bf16[8,2,512,256]{3,2,1,0:T(8,128)(2,1)} %shard_map.279), channel_id=1, source_target_pairs={{0,1},{1,0},{2,3},{3,2},{4,5},{5,4},{6,7},{7,6},{8,9},{9,8},{10,11... | collective-permute-start | bytes 12582920 | tf_op jit(solution)/shard_map/ppermute | solution.py:485
  90.2 29.6 %collective-permute-start.8 = (bf16[8,2,512,256]{3,2,1,0:T(8,128)(2,1)}, bf16[8,2,512,256]{3,2,1,0:T(8,128)(2,1)}, u32[]{:S(2)}, u32[]{:S(2)}) collective-permute-start(bf16[8,2,512,256]{3,2,1,0:T(8,128)(2,1)} %shard_map.280), channel_id=1, source_target_pairs={{0,1},{1,0},{2,3},{3,2},{4,5},{5,4},{6,7},{7,6},{8,9},{9,8},{10,11... | collective-permute-start | bytes 12582920 | tf_op jit(solution)/shard_map/ppermute | solution.py:485
  98.2 13.2 %copy-start.29 = (bf16[512,1024]{1,0:T(8,128)(2,1)}, bf16[512,1024]{1,0:T(8,128)(2,1)S(1)}, u32[]{:S(2)}) copy-start(bf16[512,1024]{1,0:T(8,128)(2,1)S(1)} %get-tuple-element.132.refs_1_) | copy-start | bytes 3145732
  99.5 13.9 %collective-permute-start.13 = (bf16[1024,256]{1,0:T(8,128)(2,1)S(1)}, bf16[1024,256]{1,0:T(8,128)(2,1)S(1)}, u32[]{:S(2)}, u32[]{:S(2)}) collective-permute-start(bf16[1024,256]{1,0:T(8,128)(2,1)S(1)} %pad_maximum_fusion.10), channel_id=1, source_target_pairs={{0,2},{2,0},{1,3},{3,1},{4,6},{6,4},{5,7},{7,5},{8,10},{10,8},{9,1... | collective-permute-start | bytes 1572872 | tf_op jit(solution)/shard_map/ppermute | solution.py:482
  113.4 6.4 %copy-start.24 = (bf16[512,1024]{1,0:T(8,128)(2,1)S(1)}, bf16[512,1024]{1,0:T(8,128)(2,1)}, u32[]{:S(2)}) copy-start(bf16[512,1024]{1,0:T(8,128)(2,1)} %copy-done.23) | copy-start | bytes 3145732
  113.4 15.3 %collective-permute-start.7 = (bf16[8,2,128,256]{3,2,1,0:T(8,128)(2,1)}, bf16[8,2,128,256]{3,2,1,0:T(8,128)(2,1)}, u32[]{:S(2)}, u32[]{:S(2)}) collective-permute-start(bf16[8,2,128,256]{3,2,1,0:T(8,128)(2,1)} %shard_map.283), channel_id=1, source_target_pairs={{0,1},{1,0},{2,3},{3,2},{4,5},{5,4},{6,7},{7,6},{8,9},{9,8},{10,11... | collective-permute-start | bytes 3145736 | tf_op jit(solution)/shard_map/ppermute | solution.py:485
  115.7 11.2 %collective-permute-start.14 = (bf16[1024,256]{1,0:T(8,128)(2,1)}, bf16[1024,256]{1,0:T(8,128)(2,1)}, u32[]{:S(2)}, u32[]{:S(2)}) collective-permute-start(bf16[1024,256]{1,0:T(8,128)(2,1)} %pad_maximum_fusion.11), channel_id=1, source_target_pairs={{0,1},{1,0},{2,3},{3,2},{4,5},{5,4},{6,7},{7,6},{8,9},{9,8},{10,11... | collective-permute-start | bytes 1572872 | tf_op jit(solution)/shard_map/ppermute | solution.py:485
  116.3 26.3 %collective-permute-start.11 = (bf16[2048,256]{1,0:T(8,128)(2,1)}, bf16[2048,256]{1,0:T(8,128)(2,1)S(1)}, u32[]{:S(2)}, u32[]{:S(2)}) collective-permute-start(bf16[2048,256]{1,0:T(8,128)(2,1)} %bitcast.372), channel_id=1, source_target_pairs={{0,2},{2,0},{1,3},{3,1},{4,6},{6,4},{5,7},{7,5},{8,10},{10,8},{9,1... | collective-permute-start | bytes 3145736 | tf_op jit(solution)/shard_map/ppermute | solution.py:482
  117.7 26.3 %collective-permute-start.12 = (bf16[2048,256]{1,0:T(8,128)(2,1)}, bf16[2048,256]{1,0:T(8,128)(2,1)S(1)}, u32[]{:S(2)}, u32[]{:S(2)}) collective-permute-start(bf16[2048,256]{1,0:T(8,128)(2,1)} %bitcast.371), channel_id=1, source_target_pairs={{0,4},{4,0},{1,5},{5,1},{2,6},{6,2},{3,7},{7,3},{8,12},{12,8},{9,1... | collective-permute-start | bytes 3145736 | tf_op jit(solution)/shard_map/ppermute | solution.py:482
  126.8 46.1 %copy-start.52 = (bf16[4,1,2,320,256]{4,3,2,1,0:T(8,128)(2,1)}, bf16[4,1,2,320,256]{4,3,2,1,0:T(8,128)(2,1)S(1)}, u32[]{:S(2)}) copy-start(bf16[4,1,2,320,256]{4,3,2,1,0:T(8,128)(2,1)S(1)} %get-tuple-element.201) | copy-start | bytes 3932164
  126.9 44.8 %collective-permute-start.10 = (bf16[2560,256]{1,0:T(8,128)(2,1)S(1)}, bf16[2560,256]{1,0:T(8,128)(2,1)S(1)}, u32[]{:S(2)}, u32[]{:S(2)}) collective-permute-start(bf16[2560,256]{1,0:T(8,128)(2,1)S(1)} %bitcast.369), channel_id=1, source_target_pairs={{0,4},{4,0},{1,5},{5,1},{2,6},{6,2},{3,7},{7,3},{8,12},{12,8},{9,1... | collective-permute-start | bytes 3932168 | tf_op jit(solution)/shard_map/ppermute | solution.py:482
  131.2 12.8 %copy-start.34 = (bf16[8,2,256,256]{3,2,1,0:T(8,128)(2,1)S(1)}, bf16[8,2,256,256]{3,2,1,0:T(8,128)(2,1)}, u32[]{:S(2)}) copy-start(bf16[8,2,256,256]{3,2,1,0:T(8,128)(2,1)} %copy-done.33) | copy-start | bytes 6291460
  131.2 13.1 %copy-start.53 = (bf16[4,1,2,256,256]{4,3,2,1,0:T(8,128)(2,1)S(1)}, bf16[4,1,2,256,256]{4,3,2,1,0:T(8,128)(2,1)}, u32[]{:S(2)}) copy-start(bf16[4,1,2,256,256]{4,3,2,1,0:T(8,128)(2,1)} %get-tuple-element.207) | copy-start | bytes 3145732
  131.3 40.4 %collective-permute-start.9 = (bf16[2560,256]{1,0:T(8,128)(2,1)S(1)}, bf16[2560,256]{1,0:T(8,128)(2,1)S(1)}, u32[]{:S(2)}, u32[]{:S(2)}) collective-permute-start(bf16[2560,256]{1,0:T(8,128)(2,1)S(1)} %bitcast.364), channel_id=1, source_target_pairs={{0,2},{2,0},{1,3},{3,1},{4,6},{6,4},{5,7},{7,5},{8,10},{10,8},{9,1... | collective-permute-start | bytes 3932168 | tf_op jit(solution)/shard_map/ppermute | solution.py:482
  144.0 35.5 %copy-start.58 = (bf16[2048,256]{1,0:T(8,128)(2,1)}, bf16[2048,256]{1,0:T(8,128)(2,1)S(1)}, u32[]{:S(2)}) copy-start(bf16[2048,256]{1,0:T(8,128)(2,1)S(1)} %collective-permute-done.12) | copy-start | bytes 3145732
  144.5 27.2 %collective-permute-start.15 = (bf16[1024,256]{1,0:T(8,128)(2,1)S(1)}, bf16[1024,256]{1,0:T(8,128)(2,1)S(1)}, u32[]{:S(2)}, u32[]{:S(2)}) collective-permute-start(bf16[1024,256]{1,0:T(8,128)(2,1)S(1)} %bitcast.384), channel_id=1, source_target_pairs={{0,8},{8,0},{16,24},{24,16},{1,9},{9,1},{17,25},{25,17},{2,10},{10... | collective-permute-start | bytes 1572872 | tf_op jit(solution)/shard_map/ppermute | solution.py:600
  171.7 7.8 %copy-start.62 = (bf16[1024,256]{1,0:T(8,128)(2,1)}, bf16[1024,256]{1,0:T(8,128)(2,1)S(1)}, u32[]{:S(2)}) copy-start(bf16[1024,256]{1,0:T(8,128)(2,1)S(1)} %collective-permute-done.15) | copy-start | bytes 1572868
  171.8 15.7 %collective-permute-start.16 = (bf16[1024,768]{1,0:T(8,128)(2,1)S(1)}, bf16[1024,768]{1,0:T(8,128)(2,1)S(1)}, u32[]{:S(2)}, u32[]{:S(2)}) collective-permute-start(bf16[1024,768]{1,0:T(8,128)(2,1)S(1)} %bitcast.361), channel_id=1, source_target_pairs={{0,1},{1,0},{2,3},{3,2},{4,5},{5,4},{6,7},{7,6},{8,9},{9,8},{10,11... | collective-permute-start | bytes 4718600 | tf_op jit(solution)/shard_map/ppermute | solution.py:485
  174.0 24.4 %collective-permute-start.19 = (bf16[1280,256]{1,0:T(8,128)(2,1)}, bf16[1280,256]{1,0:T(8,128)(2,1)}, u32[]{:S(2)}, u32[]{:S(2)}) collective-permute-start(bf16[1280,256]{1,0:T(8,128)(2,1)} %bitcast.50), channel_id=1, source_target_pairs={{0,8},{8,0},{16,24},{24,16},{1,9},{9,1},{17,25},{25,17},{2,10},{10... | collective-permute-start | bytes 1966088 | tf_op jit(solution)/shard_map/ppermute | solution.py:600
  177.7 29.1 %collective-permute-start.18 = (bf16[4,576,256]{2,1,0:T(8,128)(2,1)}, bf16[4,576,256]{2,1,0:T(8,128)(2,1)}, u32[]{:S(2)}, u32[]{:S(2)}) collective-permute-start(bf16[4,576,256]{2,1,0:T(8,128)(2,1)} %pad_maximum_fusion.4), channel_id=1, source_target_pairs={{0,4},{4,0},{1,5},{5,1},{2,6},{6,2},{3,7},{7,3},{8,12},{12,8},{9,1... | collective-permute-start | bytes 3538952 | tf_op jit(solution)/shard_map/ppermute | solution.py:482
  179.6 18.8 %collective-permute-start.20 = (bf16[512,256]{1,0:T(8,128)(2,1)S(1)}, bf16[512,256]{1,0:T(8,128)(2,1)}, u32[]{:S(2)}, u32[]{:S(2)}) collective-permute-start(bf16[512,256]{1,0:T(8,128)(2,1)S(1)} %bitcast.391), channel_id=1, source_target_pairs={{0,16},{8,24},{16,0},{24,8},{1,17},{9,25},{17,1},{25,9},{2,18},{10... | collective-permute-start | bytes 786440 | tf_op jit(solution)/shard_map/ppermute | solution.py:600
  180.2 7.4 %copy-start.20 = (bf16[2048,1024]{1,0:T(8,128)(2,1)S(1)}, bf16[2048,1024]{1,0:T(8,128)(2,1)}, u32[]{:S(2)}) copy-start(bf16[2048,1024]{1,0:T(8,128)(2,1)} %copy-done.19) | copy-start | bytes 12582916
  195.8 11.1 %copy-start.50 = (bf16[4,1,256,256]{3,2,1,0:T(8,128)(2,1)S(1)}, bf16[4,1,256,256]{3,2,1,0:T(8,128)(2,1)}, u32[]{:S(2)}) copy-start(bf16[4,1,256,256]{3,2,1,0:T(8,128)(2,1)} %get-tuple-element.211) | copy-start | bytes 1572868
  197.1 32.6 %collective-permute-start.17 = (bf16[1600,256]{1,0:T(8,128)(2,1)}, bf16[1600,256]{1,0:T(8,128)(2,1)}, u32[]{:S(2)}, u32[]{:S(2)}) collective-permute-start(bf16[1600,256]{1,0:T(8,128)(2,1)} %bitcast.58), channel_id=1, source_target_pairs={{0,4},{4,0},{1,5},{5,1},{2,6},{6,2},{3,7},{7,3},{8,12},{12,8},{9,1... | collective-permute-start | bytes 2457608 | tf_op jit(solution)/shard_map/ppermute | solution.py:482
  197.7 32.0 %collective-permute-start.23 = (bf16[512,1024]{1,0:T(8,128)(2,1)S(1)}, bf16[512,1024]{1,0:T(8,128)(2,1)}, u32[]{:S(2)}, u32[]{:S(2)}) collective-permute-start(bf16[512,1024]{1,0:T(8,128)(2,1)S(1)} %get-tuple-element.155), channel_id=1, source_target_pairs={{0,2},{2,0},{1,3},{3,1},{4,6},{6,4},{5,7},{7,5},{8,10},{10,8},{9,1... | collective-permute-start | bytes 3145736 | tf_op jit(solution)/shard_map/ppermute | solution.py:482
  198.4 8.5 %copy-start.48 = (bf16[2,2,320,256]{3,2,1,0:T(8,128)(2,1)}, bf16[2,2,320,256]{3,2,1,0:T(8,128)(2,1)S(1)}, u32[]{:S(2)}) copy-start(bf16[2,2,320,256]{3,2,1,0:T(8,128)(2,1)S(1)} %fusion.6) | copy-start | bytes 1966084
  206.9 5.3 %copy-start.46 = (f32[1024]{0:T(1024)S(1)}, f32[1024]{0:T(1024)}, u32[]{:S(2)}) copy-start(f32[1024]{0:T(1024)} %param.29) | copy-start | bytes 12292
  208.9 20.8 %collective-permute-start.21 = (bf16[1152,256]{1,0:T(8,128)(2,1)}, bf16[1152,256]{1,0:T(8,128)(2,1)}, u32[]{:S(2)}, u32[]{:S(2)}) collective-permute-start(bf16[1152,256]{1,0:T(8,128)(2,1)} %bitcast.65), channel_id=1, source_target_pairs={{0,8},{8,0},{16,24},{24,16},{1,9},{9,1},{17,25},{25,17},{2,10},{10... | collective-permute-start | bytes 1769480 | tf_op jit(solution)/shard_map/ppermute | solution.py:600
  210.9 16.6 %collective-permute-start.22 = (bf16[640,256]{1,0:T(8,128)(2,1)S(1)}, bf16[640,256]{1,0:T(8,128)(2,1)S(1)}, u32[]{:S(2)}, u32[]{:S(2)}) collective-permute-start(bf16[640,256]{1,0:T(8,128)(2,1)S(1)} %bitcast.388), channel_id=1, source_target_pairs={{0,16},{8,24},{16,0},{24,8},{1,17},{9,25},{17,1},{25,9},{2,18},{10... | collective-permute-start | bytes 983048 | tf_op jit(solution)/shard_map/ppermute | solution.py:600
  219.4 6.6 %copy-start.63 = (bf16[1024,256]{1,0:T(8,128)(2,1)S(1)}, bf16[1024,256]{1,0:T(8,128)(2,1)}, u32[]{:S(2)}) copy-start(bf16[1024,256]{1,0:T(8,128)(2,1)} %copy-done.62) | copy-start | bytes 1572868
  219.4 11.5 %copy-start.49 = (bf16[2,2,320,256]{3,2,1,0:T(8,128)(2,1)S(1)}, bf16[2,2,320,256]{3,2,1,0:T(8,128)(2,1)}, u32[]{:S(2)}) copy-start(bf16[2,2,320,256]{3,2,1,0:T(8,128)(2,1)} %copy-done.48) | copy-start | bytes 1966084
  219.4 11.5 %copy-start.51 = (bf16[4,1,256,256]{3,2,1,0:T(8,128)(2,1)S(1)}, bf16[4,1,256,256]{3,2,1,0:T(8,128)(2,1)}, u32[]{:S(2)}) copy-start(bf16[4,1,256,256]{3,2,1,0:T(8,128)(2,1)} %get-tuple-element.211) | copy-start | bytes 1572868
  225.9 8.0 %copy-start.54 = (bf16[4,1,400,256]{3,2,1,0:T(8,128)(2,1)S(1)}, bf16[4,1,400,256]{3,2,1,0:T(8,128)(2,1)}, u32[]{:S(2)}) copy-start(bf16[4,1,400,256]{3,2,1,0:T(8,128)(2,1)} %get-tuple-element.209) | copy-start | bytes 2457604
  232.0 13.4 %collective-permute-start.25 = (bf16[576,256]{1,0:T(8,128)(2,1)S(1)}, bf16[576,256]{1,0:T(8,128)(2,1)S(1)}, u32[]{:S(2)}, u32[]{:S(2)}) collective-permute-start(bf16[576,256]{1,0:T(8,128)(2,1)S(1)} %fusion.16), channel_id=1, source_target_pairs={{0,16},{8,24},{16,0},{24,8},{1,17},{9,25},{17,1},{25,9},{2,18},{10... | collective-permute-start | bytes 884744 | tf_op jit(solution)/shard_map/ppermute | solution.py:600
  233.4 12.0 %collective-permute-start.26 = (bf16[576,256]{1,0:T(8,128)(2,1)S(1)}, bf16[576,256]{1,0:T(8,128)(2,1)S(1)}, u32[]{:S(2)}, u32[]{:S(2)}) collective-permute-start(bf16[576,256]{1,0:T(8,128)(2,1)S(1)} %pad_maximum_fusion.13), channel_id=1, source_target_pairs={{0,2},{2,0},{1,3},{3,1},{4,6},{6,4},{5,7},{7,5},{8,10},{10,8},{9,1... | collective-permute-start | bytes 884744 | tf_op jit(solution)/shard_map/ppermute | solution.py:482
  235.1 14.4 %collective-permute-start.24 = (bf16[800,256]{1,0:T(8,128)(2,1)S(1)}, bf16[800,256]{1,0:T(8,128)(2,1)S(1)}, u32[]{:S(2)}, u32[]{:S(2)}) collective-permute-start(bf16[800,256]{1,0:T(8,128)(2,1)S(1)} %bitcast.385), channel_id=1, source_target_pairs={{0,8},{8,0},{16,24},{24,16},{1,9},{9,1},{17,25},{25,17},{2,10},{10... | collective-permute-start | bytes 1228808 | tf_op jit(solution)/shard_map/ppermute | solution.py:600
  249.4 5.3 %copy-start.64 = (bf16[800,256]{1,0:T(8,128)(2,1)}, bf16[800,256]{1,0:T(8,128)(2,1)S(1)}, u32[]{:S(2)}) copy-start(bf16[800,256]{1,0:T(8,128)(2,1)S(1)} %collective-permute-done.24) | copy-start | bytes 1228804
  253.2 12.8 %collective-permute-start.28 = (bf16[1152,256]{1,0:T(8,128)(2,1)S(1)}, bf16[1152,256]{1,0:T(8,128)(2,1)S(1)}, u32[]{:S(2)}, u32[]{:S(2)}) collective-permute-start(bf16[1152,256]{1,0:T(8,128)(2,1)S(1)} %pad_maximum_fusion.8), channel_id=1, source_target_pairs={{0,2},{2,0},{1,3},{3,1},{4,6},{6,4},{5,7},{7,5},{8,10},{10,8},{9,1... | collective-permute-start | bytes 1769480 | tf_op jit(solution)/shard_map/ppermute | solution.py:482
  255.8 10.4 %copy-start.65 = (bf16[800,256]{1,0:T(8,128)(2,1)S(1)}, bf16[800,256]{1,0:T(8,128)(2,1)}, u32[]{:S(2)}) copy-start(bf16[800,256]{1,0:T(8,128)(2,1)} %copy-done.64) | copy-start | bytes 1228804
  255.8 8.8 %collective-permute-start.27 = (bf16[400,256]{1,0:T(8,128)(2,1)S(1)}, bf16[400,256]{1,0:T(8,128)(2,1)S(1)}, u32[]{:S(2)}, u32[]{:S(2)}) collective-permute-start(bf16[400,256]{1,0:T(8,128)(2,1)S(1)} %fusion.22), channel_id=1, source_target_pairs={{0,16},{8,24},{16,0},{24,8},{1,17},{9,25},{17,1},{25,9},{2,18},{10... | collective-permute-start | bytes 614408 | tf_op jit(solution)/shard_map/ppermute | solution.py:600
  266.1 3.1 %collective-permute-start.30 = (bf16[2,1152,256]{2,1,0:T(8,128)(2,1)S(1)}, bf16[2,1152,256]{2,1,0:T(8,128)(2,1)}, u32[]{:S(2)}, u32[]{:S(2)}) collective-permute-start(bf16[2,1152,256]{2,1,0:T(8,128)(2,1)S(1)} %pad_maximum_fusion.3), channel_id=1, source_target_pairs={{0,1},{1,0},{2,3},{3,2},{4,5},{5,4},{6,7},{7,6},{8,9},{9,8},{10,11... | collective-permute-start | bytes 3538952 | tf_op jit(solution)/shard_map/ppermute | solution.py:485
  267.4 7.9 %collective-permute-start.29 = (bf16[400,256]{1,0:T(8,128)(2,1)S(1)}, bf16[400,256]{1,0:T(8,128)(2,1)S(1)}, u32[]{:S(2)}, u32[]{:S(2)}) collective-permute-start(bf16[400,256]{1,0:T(8,128)(2,1)S(1)} %fusion.12), channel_id=1, source_target_pairs={{0,2},{2,0},{1,3},{3,1},{4,6},{6,4},{5,7},{7,5},{8,10},{10,8},{9,1... | collective-permute-start | bytes 614408 | tf_op jit(solution)/shard_map/ppermute | solution.py:482
  275.4 1.8 collective-permute-start.31
  (38 other events, 86.0 us)
where the time goes:
time: 281 us; the launch traced here: 280 us
  Pallas kernels  110 us (39%)
  waiting for transfers between devices  60.1 us (21%)
  local copies, waits for them, and re-layouts  40.6 us (14%)
  other arithmetic  40.4 us (14%)
  starting transfers between devices  26.8 us (10%)
    pallas_call x17, Pallas kernels, grid_call(): pl.pallas_call(kernel, out_shape=[o for o, _, _ in outs], grid_spec=pltpu...  73.9 us
    pallas_call x2, Pallas kernels, attend(): pl.pallas_call(kernel, out_shape=outs, grid_spec=pltpu.PrefetchScalarGrid...  36.1 us
    ppermute x12, waiting for transfers between devices, shift(): return lax.ppermute(v, axis, [(i, (i + s) % n) for i in range(n)])  30.1 us
    unnamed x178, local copies, waits for them, and re-layouts  22.6 us
    ppermute x8, waiting for transfers between devices, over_z(): lax.ppermute(v, 'z', [(i, i ^ bit) for i in range(Z)])  17.3 us
    convert_element_type x17, other arithmetic, settle(): sum((g.astype(F32) for g in terms[1:]), terms[0].astype(F32)).astype(BF)  15.7 us
    ppermute x12, starting transfers between devices, shift(): return lax.ppermute(v, axis, [(i, (i + s) % n) for i in range(n)])  15.6 us
    ppermute x3, waiting for transfers between devices, hop(): return lax.ppermute(v, ('y', 'c'), pairs)  10.9 us
  transfers between devices with their start and end apart: 32, of which 15 were waited for; matrix products, arithmetic and copies ran while one was open for 18% of the time, Pallas kernels for 26%

commit v1 on v0

--- a/solution.py
+++ b/solution.py
@@ -196,7 +196,7 @@
 
 def qkv_call(x, g, b, w, bias, sc, r, blocks, held):
     F, n = x.shape[0], w.shape[1]
-    TR = min(256, F)
+    TR = min(128, F)
     per = F // TR
     row = lambda i: (i, 0)
     to = lambda i: (r * per + i, 0)
@@ -530,7 +530,7 @@
     ln1 = (ln1_gain[None], ln1_bias[None])
     held = qkv_call(x_own, *ln1, w_g, b_g, sc_g, 0, K, None)
     held = qkv_call(near, *ln1, w_g, b_g, sc_g, 1, K, held)
-    dg = dg_call(after(up, held[1]), w_down)
+    dg = dg_call(after(up, (held[1], w_m)), w_down)
     xs = [x_own, near]
     for i, r in enumerate(far):
         r = after(r, dg) if i == 0 else r
@@ -609,6 +609,7 @@
         return jnp.concatenate([v.reshape(B, -1) for v in vecs], axis=1).astype(BF).reshape(B, -1, W)
 
     hr = w_down.shape[0] // B // 2
+    pr = qr = 3 * hr // 4
     n_ot = D // B
     ur = hr + n_ot // 2
 
@@ -626,30 +627,36 @@
 
     do_y = [both(0)] + [shift(both(s), "y", Y, s) for s in range(1, Y)]
 
-    dnP, dnQ = wgrad_rows(act, after(up, do_y[0]), c, Y, B, dn_got, (hr,))
-    t_y, t_x = over_y([([shaped(dnP)], 2)]), over_x([([shaped(dnQ)], 1)])
-    ctx_, da_ = after((ctx, da), (t_y[2], t_x[2]))
-    (ot_give,) = wgrad_cols(ctx_, da_, 1 - c, Y, B, W)
+    (ot_give,) = wgrad_cols(ctx, after(da, do_y[0]), 1 - c, Y, B, W)
     ot_got = mate(ot_give)
-    upQ, upP = wgrad_cols(h2, after(du, ot_give), c, Y, B, W, up_got, (ur,))
-    do_y = after(do_y, ot_give)
+    dnP, dnQ, dnR = wgrad_rows(act, after(up, ot_give), c, Y, B, dn_got, (pr, pr + qr))
+    (dnP, dnQ, dnR), ot_got = lax.optimization_barrier(((dnP, dnQ, dnR), ot_got))
+    t_y, t_x, t_r = over_y([([shaped(dnP)], 2)]), over_x([([shaped(dnQ)], 1)]), over_z([[shaped(dnR)]], 1)
+    h2_, ctx_, da_ = after((h2, ctx, da), (t_y[2], t_x[2], t_r[2]))
+    upQ, upP = wgrad_cols(h2_, du, c, Y, B, W, up_got, (ur,))
+    do_y = after(do_y, (t_y[2], t_x[2], t_r[2]))
     do_c = mate(jnp.concatenate([v[F:] for v in do_y]))
     do_g = jnp.concatenate([b for s in range(Y) for b in (do_y[s][:F], do_c[s * F : (s + 1) * F])])
     (upP,) = wgrad_cols(ctx_, da_, c, Y, B, W, ot_got, (), upP)
     n_y, n_x = over_y([([shaped(upP)], 2)]), over_x([([shaped(upQ)], 1)])
-    (t_y, t_x), (n_bufs, do_g) = hold([t_y, t_x], ((n_y[2], n_x[2]), do_g))
-    (dnP,), (dnQ,) = finish(t_y), finish(t_x)
-
-    t_y, t_x, t_z = n_y, n_x, over_z([dnQ], 1)
+    (t_y, t_x, t_r), (n_bufs, do_g) = hold([t_y, t_x, t_r], ((n_y[2], n_x[2]), do_g))
+    (dnP,), (dnQ,), (dnR,) = finish(t_y), finish(t_x), finish(t_r)
+
+    t_y, t_x, t_z, t_r = n_y, n_x, over_z([dnQ], 1), over_z([dnR], zbits[1])
     dnP = settle(dnP)
     early = rows_of([sums[2], sums[0], sums[1], sums[3], g_bu[0]])
-    do_g = after(do_g, (n_bufs, t_z[2], early, dnP))
+    do_g = after(do_g, (n_bufs, t_z[2], t_r[2], early, dnP))
     (dqkv,) = attend(
         functools.partial(bwd_kernel, T, HG), (lst_k, cnt_k, base),
         [(qkv, (W, 0)), (qkv, (W, 1)), (qkv, (W, 2)), (ctx_g, None), (do_g, None), (lse, None), (lo, None), (hi, None)],
         [sds((S, 3 * W), BF)], [pltpu.VMEM((W, S), F32), pltpu.VMEM((HG, S), F32)], 20 * 10**9)
-    (t_y, t_x, t_z), (dqkv, dnP) = hold([t_y, t_x, t_z], (dqkv, dnP))
-    (upP,), (upQ,), (dnQ,) = finish(t_y), finish(t_x), finish(t_z)
+    (t_y, t_x, t_z, t_r), (dqkv, dnP) = hold([t_y, t_x, t_z, t_r], (dqkv, dnP))
+    def rest(items, k):
+        for bit in zbits[k:]:
+            items = finish(over_z(items, bit))
+        return items
+
+    (upP,), (upQ,), (dnQ,), (dnR,) = finish(t_y), finish(t_x), finish(t_z), rest(finish(t_r), 2)
 
     def of_x(i):
         return jnp.concatenate([settle([lax.dynamic_index_in_dim(g, i, 1, keepdims=False) for g in terms])
@@ -668,7 +675,7 @@
     vec = jnp.concatenate([late, early], axis=1)
     vec = jnp.pad(vec, ((0, 0), (0, -vec.shape[1] % 16), (0, 0)))
     qv = jnp.concatenate([qv, vec], axis=1).reshape(Z, X, -1, W)
-    n_x = over_x([([qv], 1)])
+    n_x = over_x([([qv], 1), (dnR, 1)])
     (t_x, t_a, t_b), n_bufs = hold([t_x, t_a, t_b], n_x[2])
     parts, upQ, dnQ = [p_own] + t_x[1], finish(t_a)[0], finish(t_b)[0]
 
@@ -677,30 +684,26 @@
     result = down_call(after(act, (n_bufs, t_a[2], t_b[2])), w_down, middle, bias_down[None])
     (t_x, t_a, t_b), (far, result) = hold([t_x, t_a, t_b], (far, result))
 
-    def rest(items, k):
-        for bit in zbits[k:]:
-            items = finish(over_z(items, bit))
-        return items
-
-    (qv,), (parts,), (upQ,), (dnQ,) = finish(t_x), finish(t_a), rest(finish(t_b), 2), rest([dnQ], 2)
+    (qv, dnR), (parts,), (upQ,), (dnQ,) = finish(t_x), finish(t_a), rest(finish(t_b), 2), rest([dnQ], 2)
 
     t_a, t_b = over_z([qv], 1), over_z([parts], zbits[1])
-    t_y = over_y([(head(dnQ), 0), (head(upQ), 0)])
+    t_y = over_y([(head(dnQ), 0), (head(upQ), 0), (head(dnR), 0)])
     far, dh_own = after((far, dh_own), (t_a[2], t_b[2], t_y[2]))
     dh1 = sum((r.astype(F32) for r in far), dh_own.astype(F32))
     _, norm_back_one = jax.vjp(lambda v: layer_norm(v, ln1_gain, ln1_bias), flat_in)
     (dx,) = norm_back_one(dh1)
     grad_inputs = (dy1 + dx).reshape(1, F, D)
     (t_a, t_b, t_y), grad_inputs = hold([t_a, t_b, t_y], grad_inputs)
-    (qv,), (parts,), (dnQ, upQ) = finish(t_a), rest(finish(t_b), 2), finish(t_y)
-
-    parts = settle(head(parts))
-    first = jnp.concatenate([parts[:hr], settle(dnQ), settle(upQ), parts[hr:]])
+    (qv,), (parts,), (dnQ, upQ, dnR) = finish(t_a), rest(finish(t_b), 2), finish(t_y)
+
+    t_b = over_z([qv], zbits[1])
+    parts, dnQ, upQ, dnR = after((head(parts), dnQ, upQ, dnR), t_b[2])
+    parts = settle(parts)
+    first = jnp.concatenate([parts[:pr], settle(dnQ), settle(dnR), settle(upQ), parts[pr:]])
 
     def share_y(g):
         return [g] + [shift(g, "y", Y, s) for s in range(1, Y)]
 
-    t_b = over_z([qv], zbits[1])
     first_y = share_y(first)
     (t_b,), first_y = hold([t_b], first_y)
     (qv,) = rest(finish(t_b), 2)

time: 281 us -> 270 us (0.961)
  waiting for transfers between devices: 60.1 us -> 48.8 us
  other arithmetic: 40.4 us -> 32.7 us
  starting transfers between devices: 26.8 us -> 33.6 us
    ppermute x12, waiting for transfers between devices: 30.1 us -> 17.7 us  [shift(): return lax.ppermute(v, axis, [(i, (i + s) % n) for i in range(n)])]
    ppermute x8 -> x10, starting transfers between devices: 7.37 us -> 17 us  [over_z(): lax.ppermute(v, 'z', [(i, i ^ bit) for i in range(Z)])]
    squeeze x0 -> x13, local copies, waits for them, and re-layouts: none -> 6.21 us  [the longest x11 5.21 us: cut(): return lax.dynamic_index_in_dim(g, i, axis, keepdims=False)]
    convert_element_type x17 -> x18, other arithmetic: 15.7 us -> 11.5 us  [settle(): sum((g.astype(F32) for g in terms[1:]), terms[0].astype(F32)).astype(BF)]
    dynamic_slice x5 -> x7, local copies, waits for them, and re-layouts: 4.19 us -> 0.66 us  [cut(): return lax.dynamic_index_in_dim(g, i, axis, keepdims=False)]
    ppermute x12, starting transfers between devices: 15.6 us -> 12.4 us  [shift(): return lax.ppermute(v, axis, [(i, (i + s) % n) for i in range(n)])]
    ppermute x8 -> x10, waiting for transfers between devices: 17.3 us -> 16.7 us  [over_z(): lax.ppermute(v, 'z', [(i, i ^ bit) for i in range(Z)])]
    unnamed x178 -> x187, local copies, waits for them, and re-layouts: 22.6 us -> 22.4 us
  transfers between devices with their start and end apart: 32 -> 34, of which waited for: 15 -> 15; matrix products, arithmetic and copies ran while one was open for 18% -> 15% of each run, Pallas kernels for 26% -> 27%
where the time goes in v1:
time: 270 us; the launch traced here: 267 us
  Pallas kernels  110 us (41%)
  waiting for transfers between devices  48.8 us (18%)
  local copies, waits for them, and re-layouts  39.7 us (15%)
  starting transfers between devices  33.6 us (12%)
  other arithmetic  32.7 us (12%)
    pallas_call x17, Pallas kernels, grid_call(): pl.pallas_call(kernel, out_shape=[o for o, _, _ in outs], grid_spec=pltpu...  75.7 us
    pallas_call x2, Pallas kernels, attend(): pl.pallas_call(kernel, out_shape=outs, grid_spec=pltpu.PrefetchScalarGrid...  34 us
    unnamed x187, local copies, waits for them, and re-layouts  22.4 us
    ppermute x12, waiting for transfers between devices, shift(): return lax.ppermute(v, axis, [(i, (i + s) % n) for i in range(n)])  17.7 us
    ppermute x10, starting transfers between devices, over_z(): lax.ppermute(v, 'z', [(i, i ^ bit) for i in range(Z)])  17 us
    ppermute x10, waiting for transfers between devices, over_z(): lax.ppermute(v, 'z', [(i, i ^ bit) for i in range(Z)])  16.7 us
    ppermute x12, starting transfers between devices, shift(): return lax.ppermute(v, axis, [(i, (i + s) % n) for i in range(n)])  12.4 us
    convert_element_type x18, other arithmetic, settle(): sum((g.astype(F32) for g in terms[1:]), terms[0].astype(F32)).astype(BF)  11.5 us
  transfers between devices with their start and end apart: 34, of which 15 were waited for; matrix products, arithmetic and copies ran while one was open for 15% of the time, Pallas kernels for 27%

profile of v1, /device:TPU:0, one launch (start us, length us, event | category | flops | bytes accessed | tf_op | source)
XLA Modules:
  0.0 266.9 jit_solution(7513796674163463034)
XLA Ops:
  1.2 2.6 collective-permute-start
  7.6 2.1 constant_dynamic-slice_fusion.19
  9.9 1.4 copy-done.8
  11.2 2.4 shard_map.271
  13.6 1.2 pad_maximum_fusion.2.wm_ref
  14.9 2.4 shard_map.272
  17.4 6.2 %shard_map.273.dg_ref = bf16[512,4096]{1,0:T(8,128)(2,1)S(1)} custom-call(bf16[512,1024]{1,0:T(8,128)(2,1)S(1)} %bitcast.341, bf16[4096,1024]{1,0:T(8,128)(2,1)S(1)} %bitcast.346), custom_call_target="tpu_custom_call" | custom-call | flops 4294967296 | bytes 13631488 | tf_op jit(solution)/shard_map/pallas_call | solution.py:162
  23.6 4.1 %collective-permute-done.x_ref = bf16[512,1024]{1,0:T(8,128)(2,1)S(1)} collective-permute-done((bf16[512,1024]{1,0:T(8,128)(2,1)}, bf16[512,1024]{1,0:T(8,128)(2,1)S(1)}, u32[]{:S(2)}, u32[]{:S(2)}) %collective-permute-start) | collective-permute-done | bytes 1048608 | tf_op jit(solution)/shard_map/ppermute | solution.py:482
  28.3 2.4 shard_map.274
  30.8 2.4 shard_map.275
  33.2 13.2 %shard_map.276 = (bf16[2048,256]{1,0:T(8,128)(2,1)S(1)}, f32[4,2048]{1,0:T(4,128)S(1)}) custom-call(s32[8,8]{1,0:T(8,128)S(1)} %select_reduce_fusion.3.lst, s32[8]{0:T(128)S(1)} %get-tuple-element.247.cnt, s32[8]{0:T(128)S(1)} %bitcast.373, bf16[2048,768]{1,0:T(8,128)(2,1)S(1)} %get-tuple-element.133.q_ref.k_ref.v_ref, ...), custom_call_target="tpu_custom_call" | custom-call | flops 12000000000 | bytes 10534912 | tf_op jit(solution)/shard_map/pallas_call | solution.py:141
  48.0 1.8 collective-permute-start.4
  50.0 7.1 %collective-permute-done.4.refs_2_ = bf16[512,256]{1,0:T(8,128)(2,1)S(1)} collective-permute-done((bf16[512,256]{1,0:T(8,128)(2,1)S(1)}, bf16[512,256]{1,0:T(8,128)(2,1)S(1)}, u32[]{:S(2)}, u32[]{:S(2)}) %collective-permute-start.4) | collective-permute-done | bytes 262176 | tf_op jit(solution)/shard_map/ppermute | solution.py:491
  57.1 4.0 %collective-permute-done.5.refs_3_ = bf16[512,256]{1,0:T(8,128)(2,1)S(1)} collective-permute-done((bf16[512,256]{1,0:T(8,128)(2,1)S(1)}, bf16[512,256]{1,0:T(8,128)(2,1)S(1)}, u32[]{:S(2)}, u32[]{:S(2)}) %collective-permute-start.5) | collective-permute-done | bytes 262176 | tf_op jit(solution)/shard_map/ppermute | solution.py:491
  61.2 2.6 shard_map.277
  63.8 1.3 copy-done.16
  65.2 14.1 %shard_map.278 = (bf16[512,4096]{1,0:T(8,128)(2,1)S(1)}, bf16[512,4096]{1,0:T(8,128)(2,1)S(1)}, f32[512,1024]{1,0:T(8,128)S(1)}, f32[1,4096]{1,0:T(1,128)S(1)}) custom-call(bf16[512,1024]{1,0:T(8,128)(2,1)S(1)} %get-tuple-element.166.h_ref.refs_0_, bf16[1024,4096]{1,0:T(8,128)(2,1)S(1)} %bitcast.376, f32[1,4096]{1,0:T(1,128)S(1)} %bitcast.377, ...), custom_call_target="tpu_custom_call" | custom-call | flops 8589934592 | bytes 24150016 | tf_op jit(solution)/shard_map/pallas_call | solution.py:162
  79.3 1.3 copy-done.32
  80.6 5.1 %shard_map.279 = bf16[8,2,512,256]{3,2,1,0:T(8,128)(2,1)} custom-call(s32[1]{0:T(128)} %bitcast.30.half_ref, bf16[512,4096]{1,0:T(8,128)(2,1)S(1)} %get-tuple-element.191.refs_0_.a_ref, bf16[512,1024]{1,0:T(8,128)(2,1)S(1)} %bitcast.342), custom_call_target="tpu_custom_call" | custom-call | flops 2147483648 | bytes 9437184 | tf_op jit(solution)/shard_map/pallas_call | solution.py:162
  86.3 4.1 %shard_map.280 = bf16[8,2,512,256]{3,2,1,0:T(8,128)(2,1)} custom-call(s32[1]{0:T(128)} %bitcast.30.half_ref, bf16[512,1024]{1,0:T(8,128)(2,1)S(1)} %get-tuple-element.166.h_ref.refs_0_, bf16[512,4096]{1,0:T(8,128)(2,1)S(1)} %get-tuple-element.150.refs_1_), custom_call_target="tpu_custom_call" | custom-call | flops 2147483648 | bytes 9437184 | tf_op jit(solution)/shard_map/pallas_call | solution.py:162
  90.8 1.2 copy-done.14
  92.0 1.6 copy-done.17
  93.6 1.6 copy-done.33
  95.2 2.9 %shard_map.281 = (f32[512,1024]{1,0:T(8,128)S(1)}, bf16[512,1024]{1,0:T(8,128)(2,1)S(1)}, bf16[512,1024]{1,0:T(8,128)(2,1)S(1)}, f32[4,1024]{1,0:T(4,128)S(1)}) custom-call(f32[512,1024]{1,0:T(8,128)S(1)} %copy-done.33, f32[512,1024]{1,0:T(8,128)S(1)} %copy-done.17, bf16[512,1024]{1,0:T(8,128)(2,1)S(1)} %bitcast.343, f32[1,1024]{1,0:T(1,128)S(1)} %bitcast.368, ...), custom_call_target="tpu_custom_call" | custom-call | flops 1073741824 | bytes 11554816 | tf_op jit(solution)/shard_map/pallas_call | solution.py:162
  100.3 2.0 shard_map.282
  103.6 1.7 collective-permute-start.14
  106.1 2.2 copy-done.6
  108.3 5.0 %shard_map.283 = (bf16[8,2,192,256]{3,2,1,0:T(8,128)(2,1)S(1)}, bf16[8,2,192,256]{3,2,1,0:T(8,128)(2,1)S(1)}, bf16[8,2,128,256]{3,2,1,0:T(8,128)(2,1)S(1)}) custom-call(s32[1]{0:T(128)} %bitcast.4.half_ref, bf16[512,4096]{1,0:T(8,128)(2,1)S(1)} %copy-done.6, bf16[512,1024]{1,0:T(8,128)(2,1)S(1)} %bitcast.344, ...), custom_call_target="tpu_custom_call" | custom-call | flops 2147483648 | bytes 13631488 | tf_op jit(solution)/shard_map/pallas_call | solution.py:162
  113.4 4.4 %collective-permute-start.13 = (bf16[1024,256]{1,0:T(8,128)(2,1)S(1)}, bf16[1024,256]{1,0:T(8,128)(2,1)S(1)}, u32[]{:S(2)}, u32[]{:S(2)}) collective-permute-start(bf16[1024,256]{1,0:T(8,128)(2,1)S(1)} %bitcast.432), channel_id=1, source_target_pairs={{0,8},{8,0},{16,24},{24,16},{1,9},{9,1},{17,25},{25,17},{2,10},{10... | collective-permute-start | bytes 1572872 | tf_op jit(solution)/shard_map/ppermute | solution.py:600
  118.9 1.8 fusion.47
  121.0 4.5 %shard_map.284 = (bf16[8,2,320,256]{3,2,1,0:T(8,128)(2,1)S(1)}, bf16[8,2,192,256]{3,2,1,0:T(8,128)(2,1)S(1)}) custom-call(s32[1]{0:T(128)} %bitcast.4.half_ref, bf16[512,1024]{1,0:T(8,128)(2,1)S(1)} %copy-done.25, bf16[512,4096]{1,0:T(8,128)(2,1)S(1)} %copy-done.12, bf16[8,2,512,256]{3,2,1,0:T(8,128)(2,1)} %collective-permute-done.8.refs_2_), custom_call_target="tpu_custom_call" | custom-call | flops 2147483648 | bytes 13631488 | tf_op jit(solution)/shard_map/pallas_call | solution.py:162
  126.9 2.4 shard_map.285
  131.4 2.0 collective-permute-start.10
  133.5 5.0 %collective-permute-done.12 = bf16[1536,256]{1,0:T(8,128)(2,1)S(1)} collective-permute-done((bf16[1536,256]{1,0:T(8,128)(2,1)S(1)}, bf16[1536,256]{1,0:T(8,128)(2,1)S(1)}, u32[]{:S(2)}, u32[]{:S(2)}) %collective-permute-start.12) | collective-permute-done | bytes 786464 | tf_op jit(solution)/shard_map/ppermute | solution.py:482
  139.0 1.3 collective-permute-start.17
  140.3 1.4 collective-permute-start.16
  141.7 20.8 %shard_map.286.b_ref.dq_ref = bf16[2048,768]{1,0:T(8,128)(2,1)S(1)} custom-call(s32[8,8]{1,0:T(8,128)S(1)} %select_reduce_fusion.2.lst, s32[8]{0:T(128)S(1)} %get-tuple-element.305.cnt, s32[8]{0:T(128)S(1)} %bitcast.374, bf16[2048,768]{1,0:T(8,128)(2,1)S(1)} %copy-done.10, bf16[2048,768]{1,0:T(8,128)(2,1)S(1)} %copy-done.10, ...), custom_call_target="tpu_custom_call" | custom-call | flops 20000000000 | bytes 14729216 | tf_op jit(solution)/shard_map/pallas_call | solution.py:141
  163.9 1.3 collective-permute-done.9
  169.3 2.1 collective-permute-start.21
  172.6 1.3 copy-done.1
  173.9 4.6 %shard_map.287 = bf16[8,384,256]{2,1,0:T(8,128)(2,1)S(1)} custom-call(bf16[2048,1024]{1,0:T(8,128)(2,1)S(1)} %copy-done.1, bf16[2048,768]{1,0:T(8,128)(2,1)S(1)} %shard_map.286.b_ref.dq_ref), custom_call_target="tpu_custom_call" | custom-call | flops 402653184 | bytes 1114112 | tf_op jit(solution)/shard_map/pallas_call | solution.py:162
  183.3 6.0 %shard_map.288 = (bf16[512,1024]{1,0:T(8,128)(2,1)S(1)}, bf16[512,1024]{1,0:T(8,128)(2,1)S(1)}, f32[2,1024]{1,0:T(2,128)S(1)}) custom-call(bf16[2048,768]{1,0:T(8,128)(2,1)S(1)} %shard_map.286.b_ref.dq_ref, bf16[1024,768]{1,0:T(8,128)(2,1)S(1)} %collective-permute-done.18.got_ref, bf16[1024,768]{1,0:T(8,128)(2,1)S(1)} %copy-done.4, ...), custom_call_target="tpu_custom_call" | custom-call | flops 402653184 | bytes 1770496 | tf_op jit(solution)/shard_map/pallas_call | solution.py:162
  189.4 1.5 pad_maximum_fusion
  190.9 1.5 collective-permute-start.25
  194.0 3.9 %collective-permute-done.20 = bf16[4,512,256]{2,1,0:T(8,128)(2,1)} collective-permute-done((bf16[4,512,256]{2,1,0:T(8,128)(2,1)}, bf16[4,512,256]{2,1,0:T(8,128)(2,1)}, u32[]{:S(2)}, u32[]{:S(2)}) %collective-permute-start.20) | collective-permute-done | bytes 1048608 | tf_op jit(solution)/shard_map/ppermute | solution.py:482
  199.3 1.3 add_convert_fusion.4
  200.6 1.4 collective-permute-start.24
  202.0 3.4 %copy-done.19 = bf16[4096,1024]{1,0:T(8,128)(2,1)S(1)} copy-done((bf16[4096,1024]{1,0:T(8,128)(2,1)S(1)}, bf16[4096,1024]{1,0:T(8,128)(2,1)}, u32[]{:S(2)}) %copy-start.19) | copy-done | bytes 8388632
  205.4 6.6 %shard_map.289 = bf16[512,1024]{1,0:T(8,128)(2,1)} custom-call(bf16[512,4096]{1,0:T(8,128)(2,1)S(1)} %copy-done.7, bf16[4096,1024]{1,0:T(8,128)(2,1)S(1)} %copy-done.19, f32[512,1024]{1,0:T(8,128)S(1)} %copy-done.18, f32[1,1024]{1,0:T(1,128)S(1)} %bitcast.371), custom_call_target="tpu_custom_call" | custom-call | flops 536870912 | bytes 1966592 | tf_op jit(solution)/shard_map/pallas_call | solution.py:162
  219.8 1.6 collective-permute-start.28
  221.4 1.8 collective-permute-start.27
  223.3 1.9 collective-permute-start.26
  227.6 2.2 add_bitcast_fusion
  229.9 3.8 %collective-permute-done.27 = bf16[512,256]{1,0:T(8,128)(2,1)S(1)} collective-permute-done((bf16[512,256]{1,0:T(8,128)(2,1)S(1)}, bf16[512,256]{1,0:T(8,128)(2,1)S(1)}, u32[]{:S(2)}, u32[]{:S(2)}) %collective-permute-start.27) | collective-permute-done | bytes 262176 | tf_op jit(solution)/shard_map/ppermute | solution.py:600
  233.7 4.0 %collective-permute-done.26 = bf16[800,256]{1,0:T(8,128)(2,1)S(1)} collective-permute-done((bf16[800,256]{1,0:T(8,128)(2,1)S(1)}, bf16[800,256]{1,0:T(8,128)(2,1)S(1)}, u32[]{:S(2)}, u32[]{:S(2)}) %collective-permute-start.26) | collective-permute-done | bytes 409632 | tf_op jit(solution)/shard_map/ppermute | solution.py:600
  239.1 1.5 collective-permute-start.29
  240.5 8.4 %collective-permute-done.29 = bf16[400,256]{1,0:T(8,128)(2,1)S(1)} collective-permute-done((bf16[400,256]{1,0:T(8,128)(2,1)S(1)}, bf16[400,256]{1,0:T(8,128)(2,1)S(1)}, u32[]{:S(2)}, u32[]{:S(2)}) %collective-permute-start.29) | collective-permute-done | bytes 204832 | tf_op jit(solution)/shard_map/ppermute | solution.py:600
  248.9 2.9 %collective-permute-done.30 = bf16[1152,256]{1,0:T(8,128)(2,1)S(1)} collective-permute-done((bf16[1152,256]{1,0:T(8,128)(2,1)S(1)}, bf16[1152,256]{1,0:T(8,128)(2,1)S(1)}, u32[]{:S(2)}, u32[]{:S(2)}) %collective-permute-start.30) | collective-permute-done | bytes 589856 | tf_op jit(solution)/shard_map/ppermute | solution.py:482
  254.3 1.8 collective-permute-done.32
  256.1 1.7 broadcast_select_fusion.3
  259.1 1.5 convert_element_type.644
  260.6 1.6 maximum_convert_fusion
  262.5 1.6 collective-permute-done.33
  264.5 1.3 convert_element_type.651
  (368 shorter events, 48.7 us)
Async XLA Ops:
  0.6 14.2 %collective-permute-start.1 = (bf16[512,1024]{1,0:T(8,128)(2,1)}, bf16[512,1024]{1,0:T(8,128)(2,1)S(1)}, u32[]{:S(2)}, u32[]{:S(2)}) collective-permute-start(bf16[512,1024]{1,0:T(8,128)(2,1)} %bitcast.333), channel_id=1, source_target_pairs={{0,1},{1,0},{2,3},{3,2},{4,5},{5,4},{6,7},{7,6},{8,9},{9,8},{10,11... | collective-permute-start | bytes 3145736 | tf_op jit(solution)/shard_map/ppermute | solution.py:485
  1.2 26.6 %collective-permute-start = (bf16[512,1024]{1,0:T(8,128)(2,1)}, bf16[512,1024]{1,0:T(8,128)(2,1)S(1)}, u32[]{:S(2)}, u32[]{:S(2)}) collective-permute-start(bf16[512,1024]{1,0:T(8,128)(2,1)} %bitcast.334), channel_id=1, source_target_pairs={{0,2},{2,0},{1,3},{3,1},{4,6},{6,4},{5,7},{7,5},{8,10},{10,8},{9,1... | collective-permute-start | bytes 3145736 | tf_op jit(solution)/shard_map/ppermute | solution.py:482
  9.9 20.9 %copy-start.3 = (bf16[1024,768]{1,0:T(8,128)(2,1)}, bf16[1024,768]{1,0:T(8,128)(2,1)S(1)}, u32[]{:S(2)}) copy-start(bf16[1024,768]{1,0:T(8,128)(2,1)S(1)} %pad_maximum_fusion.1.w_ref) | copy-start | bytes 4718596
  27.7 3.0 %collective-permute-start.2 = (bf16[512,1024]{1,0:T(8,128)(2,1)S(1)}, bf16[512,1024]{1,0:T(8,128)(2,1)S(1)}, u32[]{:S(2)}, u32[]{:S(2)}) collective-permute-start(bf16[512,1024]{1,0:T(8,128)(2,1)S(1)} %collective-permute-done.x_ref), channel_id=1, source_target_pairs={{0,1},{1,0},{2,3},{3,2},{4,5},{5,4},{6,7},{7,6},{8,9},{9,8},{10,11... | collective-permute-start | bytes 3145736 | tf_op jit(solution)/shard_map/ppermute | solution.py:485
  30.7 34.4 %slice-start.2 = ((s8[8388608]{0:T(1024)(128)(4,1)}), s8[4194304]{0:T(1024)(128)(4,1)S(1)}, s32[]{:S(2)}) async-start(s8[8388608]{0:T(1024)(128)(4,1)} %bitcast.375), calls=%async_computation.2 | async-start | bytes 8388608
  33.2 13.3 %copy-start = (bf16[2048,1024]{1,0:T(8,128)(2,1)}, bf16[2048,1024]{1,0:T(8,128)(2,1)S(1)}, u32[]{:S(2)}) copy-start(bf16[2048,1024]{1,0:T(8,128)(2,1)S(1)} %get-tuple-element.132.a_ref) | copy-start | bytes 12582916
  33.2 13.3 %copy-start.9 = (bf16[2048,768]{1,0:T(8,128)(2,1)}, bf16[2048,768]{1,0:T(8,128)(2,1)S(1)}, u32[]{:S(2)}) copy-start(bf16[2048,768]{1,0:T(8,128)(2,1)S(1)} %get-tuple-element.133.q_ref.k_ref.v_ref) | copy-start | bytes 9437188
  33.2 32.0 %slice-start.3 = ((s8[8388608]{0:T(1024)(128)(4,1)}), s8[4194304]{0:T(1024)(128)(4,1)S(1)}, s32[]{:S(2)}) async-start(s8[8388608]{0:T(1024)(128)(4,1)} %bitcast.375), calls=%async_computation.3 | async-start | bytes 8388608
  46.4 14.7 %copy-start.26 = (bf16[2048,256]{1,0:T(8,128)(2,1)}, bf16[2048,256]{1,0:T(8,128)(2,1)S(1)}, u32[]{:S(2)}) copy-start(bf16[2048,256]{1,0:T(8,128)(2,1)S(1)} %get-tuple-element.134.refs_0_.ctx_ref) | copy-start | bytes 3145732
  47.4 2.6 collective-permute-start.3
  48.0 9.2 %collective-permute-start.4 = (bf16[512,256]{1,0:T(8,128)(2,1)S(1)}, bf16[512,256]{1,0:T(8,128)(2,1)S(1)}, u32[]{:S(2)}, u32[]{:S(2)}) collective-permute-start(bf16[512,256]{1,0:T(8,128)(2,1)S(1)} %get-tuple-element.275), channel_id=1, source_target_pairs={{0,2},{1,3},{2,0},{3,1},{4,6},{5,7},{6,4},{7,5},{8,10},{9,11},{10,... | collective-permute-start | bytes 786440 | tf_op jit(solution)/shard_map/ppermute | solution.py:491
  49.7 11.4 %collective-permute-start.5 = (bf16[512,256]{1,0:T(8,128)(2,1)S(1)}, bf16[512,256]{1,0:T(8,128)(2,1)S(1)}, u32[]{:S(2)}, u32[]{:S(2)}) collective-permute-start(bf16[512,256]{1,0:T(8,128)(2,1)S(1)} %get-tuple-element.274), channel_id=1, source_target_pairs={{0,3},{1,2},{2,1},{3,0},{4,7},{5,6},{6,5},{7,4},{8,11},{9,10},{10,... | collective-permute-start | bytes 786440 | tf_op jit(solution)/shard_map/ppermute | solution.py:491
  49.8 11.3 %copy-start.2 = (bf16[1024,1024]{1,0:T(8,128)(2,1)S(1)}, bf16[1024,1024]{1,0:T(8,128)(2,1)}, u32[]{:S(2)}) copy-start(bf16[1024,1024]{1,0:T(8,128)(2,1)} %w_ref.6) | copy-start | bytes 6291460
  49.8 11.3 %copy-start.43 = (f32[1024]{0:T(1024)S(1)}, f32[1024]{0:T(1024)}, u32[]{:S(2)}) copy-start(f32[1024]{0:T(1024)} %param.24) | copy-start | bytes 12292
  49.8 11.3 %copy-start.44 = (f32[1024]{0:T(1024)S(1)}, f32[1024]{0:T(1024)}, u32[]{:S(2)}) copy-start(f32[1024]{0:T(1024)} %param.23) | copy-start | bytes 12292
  49.8 11.3 %copy-start.45 = (f32[1024]{0:T(1024)S(1)}, f32[1024]{0:T(1024)}, u32[]{:S(2)}) copy-start(f32[1024]{0:T(1024)} %param.25) | copy-start | bytes 12292
  50.0 13.8 %copy-start.20 = (bf16[2048,1024]{1,0:T(8,128)(2,1)}, bf16[2048,1024]{1,0:T(8,128)(2,1)S(1)}, u32[]{:S(2)}) copy-start(bf16[2048,1024]{1,0:T(8,128)(2,1)S(1)} %constant_dynamic-update-slice_fusion.x_ref) | copy-start | bytes 12582916
  65.1 21.2 %copy-start.24 = (bf16[512,1024]{1,0:T(8,128)(2,1)}, bf16[512,1024]{1,0:T(8,128)(2,1)S(1)}, u32[]{:S(2)}) copy-start(bf16[512,1024]{1,0:T(8,128)(2,1)S(1)} %get-tuple-element.166.h_ref.refs_0_) | copy-start | bytes 3145732
  85.7 20.4 %collective-permute-start.6 = (bf16[8,2,512,256]{3,2,1,0:T(8,128)(2,1)}, bf16[8,2,512,256]{3,2,1,0:T(8,128)(2,1)}, u32[]{:S(2)}, u32[]{:S(2)}) collective-permute-start(bf16[8,2,512,256]{3,2,1,0:T(8,128)(2,1)} %shard_map.279), channel_id=1, source_target_pairs={{0,1},{1,0},{2,3},{3,2},{4,5},{5,4},{6,7},{7,6},{8,9},{9,8},{10,11... | collective-permute-start | bytes 12582920 | tf_op jit(solution)/shard_map/ppermute | solution.py:485
  90.4 30.4 %collective-permute-start.8 = (bf16[8,2,512,256]{3,2,1,0:T(8,128)(2,1)}, bf16[8,2,512,256]{3,2,1,0:T(8,128)(2,1)}, u32[]{:S(2)}, u32[]{:S(2)}) collective-permute-start(bf16[8,2,512,256]{3,2,1,0:T(8,128)(2,1)} %shard_map.280), channel_id=1, source_target_pairs={{0,1},{1,0},{2,3},{3,2},{4,5},{5,4},{6,7},{7,6},{8,9},{9,8},{10,11... | collective-permute-start | bytes 12582920 | tf_op jit(solution)/shard_map/ppermute | solution.py:485
  102.3 11.1 %collective-permute-start.7 = (bf16[8,2,128,256]{3,2,1,0:T(8,128)(2,1)}, bf16[8,2,128,256]{3,2,1,0:T(8,128)(2,1)}, u32[]{:S(2)}, u32[]{:S(2)}) collective-permute-start(bf16[8,2,128,256]{3,2,1,0:T(8,128)(2,1)} %shard_map.282), channel_id=1, source_target_pairs={{0,1},{1,0},{2,3},{3,2},{4,5},{5,4},{6,7},{7,6},{8,9},{9,8},{10,11... | collective-permute-start | bytes 3145736 | tf_op jit(solution)/shard_map/ppermute | solution.py:485
  103.6 15.1 %collective-permute-start.14 = (bf16[1024,256]{1,0:T(8,128)(2,1)}, bf16[1024,256]{1,0:T(8,128)(2,1)}, u32[]{:S(2)}, u32[]{:S(2)}) collective-permute-start(bf16[1024,256]{1,0:T(8,128)(2,1)} %pad_maximum_fusion.10), channel_id=1, source_target_pairs={{0,2},{2,0},{1,3},{3,1},{4,6},{6,4},{5,7},{7,5},{8,10},{10,8},{9,1... | collective-permute-start | bytes 1572872 | tf_op jit(solution)/shard_map/ppermute | solution.py:482
  113.3 50.5 %copy-start.36 = (bf16[8,2,128,256]{3,2,1,0:T(8,128)(2,1)}, bf16[8,2,128,256]{3,2,1,0:T(8,128)(2,1)S(1)}, u32[]{:S(2)}) copy-start(bf16[8,2,128,256]{3,2,1,0:T(8,128)(2,1)S(1)} %get-tuple-element.162) | copy-start | bytes 3145732
  113.4 20.1 %collective-permute-start.13 = (bf16[1024,256]{1,0:T(8,128)(2,1)S(1)}, bf16[1024,256]{1,0:T(8,128)(2,1)S(1)}, u32[]{:S(2)}, u32[]{:S(2)}) collective-permute-start(bf16[1024,256]{1,0:T(8,128)(2,1)S(1)} %bitcast.432), channel_id=1, source_target_pairs={{0,8},{8,0},{16,24},{24,16},{1,9},{9,1},{17,25},{25,17},{2,10},{10... | collective-permute-start | bytes 1572872 | tf_op jit(solution)/shard_map/ppermute | solution.py:600
  118.0 48.1 %copy-start.52 = (bf16[4,1,2,192,256]{4,3,2,1,0:T(8,128)(2,1)}, bf16[4,1,2,192,256]{4,3,2,1,0:T(8,128)(2,1)S(1)}, u32[]{:S(2)}) copy-start(bf16[4,1,2,192,256]{4,3,2,1,0:T(8,128)(2,1)S(1)} %get-tuple-element.263) | copy-start | bytes 2359300
  118.0 20.5 %collective-permute-start.12 = (bf16[1536,256]{1,0:T(8,128)(2,1)S(1)}, bf16[1536,256]{1,0:T(8,128)(2,1)S(1)}, u32[]{:S(2)}, u32[]{:S(2)}) collective-permute-start(bf16[1536,256]{1,0:T(8,128)(2,1)S(1)} %bitcast.424), channel_id=1, source_target_pairs={{0,4},{4,0},{1,5},{5,1},{2,6},{6,2},{3,7},{7,3},{8,12},{12,8},{9,1... | collective-permute-start | bytes 2359304 | tf_op jit(solution)/shard_map/ppermute | solution.py:482
  118.1 20.5 %collective-permute-start.11 = (bf16[1536,256]{1,0:T(8,128)(2,1)S(1)}, bf16[1536,256]{1,0:T(8,128)(2,1)S(1)}, u32[]{:S(2)}, u32[]{:S(2)}) collective-permute-start(bf16[1536,256]{1,0:T(8,128)(2,1)S(1)} %bitcast.419), channel_id=1, source_target_pairs={{0,2},{2,0},{1,3},{3,1},{4,6},{6,4},{5,7},{7,5},{8,10},{10,8},{9,1... | collective-permute-start | bytes 2359304 | tf_op jit(solution)/shard_map/ppermute | solution.py:482
  120.8 10.6 %collective-permute-start.15 = (bf16[1024,256]{1,0:T(8,128)(2,1)S(1)}, bf16[1024,256]{1,0:T(8,128)(2,1)S(1)}, u32[]{:S(2)}, u32[]{:S(2)}) collective-permute-start(bf16[1024,256]{1,0:T(8,128)(2,1)S(1)} %pad_maximum_fusion.11), channel_id=1, source_target_pairs={{0,1},{1,0},{2,3},{3,2},{4,5},{5,4},{6,7},{7,6},{8,9},{9,8},{10,11... | collective-permute-start | bytes 1572872 | tf_op jit(solution)/shard_map/ppermute | solution.py:485
  125.7 42.3 %copy-start.50 = (bf16[4,1,2,320,256]{4,3,2,1,0:T(8,128)(2,1)}, bf16[4,1,2,320,256]{4,3,2,1,0:T(8,128)(2,1)S(1)}, u32[]{:S(2)}) copy-start(bf16[4,1,2,320,256]{4,3,2,1,0:T(8,128)(2,1)S(1)} %get-tuple-element.255) | copy-start | bytes 3932164
  130.8 34.4 %collective-permute-start.9 = (bf16[2560,256]{1,0:T(8,128)(2,1)S(1)}, bf16[2560,256]{1,0:T(8,128)(2,1)S(1)}, u32[]{:S(2)}, u32[]{:S(2)}) collective-permute-start(bf16[2560,256]{1,0:T(8,128)(2,1)S(1)} %bitcast.412), channel_id=1, source_target_pairs={{0,2},{2,0},{1,3},{3,1},{4,6},{6,4},{5,7},{7,5},{8,10},{10,8},{9,1... | collective-permute-start | bytes 3932168 | tf_op jit(solution)/shard_map/ppermute | solution.py:482
  131.4 33.8 %collective-permute-start.10 = (bf16[2560,256]{1,0:T(8,128)(2,1)S(1)}, bf16[2560,256]{1,0:T(8,128)(2,1)S(1)}, u32[]{:S(2)}, u32[]{:S(2)}) collective-permute-start(bf16[2560,256]{1,0:T(8,128)(2,1)S(1)} %bitcast.413), channel_id=1, source_target_pairs={{0,4},{4,0},{1,5},{5,1},{2,6},{6,2},{3,7},{7,3},{8,12},{12,8},{9,1... | collective-permute-start | bytes 3932168 | tf_op jit(solution)/shard_map/ppermute | solution.py:482
  133.5 30.3 %copy-start.58 = (bf16[1024,256]{1,0:T(8,128)(2,1)}, bf16[1024,256]{1,0:T(8,128)(2,1)S(1)}, u32[]{:S(2)}) copy-start(bf16[1024,256]{1,0:T(8,128)(2,1)S(1)} %collective-permute-done.13) | copy-start | bytes 1572868
  138.5 27.6 %copy-start.56 = (bf16[1536,256]{1,0:T(8,128)(2,1)}, bf16[1536,256]{1,0:T(8,128)(2,1)S(1)}, u32[]{:S(2)}) copy-start(bf16[1536,256]{1,0:T(8,128)(2,1)S(1)} %collective-permute-done.12) | copy-start | bytes 2359300
  139.0 24.9 %collective-permute-start.17 = (bf16[512,256]{1,0:T(8,128)(2,1)S(1)}, bf16[512,256]{1,0:T(8,128)(2,1)S(1)}, u32[]{:S(2)}, u32[]{:S(2)}) collective-permute-start(bf16[512,256]{1,0:T(8,128)(2,1)S(1)} %bitcast.448), channel_id=1, source_target_pairs={{0,16},{8,24},{16,0},{24,8},{1,17},{9,25},{17,1},{25,9},{2,18},{10... | collective-permute-start | bytes 786440 | tf_op jit(solution)/shard_map/ppermute | solution.py:600
  140.3 23.6 %collective-permute-start.16 = (bf16[768,256]{1,0:T(8,128)(2,1)S(1)}, bf16[768,256]{1,0:T(8,128)(2,1)S(1)}, u32[]{:S(2)}, u32[]{:S(2)}) collective-permute-start(bf16[768,256]{1,0:T(8,128)(2,1)S(1)} %bitcast.441), channel_id=1, source_target_pairs={{0,8},{8,0},{16,24},{24,16},{1,9},{9,1},{17,25},{25,17},{2,10},{10... | collective-permute-start | bytes 1179656 | tf_op jit(solution)/shard_map/ppermute | solution.py:600
  163.9 8.7 %copy-start.65 = (bf16[512,256]{1,0:T(8,128)(2,1)}, bf16[512,256]{1,0:T(8,128)(2,1)S(1)}, u32[]{:S(2)}) copy-start(bf16[512,256]{1,0:T(8,128)(2,1)S(1)} %collective-permute-done.17) | copy-start | bytes 786436
  163.9 14.6 %copy-start.64 = (bf16[768,256]{1,0:T(8,128)(2,1)}, bf16[768,256]{1,0:T(8,128)(2,1)S(1)}, u32[]{:S(2)}) copy-start(bf16[768,256]{1,0:T(8,128)(2,1)S(1)} %collective-permute-done.16) | copy-start | bytes 1179652
  165.2 15.1 %copy-start.54 = (bf16[2560,256]{1,0:T(8,128)(2,1)}, bf16[2560,256]{1,0:T(8,128)(2,1)S(1)}, u32[]{:S(2)}) copy-start(bf16[2560,256]{1,0:T(8,128)(2,1)S(1)} %collective-permute-done.10) | copy-start | bytes 3932164
  166.9 27.1 %collective-permute-start.22 = (bf16[384,256]{1,0:T(8,128)(2,1)}, bf16[384,256]{1,0:T(8,128)(2,1)}, u32[]{:S(2)}, u32[]{:S(2)}) collective-permute-start(bf16[384,256]{1,0:T(8,128)(2,1)} %bitcast.70), channel_id=1, source_target_pairs={{0,16},{8,24},{16,0},{24,8},{1,17},{9,25},{17,1},{25,9},{2,18},{10... | collective-permute-start | bytes 589832 | tf_op jit(solution)/shard_map/ppermute | solution.py:600
  169.3 24.8 %collective-permute-start.21 = (bf16[1280,256]{1,0:T(8,128)(2,1)}, bf16[1280,256]{1,0:T(8,128)(2,1)}, u32[]{:S(2)}, u32[]{:S(2)}) collective-permute-start(bf16[1280,256]{1,0:T(8,128)(2,1)} %bitcast.54), channel_id=1, source_target_pairs={{0,8},{8,0},{16,24},{24,16},{1,9},{9,1},{17,25},{25,17},{2,10},{10... | collective-permute-start | bytes 1966088 | tf_op jit(solution)/shard_map/ppermute | solution.py:600
  172.4 25.6 %collective-permute-start.20 = (bf16[4,512,256]{2,1,0:T(8,128)(2,1)}, bf16[4,512,256]{2,1,0:T(8,128)(2,1)}, u32[]{:S(2)}, u32[]{:S(2)}) collective-permute-start(bf16[4,512,256]{2,1,0:T(8,128)(2,1)} %pad_maximum_fusion.7), channel_id=1, source_target_pairs={{0,4},{4,0},{1,5},{5,1},{2,6},{6,2},{3,7},{7,3},{8,12},{12,8},{9,1... | collective-permute-start | bytes 3145736 | tf_op jit(solution)/shard_map/ppermute | solution.py:482
  172.5 9.5 %collective-permute-start.18 = (bf16[1024,768]{1,0:T(8,128)(2,1)S(1)}, bf16[1024,768]{1,0:T(8,128)(2,1)S(1)}, u32[]{:S(2)}, u32[]{:S(2)}) collective-permute-start(bf16[1024,768]{1,0:T(8,128)(2,1)S(1)} %bitcast.405), channel_id=1, source_target_pairs={{0,1},{1,0},{2,3},{3,2},{4,5},{5,4},{6,7},{7,6},{8,9},{9,8},{10,11... | collective-permute-start | bytes 4718600 | tf_op jit(solution)/shard_map/ppermute | solution.py:485
  190.9 25.7 %collective-permute-start.25 = (bf16[512,1024]{1,0:T(8,128)(2,1)S(1)}, bf16[512,1024]{1,0:T(8,128)(2,1)S(1)}, u32[]{:S(2)}, u32[]{:S(2)}) collective-permute-start(bf16[512,1024]{1,0:T(8,128)(2,1)S(1)} %get-tuple-element.190), channel_id=1, source_target_pairs={{0,2},{2,0},{1,3},{3,1},{4,6},{6,4},{5,7},{7,5},{8,10},{10,8},{9,1... | collective-permute-start | bytes 3145736 | tf_op jit(solution)/shard_map/ppermute | solution.py:482
  192.5 45.2 %copy-start.51 = (bf16[4,1,400,256]{3,2,1,0:T(8,128)(2,1)}, bf16[4,1,400,256]{3,2,1,0:T(8,128)(2,1)S(1)}, u32[]{:S(2)}) copy-start(bf16[4,1,400,256]{3,2,1,0:T(8,128)(2,1)S(1)} %get-tuple-element.261) | copy-start | bytes 2457604
  192.5 9.4 %copy-start.18 = (f32[512,1024]{1,0:T(8,128)S(1)}, f32[512,1024]{1,0:T(8,128)}, u32[]{:S(2)}) copy-start(f32[512,1024]{1,0:T(8,128)} %copy-done.16) | copy-start | bytes 6291460
  192.6 24.0 %collective-permute-start.19 = (bf16[1856,256]{1,0:T(8,128)(2,1)S(1)}, bf16[1856,256]{1,0:T(8,128)(2,1)S(1)}, u32[]{:S(2)}, u32[]{:S(2)}) collective-permute-start(bf16[1856,256]{1,0:T(8,128)(2,1)S(1)} %pad_maximum_fusion.8), channel_id=1, source_target_pairs={{0,4},{4,0},{1,5},{5,1},{2,6},{6,2},{3,7},{7,3},{8,12},{12,8},{9,1... | collective-permute-start | bytes 2850824 | tf_op jit(solution)/shard_map/ppermute | solution.py:482
  194.0 8.0 %copy-start.46 = (f32[1024]{0:T(1024)S(1)}, f32[1024]{0:T(1024)}, u32[]{:S(2)}) copy-start(f32[1024]{0:T(1024)} %param.29) | copy-start | bytes 12292
  199.1 17.2 %collective-permute-start.23 = (bf16[1024,256]{1,0:T(8,128)(2,1)S(1)}, bf16[1024,256]{1,0:T(8,128)(2,1)S(1)}, u32[]{:S(2)}, u32[]{:S(2)}) collective-permute-start(bf16[1024,256]{1,0:T(8,128)(2,1)S(1)} %bitcast.425), channel_id=1, source_target_pairs={{0,8},{8,0},{16,24},{24,16},{1,9},{9,1},{17,25},{25,17},{2,10},{10... | collective-permute-start | bytes 1572872 | tf_op jit(solution)/shard_map/ppermute | solution.py:600
  200.6 15.2 %collective-permute-start.24 = (bf16[640,256]{1,0:T(8,128)(2,1)S(1)}, bf16[640,256]{1,0:T(8,128)(2,1)S(1)}, u32[]{:S(2)}, u32[]{:S(2)}) collective-permute-start(bf16[640,256]{1,0:T(8,128)(2,1)S(1)} %bitcast.444), channel_id=1, source_target_pairs={{0,16},{8,24},{16,0},{24,8},{1,17},{9,25},{17,1},{25,9},{2,18},{10... | collective-permute-start | bytes 983048 | tf_op jit(solution)/shard_map/ppermute | solution.py:600
  219.8 13.9 %collective-permute-start.28 = (bf16[640,256]{1,0:T(8,128)(2,1)S(1)}, bf16[640,256]{1,0:T(8,128)(2,1)S(1)}, u32[]{:S(2)}, u32[]{:S(2)}) collective-permute-start(bf16[640,256]{1,0:T(8,128)(2,1)S(1)} %pad_maximum_fusion.13), channel_id=1, source_target_pairs={{0,2},{2,0},{1,3},{3,1},{4,6},{6,4},{5,7},{7,5},{8,10},{10,8},{9,1... | collective-permute-start | bytes 983048 | tf_op jit(solution)/shard_map/ppermute | solution.py:482
  221.4 12.3 %collective-permute-start.27 = (bf16[512,256]{1,0:T(8,128)(2,1)S(1)}, bf16[512,256]{1,0:T(8,128)(2,1)S(1)}, u32[]{:S(2)}, u32[]{:S(2)}) collective-permute-start(bf16[512,256]{1,0:T(8,128)(2,1)S(1)} %fusion.13), channel_id=1, source_target_pairs={{0,16},{8,24},{16,0},{24,8},{1,17},{9,25},{17,1},{25,9},{2,18},{10... | collective-permute-start | bytes 786440 | tf_op jit(solution)/shard_map/ppermute | solution.py:600
  223.3 14.4 %collective-permute-start.26 = (bf16[800,256]{1,0:T(8,128)(2,1)S(1)}, bf16[800,256]{1,0:T(8,128)(2,1)S(1)}, u32[]{:S(2)}, u32[]{:S(2)}) collective-permute-start(bf16[800,256]{1,0:T(8,128)(2,1)S(1)} %bitcast.435), channel_id=1, source_target_pairs={{0,8},{8,0},{16,24},{24,16},{1,9},{9,1},{17,25},{25,17},{2,10},{10... | collective-permute-start | bytes 1228808 | tf_op jit(solution)/shard_map/ppermute | solution.py:600
  229.8 8.2 %copy-start.61 = (bf16[192,256]{1,0:T(8,128)(2,1)S(1)}, bf16[192,256]{1,0:T(8,128)(2,1)}, u32[]{:S(2)}) copy-start(bf16[192,256]{1,0:T(8,128)(2,1)} %get-tuple-element.211) | copy-start | bytes 294916
  229.8 8.2 %copy-start.62 = (bf16[192,256]{1,0:T(8,128)(2,1)S(1)}, bf16[192,256]{1,0:T(8,128)(2,1)}, u32[]{:S(2)}) copy-start(bf16[192,256]{1,0:T(8,128)(2,1)} %get-tuple-element.210) | copy-start | bytes 294916
  229.8 8.2 %copy-start.63 = (bf16[192,256]{1,0:T(8,128)(2,1)S(1)}, bf16[192,256]{1,0:T(8,128)(2,1)}, u32[]{:S(2)}) copy-start(bf16[192,256]{1,0:T(8,128)(2,1)} %dynamic-slice_bitcast_fusion.12) | copy-start | bytes 294916
  229.9 8.3 %copy-start.67 = (bf16[128,256]{1,0:T(8,128)(2,1)S(1)}, bf16[128,256]{1,0:T(8,128)(2,1)}, u32[]{:S(2)}) copy-start(bf16[128,256]{1,0:T(8,128)(2,1)} %dynamic-slice_bitcast_fusion.18) | copy-start | bytes 196612
  229.9 8.3 %copy-start.68 = (bf16[128,256]{1,0:T(8,128)(2,1)S(1)}, bf16[128,256]{1,0:T(8,128)(2,1)}, u32[]{:S(2)}) copy-start(bf16[128,256]{1,0:T(8,128)(2,1)} %dynamic-slice_bitcast_fusion.17) | copy-start | bytes 196612
  229.9 8.3 %copy-start.57 = (bf16[320,256]{1,0:T(8,128)(2,1)S(1)}, bf16[320,256]{1,0:T(8,128)(2,1)}, u32[]{:S(2)}) copy-start(bf16[320,256]{1,0:T(8,128)(2,1)} %dynamic-slice_bitcast_fusion.10) | copy-start | bytes 491524
  238.5 14.5 %copy-start.60 = (bf16[800,256]{1,0:T(8,128)(2,1)S(1)}, bf16[800,256]{1,0:T(8,128)(2,1)}, u32[]{:S(2)}) copy-start(bf16[800,256]{1,0:T(8,128)(2,1)} %copy-done.59) | copy-start | bytes 1228804
  238.5 13.3 %collective-permute-start.30 = (bf16[1152,256]{1,0:T(8,128)(2,1)S(1)}, bf16[1152,256]{1,0:T(8,128)(2,1)S(1)}, u32[]{:S(2)}, u32[]{:S(2)}) collective-permute-start(bf16[1152,256]{1,0:T(8,128)(2,1)S(1)} %slice_dynamic-update-slice_fusion), channel_id=1, source_target_pairs={{0,2},{2,0},{1,3},{3,1},{4,6},{6,4},{5,7},{7,5},{8,10},{10,8},{9,1... | collective-permute-start | bytes 1769480 | tf_op jit(solution)/shard_map/ppermute | solution.py:482
  239.1 9.9 %collective-permute-start.29 = (bf16[400,256]{1,0:T(8,128)(2,1)S(1)}, bf16[400,256]{1,0:T(8,128)(2,1)S(1)}, u32[]{:S(2)}, u32[]{:S(2)}) collective-permute-start(bf16[400,256]{1,0:T(8,128)(2,1)S(1)} %fusion.18), channel_id=1, source_target_pairs={{0,16},{8,24},{16,0},{24,8},{1,17},{9,25},{17,1},{25,9},{2,18},{10... | collective-permute-start | bytes 614408 | tf_op jit(solution)/shard_map/ppermute | solution.py:600
  252.9 3.2 %collective-permute-start.32 = (bf16[2,1152,256]{2,1,0:T(8,128)(2,1)}, bf16[2,1152,256]{2,1,0:T(8,128)(2,1)}, u32[]{:S(2)}, u32[]{:S(2)}) collective-permute-start(bf16[2,1152,256]{2,1,0:T(8,128)(2,1)} %pad_maximum_fusion.3), channel_id=1, source_target_pairs={{0,1},{1,0},{2,3},{3,2},{4,5},{5,4},{6,7},{7,6},{8,9},{9,8},{10,11... | collective-permute-start | bytes 3538952 | tf_op jit(solution)/shard_map/ppermute | solution.py:485
  254.0 8.2 %collective-permute-start.31 = (bf16[400,256]{1,0:T(8,128)(2,1)S(1)}, bf16[400,256]{1,0:T(8,128)(2,1)S(1)}, u32[]{:S(2)}, u32[]{:S(2)}) collective-permute-start(bf16[400,256]{1,0:T(8,128)(2,1)S(1)} %fusion.11), channel_id=1, source_target_pairs={{0,2},{2,0},{1,3},{3,1},{4,6},{6,4},{5,7},{7,5},{8,10},{10,8},{9,1... | collective-permute-start | bytes 614408 | tf_op jit(solution)/shard_map/ppermute | solution.py:482
  262.3 1.8 collective-permute-start.33
  (44 other events, 121.0 us)

commit v2 on v1

--- a/solution.py
+++ b/solution.py
@@ -609,7 +609,7 @@
         return jnp.concatenate([v.reshape(B, -1) for v in vecs], axis=1).astype(BF).reshape(B, -1, W)
 
     hr = w_down.shape[0] // B // 2
-    pr = qr = 3 * hr // 4
+    pr = qr = 5 * hr // 8 // 16 * 16
     n_ot = D // B
     ur = hr + n_ot // 2
 

time: 270 us -> 268 us (level); the launches traced: 267 us -> 268 us
  starting transfers between devices: 33.6 us -> 44.2 us
  Pallas kernels: 110 us -> 102 us
  local copies, waits for them, and re-layouts: 39.7 us -> 36.7 us
    ppermute x10, starting transfers between devices: 17 us -> 25.5 us  [over_z(): lax.ppermute(v, 'z', [(i, i ^ bit) for i in range(Z)])]
    pallas_call x2, Pallas kernels: 34 us -> 26 us  [attend(): pl.pallas_call(kernel, out_shape=outs, grid_spec=pltpu.PrefetchScalarGrid...]
    ppermute x10, waiting for transfers between devices: 16.7 us -> 22.3 us  [over_z(): lax.ppermute(v, 'z', [(i, i ^ bit) for i in range(Z)])]
    ppermute x12, waiting for transfers between devices: 17.7 us -> 14.9 us  [shift(): return lax.ppermute(v, axis, [(i, (i + s) % n) for i in range(n)])]
    unnamed x187 -> x185, local copies, waits for them, and re-layouts: 22.4 us -> 20.9 us
  transfers between devices with their start and end apart: 34 -> 34, of which waited for: 15 -> 17; matrix products, arithmetic and copies ran while one was open for 15% -> 15% of each run, Pallas kernels for 27% -> 25%
where the time goes in v2:
time: 268 us
  Pallas kernels  102 us (38%)
  waiting for transfers between devices  50.7 us (19%)
  starting transfers between devices  44.2 us (16%)
  local copies, waits for them, and re-layouts  36.7 us (14%)
  other arithmetic  32.7 us (12%)
    pallas_call x17, Pallas kernels, grid_call(): pl.pallas_call(kernel, out_shape=[o for o, _, _ in outs], grid_spec=pltpu...  75.6 us
    pallas_call x2, Pallas kernels, attend(): pl.pallas_call(kernel, out_shape=outs, grid_spec=pltpu.PrefetchScalarGrid...  26 us
    ppermute x10, starting transfers between devices, over_z(): lax.ppermute(v, 'z', [(i, i ^ bit) for i in range(Z)])  25.5 us
    ppermute x10, waiting for transfers between devices, over_z(): lax.ppermute(v, 'z', [(i, i ^ bit) for i in range(Z)])  22.3 us
    unnamed x185, local copies, waits for them, and re-layouts  20.9 us
    ppermute x12, waiting for transfers between devices, shift(): return lax.ppermute(v, axis, [(i, (i + s) % n) for i in range(n)])  14.9 us
    ppermute x12, starting transfers between devices, shift(): return lax.ppermute(v, axis, [(i, (i + s) % n) for i in range(n)])  14.5 us
    convert_element_type x18, other arithmetic, settle(): sum((g.astype(F32) for g in terms[1:]), terms[0].astype(F32)).astype(BF)  11.4 us
  transfers between devices with their start and end apart: 34, of which 17 were waited for; matrix products, arithmetic and copies ran while one was open for 15% of the time, Pallas kernels for 25%

profile of v2, /device:TPU:0, one launch (start us, length us, event | category | flops | bytes accessed | tf_op | source)
XLA Modules:
  0.0 268.3 jit_solution(3647569399858217795)
XLA Ops:
  1.2 2.6 collective-permute-start
  7.6 2.1 constant_dynamic-slice_fusion.19
  9.9 1.4 copy-done.8
  11.2 2.4 shard_map.271
  13.6 1.2 pad_maximum_fusion.2.wm_ref
  14.9 2.4 shard_map.272
  17.4 6.2 %shard_map.273.dg_ref = bf16[512,4096]{1,0:T(8,128)(2,1)S(1)} custom-call(bf16[512,1024]{1,0:T(8,128)(2,1)S(1)} %bitcast.341, bf16[4096,1024]{1,0:T(8,128)(2,1)S(1)} %bitcast.346), custom_call_target="tpu_custom_call" | custom-call | flops 4294967296 | bytes 13631488 | tf_op jit(solution)/shard_map/pallas_call | solution.py:162
  23.6 4.1 %collective-permute-done.x_ref = bf16[512,1024]{1,0:T(8,128)(2,1)S(1)} collective-permute-done((bf16[512,1024]{1,0:T(8,128)(2,1)}, bf16[512,1024]{1,0:T(8,128)(2,1)S(1)}, u32[]{:S(2)}, u32[]{:S(2)}) %collective-permute-start) | collective-permute-done | bytes 1048608 | tf_op jit(solution)/shard_map/ppermute | solution.py:482
  28.3 2.4 shard_map.274
  30.8 2.4 shard_map.275
  33.2 9.8 %shard_map.276 = (bf16[2048,256]{1,0:T(8,128)(2,1)S(1)}, f32[4,2048]{1,0:T(4,128)S(1)}) custom-call(s32[8,8]{1,0:T(8,128)S(1)} %select_reduce_fusion.3.lst, s32[8]{0:T(128)S(1)} %get-tuple-element.247.cnt, s32[8]{0:T(128)S(1)} %bitcast.373, bf16[2048,768]{1,0:T(8,128)(2,1)S(1)} %get-tuple-element.133.q_ref.k_ref.v_ref, ...), custom_call_target="tpu_custom_call" | custom-call | flops 12000000000 | bytes 10534912 | tf_op jit(solution)/shard_map/pallas_call | solution.py:141
  44.5 1.8 collective-permute-start.4
  46.6 7.1 %collective-permute-done.4.refs_2_ = bf16[512,256]{1,0:T(8,128)(2,1)S(1)} collective-permute-done((bf16[512,256]{1,0:T(8,128)(2,1)S(1)}, bf16[512,256]{1,0:T(8,128)(2,1)S(1)}, u32[]{:S(2)}, u32[]{:S(2)}) %collective-permute-start.4) | collective-permute-done | bytes 262176 | tf_op jit(solution)/shard_map/ppermute | solution.py:491
  53.7 4.0 %collective-permute-done.5.refs_3_ = bf16[512,256]{1,0:T(8,128)(2,1)S(1)} collective-permute-done((bf16[512,256]{1,0:T(8,128)(2,1)S(1)}, bf16[512,256]{1,0:T(8,128)(2,1)S(1)}, u32[]{:S(2)}, u32[]{:S(2)}) %collective-permute-start.5) | collective-permute-done | bytes 262176 | tf_op jit(solution)/shard_map/ppermute | solution.py:491
  57.7 2.6 shard_map.277
  60.4 1.3 copy-done.16
  61.7 14.1 %shard_map.278 = (bf16[512,4096]{1,0:T(8,128)(2,1)S(1)}, bf16[512,4096]{1,0:T(8,128)(2,1)S(1)}, f32[512,1024]{1,0:T(8,128)S(1)}, f32[1,4096]{1,0:T(1,128)S(1)}) custom-call(bf16[512,1024]{1,0:T(8,128)(2,1)S(1)} %get-tuple-element.166.h_ref.refs_0_, bf16[1024,4096]{1,0:T(8,128)(2,1)S(1)} %bitcast.376, f32[1,4096]{1,0:T(1,128)S(1)} %bitcast.377, ...), custom_call_target="tpu_custom_call" | custom-call | flops 8589934592 | bytes 24150016 | tf_op jit(solution)/shard_map/pallas_call | solution.py:162
  75.9 1.3 copy-done.32
  77.2 5.1 %shard_map.279 = bf16[8,2,512,256]{3,2,1,0:T(8,128)(2,1)} custom-call(s32[1]{0:T(128)} %bitcast.30.half_ref, bf16[512,4096]{1,0:T(8,128)(2,1)S(1)} %get-tuple-element.191.refs_0_.a_ref, bf16[512,1024]{1,0:T(8,128)(2,1)S(1)} %bitcast.342), custom_call_target="tpu_custom_call" | custom-call | flops 2147483648 | bytes 9437184 | tf_op jit(solution)/shard_map/pallas_call | solution.py:162
  82.8 4.1 %shard_map.280 = bf16[8,2,512,256]{3,2,1,0:T(8,128)(2,1)} custom-call(s32[1]{0:T(128)} %bitcast.30.half_ref, bf16[512,1024]{1,0:T(8,128)(2,1)S(1)} %get-tuple-element.166.h_ref.refs_0_, bf16[512,4096]{1,0:T(8,128)(2,1)S(1)} %get-tuple-element.150.refs_1_), custom_call_target="tpu_custom_call" | custom-call | flops 2147483648 | bytes 9437184 | tf_op jit(solution)/shard_map/pallas_call | solution.py:162
  87.3 1.2 copy-done.14
  88.5 1.6 copy-done.17
  90.1 1.6 copy-done.33
  91.7 2.9 %shard_map.281 = (f32[512,1024]{1,0:T(8,128)S(1)}, bf16[512,1024]{1,0:T(8,128)(2,1)S(1)}, bf16[512,1024]{1,0:T(8,128)(2,1)S(1)}, f32[4,1024]{1,0:T(4,128)S(1)}) custom-call(f32[512,1024]{1,0:T(8,128)S(1)} %copy-done.33, f32[512,1024]{1,0:T(8,128)S(1)} %copy-done.17, bf16[512,1024]{1,0:T(8,128)(2,1)S(1)} %bitcast.343, f32[1,1024]{1,0:T(1,128)S(1)} %bitcast.368, ...), custom_call_target="tpu_custom_call" | custom-call | flops 1073741824 | bytes 11554816 | tf_op jit(solution)/shard_map/pallas_call | solution.py:162
  96.8 2.0 shard_map.282
  100.1 1.7 collective-permute-start.14
  102.0 2.2 copy-done.6
  104.2 5.0 %shard_map.283 = (bf16[8,2,160,256]{3,2,1,0:T(8,128)(2,1)S(1)}, bf16[8,2,160,256]{3,2,1,0:T(8,128)(2,1)S(1)}, bf16[8,2,192,256]{3,2,1,0:T(8,128)(2,1)S(1)}) custom-call(s32[1]{0:T(128)} %bitcast.4.half_ref, bf16[512,4096]{1,0:T(8,128)(2,1)S(1)} %copy-done.6, bf16[512,1024]{1,0:T(8,128)(2,1)S(1)} %bitcast.344, ...), custom_call_target="tpu_custom_call" | custom-call | flops 2147483648 | bytes 13631488 | tf_op jit(solution)/shard_map/pallas_call | solution.py:162
  109.4 6.5 %collective-permute-start.13 = (bf16[1536,256]{1,0:T(8,128)(2,1)S(1)}, bf16[1536,256]{1,0:T(8,128)(2,1)S(1)}, u32[]{:S(2)}, u32[]{:S(2)}) collective-permute-start(bf16[1536,256]{1,0:T(8,128)(2,1)S(1)} %bitcast.422), channel_id=1, source_target_pairs={{0,8},{8,0},{16,24},{24,16},{1,9},{9,1},{17,25},{25,17},{2,10},{10... | collective-permute-start | bytes 2359304 | tf_op jit(solution)/shard_map/ppermute | solution.py:600
  116.8 1.7 fusion.47
  118.8 4.5 %shard_map.284 = (bf16[8,2,320,256]{3,2,1,0:T(8,128)(2,1)S(1)}, bf16[8,2,192,256]{3,2,1,0:T(8,128)(2,1)S(1)}) custom-call(s32[1]{0:T(128)} %bitcast.4.half_ref, bf16[512,1024]{1,0:T(8,128)(2,1)S(1)} %copy-done.25, bf16[512,4096]{1,0:T(8,128)(2,1)S(1)} %copy-done.12, bf16[8,2,512,256]{3,2,1,0:T(8,128)(2,1)} %collective-permute-done.8.refs_2_), custom_call_target="tpu_custom_call" | custom-call | flops 2147483648 | bytes 13631488 | tf_op jit(solution)/shard_map/pallas_call | solution.py:162
  123.3 2.4 shard_map.285
  128.5 3.0 %collective-permute-start.10 = (bf16[2560,256]{1,0:T(8,128)(2,1)S(1)}, bf16[2560,256]{1,0:T(8,128)(2,1)S(1)}, u32[]{:S(2)}, u32[]{:S(2)}) collective-permute-start(bf16[2560,256]{1,0:T(8,128)(2,1)S(1)} %bitcast.413), channel_id=1, source_target_pairs={{0,4},{4,0},{1,5},{5,1},{2,6},{6,2},{3,7},{7,3},{8,12},{12,8},{9,1... | collective-permute-start | bytes 3932168 | tf_op jit(solution)/shard_map/ppermute | solution.py:482
  132.1 1.8 collective-permute-done.11
  134.2 5.3 %collective-permute-start.17 = (bf16[768,256]{1,0:T(8,128)(2,1)S(1)}, bf16[768,256]{1,0:T(8,128)(2,1)S(1)}, u32[]{:S(2)}, u32[]{:S(2)}) collective-permute-start(bf16[768,256]{1,0:T(8,128)(2,1)S(1)} %bitcast.438), channel_id=1, source_target_pairs={{0,16},{8,24},{16,0},{24,8},{1,17},{9,25},{17,1},{25,9},{2,18},{10... | collective-permute-start | bytes 1179656 | tf_op jit(solution)/shard_map/ppermute | solution.py:600
  139.6 2.0 collective-permute-start.16
  141.6 16.2 %shard_map.286.b_ref.dq_ref = bf16[2048,768]{1,0:T(8,128)(2,1)S(1)} custom-call(s32[8,8]{1,0:T(8,128)S(1)} %select_reduce_fusion.2.lst, s32[8]{0:T(128)S(1)} %get-tuple-element.305.cnt, s32[8]{0:T(128)S(1)} %bitcast.374, bf16[2048,768]{1,0:T(8,128)(2,1)S(1)} %copy-done.10, bf16[2048,768]{1,0:T(8,128)(2,1)S(1)} %copy-done.10, ...), custom_call_target="tpu_custom_call" | custom-call | flops 20000000000 | bytes 14729216 | tf_op jit(solution)/shard_map/pallas_call | solution.py:141
  158.6 1.7 collective-permute-done.9
  162.1 5.2 %collective-permute-start.22 = (bf16[320,256]{1,0:T(8,128)(2,1)}, bf16[320,256]{1,0:T(8,128)(2,1)}, u32[]{:S(2)}, u32[]{:S(2)}) collective-permute-start(bf16[320,256]{1,0:T(8,128)(2,1)} %bitcast.70), channel_id=1, source_target_pairs={{0,16},{8,24},{16,0},{24,8},{1,17},{9,25},{17,1},{25,9},{2,18},{10... | collective-permute-start | bytes 491528 | tf_op jit(solution)/shard_map/ppermute | solution.py:600
  168.5 4.0 %collective-permute-start.21 = (bf16[1280,256]{1,0:T(8,128)(2,1)}, bf16[1280,256]{1,0:T(8,128)(2,1)}, u32[]{:S(2)}, u32[]{:S(2)}) collective-permute-start(bf16[1280,256]{1,0:T(8,128)(2,1)} %bitcast.54), channel_id=1, source_target_pairs={{0,8},{8,0},{16,24},{24,16},{1,9},{9,1},{17,25},{25,17},{2,10},{10... | collective-permute-start | bytes 1966088 | tf_op jit(solution)/shard_map/ppermute | solution.py:600
  175.1 4.6 %shard_map.287 = bf16[8,384,256]{2,1,0:T(8,128)(2,1)S(1)} custom-call(bf16[2048,1024]{1,0:T(8,128)(2,1)S(1)} %copy-done.1, bf16[2048,768]{1,0:T(8,128)(2,1)S(1)} %shard_map.286.b_ref.dq_ref), custom_call_target="tpu_custom_call" | custom-call | flops 402653184 | bytes 1114112 | tf_op jit(solution)/shard_map/pallas_call | solution.py:162
  179.7 1.1 copy-done.23
  183.2 1.2 copy-done.21
  185.0 6.0 %shard_map.288 = (bf16[512,1024]{1,0:T(8,128)(2,1)S(1)}, bf16[512,1024]{1,0:T(8,128)(2,1)S(1)}, f32[2,1024]{1,0:T(2,128)S(1)}) custom-call(bf16[2048,768]{1,0:T(8,128)(2,1)S(1)} %shard_map.286.b_ref.dq_ref, bf16[1024,768]{1,0:T(8,128)(2,1)S(1)} %collective-permute-done.18.got_ref, bf16[1024,768]{1,0:T(8,128)(2,1)S(1)} %copy-done.4, ...), custom_call_target="tpu_custom_call" | custom-call | flops 402653184 | bytes 1770496 | tf_op jit(solution)/shard_map/pallas_call | solution.py:162
  191.0 1.5 pad_maximum_fusion
  194.5 3.0 %collective-permute-done.20 = bf16[4,480,256]{2,1,0:T(8,128)(2,1)} collective-permute-done((bf16[4,480,256]{2,1,0:T(8,128)(2,1)}, bf16[4,480,256]{2,1,0:T(8,128)(2,1)}, u32[]{:S(2)}, u32[]{:S(2)}) %collective-permute-start.20) | collective-permute-done | bytes 983072 | tf_op jit(solution)/shard_map/ppermute | solution.py:482
  197.5 1.3 add_convert_fusion.4
  199.4 1.1 add_convert_fusion.1
  201.2 3.4 %copy-done.19 = bf16[4096,1024]{1,0:T(8,128)(2,1)S(1)} copy-done((bf16[4096,1024]{1,0:T(8,128)(2,1)S(1)}, bf16[4096,1024]{1,0:T(8,128)(2,1)}, u32[]{:S(2)}) %copy-start.19) | copy-done | bytes 8388632
  204.5 6.6 %shard_map.289 = bf16[512,1024]{1,0:T(8,128)(2,1)} custom-call(bf16[512,4096]{1,0:T(8,128)(2,1)S(1)} %copy-done.7, bf16[4096,1024]{1,0:T(8,128)(2,1)S(1)} %copy-done.19, f32[512,1024]{1,0:T(8,128)S(1)} %copy-done.18, f32[1,1024]{1,0:T(1,128)S(1)} %bitcast.371), custom_call_target="tpu_custom_call" | custom-call | flops 536870912 | bytes 1966592 | tf_op jit(solution)/shard_map/pallas_call | solution.py:162
  214.9 2.4 collective-permute-done.23
  219.0 1.2 fusion.13
  226.0 2.2 add_bitcast_fusion
  228.3 7.4 %collective-permute-done.27 = bf16[480,256]{1,0:T(8,128)(2,1)S(1)} collective-permute-done((bf16[480,256]{1,0:T(8,128)(2,1)S(1)}, bf16[480,256]{1,0:T(8,128)(2,1)S(1)}, u32[]{:S(2)}, u32[]{:S(2)}) %collective-permute-start.27) | collective-permute-done | bytes 245792 | tf_op jit(solution)/shard_map/ppermute | solution.py:600
  235.7 3.2 %collective-permute-done.26 = bf16[800,256]{1,0:T(8,128)(2,1)S(1)} collective-permute-done((bf16[800,256]{1,0:T(8,128)(2,1)S(1)}, bf16[800,256]{1,0:T(8,128)(2,1)S(1)}, u32[]{:S(2)}, u32[]{:S(2)}) %collective-permute-start.26) | collective-permute-done | bytes 409632 | tf_op jit(solution)/shard_map/ppermute | solution.py:600
  239.7 1.4 collective-permute-start.30
  241.8 9.3 %collective-permute-done.29 = bf16[400,256]{1,0:T(8,128)(2,1)S(1)} collective-permute-done((bf16[400,256]{1,0:T(8,128)(2,1)S(1)}, bf16[400,256]{1,0:T(8,128)(2,1)S(1)}, u32[]{:S(2)}, u32[]{:S(2)}) %collective-permute-start.29) | collective-permute-done | bytes 204832 | tf_op jit(solution)/shard_map/ppermute | solution.py:600
  251.1 2.1 collective-permute-done.30
  255.4 1.4 collective-permute-start.31
  257.5 1.7 broadcast_select_fusion.3
  260.5 1.5 convert_element_type.644
  262.1 1.6 maximum_convert_fusion
  263.9 1.6 collective-permute-done.33
  265.9 1.3 convert_element_type.651
  (366 shorter events, 46.9 us)
Async XLA Ops:
  0.6 14.2 %collective-permute-start.1 = (bf16[512,1024]{1,0:T(8,128)(2,1)}, bf16[512,1024]{1,0:T(8,128)(2,1)S(1)}, u32[]{:S(2)}, u32[]{:S(2)}) collective-permute-start(bf16[512,1024]{1,0:T(8,128)(2,1)} %bitcast.333), channel_id=1, source_target_pairs={{0,1},{1,0},{2,3},{3,2},{4,5},{5,4},{6,7},{7,6},{8,9},{9,8},{10,11... | collective-permute-start | bytes 3145736 | tf_op jit(solution)/shard_map/ppermute | solution.py:485
  1.2 26.6 %collective-permute-start = (bf16[512,1024]{1,0:T(8,128)(2,1)}, bf16[512,1024]{1,0:T(8,128)(2,1)S(1)}, u32[]{:S(2)}, u32[]{:S(2)}) collective-permute-start(bf16[512,1024]{1,0:T(8,128)(2,1)} %bitcast.334), channel_id=1, source_target_pairs={{0,2},{2,0},{1,3},{3,1},{4,6},{6,4},{5,7},{7,5},{8,10},{10,8},{9,1... | collective-permute-start | bytes 3145736 | tf_op jit(solution)/shard_map/ppermute | solution.py:482
  9.9 20.9 %copy-start.3 = (bf16[1024,768]{1,0:T(8,128)(2,1)}, bf16[1024,768]{1,0:T(8,128)(2,1)S(1)}, u32[]{:S(2)}) copy-start(bf16[1024,768]{1,0:T(8,128)(2,1)S(1)} %pad_maximum_fusion.1.w_ref) | copy-start | bytes 4718596
  27.7 3.0 %collective-permute-start.2 = (bf16[512,1024]{1,0:T(8,128)(2,1)S(1)}, bf16[512,1024]{1,0:T(8,128)(2,1)S(1)}, u32[]{:S(2)}, u32[]{:S(2)}) collective-permute-start(bf16[512,1024]{1,0:T(8,128)(2,1)S(1)} %collective-permute-done.x_ref), channel_id=1, source_target_pairs={{0,1},{1,0},{2,3},{3,2},{4,5},{5,4},{6,7},{7,6},{8,9},{9,8},{10,11... | collective-permute-start | bytes 3145736 | tf_op jit(solution)/shard_map/ppermute | solution.py:485
  30.7 31.0 %slice-start.2 = ((s8[8388608]{0:T(1024)(128)(4,1)}), s8[4194304]{0:T(1024)(128)(4,1)S(1)}, s32[]{:S(2)}) async-start(s8[8388608]{0:T(1024)(128)(4,1)} %bitcast.375), calls=%async_computation.2 | async-start | bytes 8388608
  33.2 9.8 %copy-start = (bf16[2048,1024]{1,0:T(8,128)(2,1)}, bf16[2048,1024]{1,0:T(8,128)(2,1)S(1)}, u32[]{:S(2)}) copy-start(bf16[2048,1024]{1,0:T(8,128)(2,1)S(1)} %get-tuple-element.132.a_ref) | copy-start | bytes 12582916
  33.2 9.8 %copy-start.9 = (bf16[2048,768]{1,0:T(8,128)(2,1)}, bf16[2048,768]{1,0:T(8,128)(2,1)S(1)}, u32[]{:S(2)}) copy-start(bf16[2048,768]{1,0:T(8,128)(2,1)S(1)} %get-tuple-element.133.q_ref.k_ref.v_ref) | copy-start | bytes 9437188
  33.2 28.5 %slice-start.3 = ((s8[8388608]{0:T(1024)(128)(4,1)}), s8[4194304]{0:T(1024)(128)(4,1)S(1)}, s32[]{:S(2)}) async-start(s8[8388608]{0:T(1024)(128)(4,1)} %bitcast.375), calls=%async_computation.3 | async-start | bytes 8388608
  43.0 14.7 %copy-start.26 = (bf16[2048,256]{1,0:T(8,128)(2,1)}, bf16[2048,256]{1,0:T(8,128)(2,1)S(1)}, u32[]{:S(2)}) copy-start(bf16[2048,256]{1,0:T(8,128)(2,1)S(1)} %get-tuple-element.134.refs_0_.ctx_ref) | copy-start | bytes 3145732
  44.0 2.6 collective-permute-start.3
  44.5 9.2 %collective-permute-start.4 = (bf16[512,256]{1,0:T(8,128)(2,1)S(1)}, bf16[512,256]{1,0:T(8,128)(2,1)S(1)}, u32[]{:S(2)}, u32[]{:S(2)}) collective-permute-start(bf16[512,256]{1,0:T(8,128)(2,1)S(1)} %get-tuple-element.275), channel_id=1, source_target_pairs={{0,2},{1,3},{2,0},{3,1},{4,6},{5,7},{6,4},{7,5},{8,10},{9,11},{10,... | collective-permute-start | bytes 786440 | tf_op jit(solution)/shard_map/ppermute | solution.py:491
  46.3 11.4 %collective-permute-start.5 = (bf16[512,256]{1,0:T(8,128)(2,1)S(1)}, bf16[512,256]{1,0:T(8,128)(2,1)S(1)}, u32[]{:S(2)}, u32[]{:S(2)}) collective-permute-start(bf16[512,256]{1,0:T(8,128)(2,1)S(1)} %get-tuple-element.274), channel_id=1, source_target_pairs={{0,3},{1,2},{2,1},{3,0},{4,7},{5,6},{6,5},{7,4},{8,11},{9,10},{10,... | collective-permute-start | bytes 786440 | tf_op jit(solution)/shard_map/ppermute | solution.py:491
  46.4 11.3 %copy-start.2 = (bf16[1024,1024]{1,0:T(8,128)(2,1)S(1)}, bf16[1024,1024]{1,0:T(8,128)(2,1)}, u32[]{:S(2)}) copy-start(bf16[1024,1024]{1,0:T(8,128)(2,1)} %w_ref.6) | copy-start | bytes 6291460
  46.4 11.3 %copy-start.43 = (f32[1024]{0:T(1024)S(1)}, f32[1024]{0:T(1024)}, u32[]{:S(2)}) copy-start(f32[1024]{0:T(1024)} %param.24) | copy-start | bytes 12292
  46.4 11.3 %copy-start.44 = (f32[1024]{0:T(1024)S(1)}, f32[1024]{0:T(1024)}, u32[]{:S(2)}) copy-start(f32[1024]{0:T(1024)} %param.23) | copy-start | bytes 12292
  46.4 11.3 %copy-start.45 = (f32[1024]{0:T(1024)S(1)}, f32[1024]{0:T(1024)}, u32[]{:S(2)}) copy-start(f32[1024]{0:T(1024)} %param.25) | copy-start | bytes 12292
  46.6 13.8 %copy-start.20 = (bf16[2048,1024]{1,0:T(8,128)(2,1)}, bf16[2048,1024]{1,0:T(8,128)(2,1)S(1)}, u32[]{:S(2)}) copy-start(bf16[2048,1024]{1,0:T(8,128)(2,1)S(1)} %constant_dynamic-update-slice_fusion.x_ref) | copy-start | bytes 12582916
  61.7 21.1 %copy-start.24 = (bf16[512,1024]{1,0:T(8,128)(2,1)}, bf16[512,1024]{1,0:T(8,128)(2,1)S(1)}, u32[]{:S(2)}) copy-start(bf16[512,1024]{1,0:T(8,128)(2,1)S(1)} %get-tuple-element.166.h_ref.refs_0_) | copy-start | bytes 3145732
  82.3 19.8 %collective-permute-start.6 = (bf16[8,2,512,256]{3,2,1,0:T(8,128)(2,1)}, bf16[8,2,512,256]{3,2,1,0:T(8,128)(2,1)}, u32[]{:S(2)}, u32[]{:S(2)}) collective-permute-start(bf16[8,2,512,256]{3,2,1,0:T(8,128)(2,1)} %shard_map.279), channel_id=1, source_target_pairs={{0,1},{1,0},{2,3},{3,2},{4,5},{5,4},{6,7},{7,6},{8,9},{9,8},{10,11... | collective-permute-start | bytes 12582920 | tf_op jit(solution)/shard_map/ppermute | solution.py:485
  87.0 31.7 %collective-permute-start.8 = (bf16[8,2,512,256]{3,2,1,0:T(8,128)(2,1)}, bf16[8,2,512,256]{3,2,1,0:T(8,128)(2,1)}, u32[]{:S(2)}, u32[]{:S(2)}) collective-permute-start(bf16[8,2,512,256]{3,2,1,0:T(8,128)(2,1)} %shard_map.280), channel_id=1, source_target_pairs={{0,1},{1,0},{2,3},{3,2},{4,5},{5,4},{6,7},{7,6},{8,9},{9,8},{10,11... | collective-permute-start | bytes 12582920 | tf_op jit(solution)/shard_map/ppermute | solution.py:485
  98.8 10.5 %collective-permute-start.7 = (bf16[8,2,128,256]{3,2,1,0:T(8,128)(2,1)}, bf16[8,2,128,256]{3,2,1,0:T(8,128)(2,1)}, u32[]{:S(2)}, u32[]{:S(2)}) collective-permute-start(bf16[8,2,128,256]{3,2,1,0:T(8,128)(2,1)} %shard_map.282), channel_id=1, source_target_pairs={{0,1},{1,0},{2,3},{3,2},{4,5},{5,4},{6,7},{7,6},{8,9},{9,8},{10,11... | collective-permute-start | bytes 3145736 | tf_op jit(solution)/shard_map/ppermute | solution.py:485
  100.1 16.7 %collective-permute-start.14 = (bf16[1024,256]{1,0:T(8,128)(2,1)}, bf16[1024,256]{1,0:T(8,128)(2,1)}, u32[]{:S(2)}, u32[]{:S(2)}) collective-permute-start(bf16[1024,256]{1,0:T(8,128)(2,1)} %pad_maximum_fusion.10), channel_id=1, source_target_pairs={{0,2},{2,0},{1,3},{3,1},{4,6},{6,4},{5,7},{7,5},{8,10},{10,8},{9,1... | collective-permute-start | bytes 1572872 | tf_op jit(solution)/shard_map/ppermute | solution.py:482
  109.3 49.3 %copy-start.36 = (bf16[8,2,192,256]{3,2,1,0:T(8,128)(2,1)}, bf16[8,2,192,256]{3,2,1,0:T(8,128)(2,1)S(1)}, u32[]{:S(2)}) copy-start(bf16[8,2,192,256]{3,2,1,0:T(8,128)(2,1)S(1)} %get-tuple-element.162) | copy-start | bytes 4718596
  109.4 24.6 %collective-permute-start.13 = (bf16[1536,256]{1,0:T(8,128)(2,1)S(1)}, bf16[1536,256]{1,0:T(8,128)(2,1)S(1)}, u32[]{:S(2)}, u32[]{:S(2)}) collective-permute-start(bf16[1536,256]{1,0:T(8,128)(2,1)S(1)} %bitcast.422), channel_id=1, source_target_pairs={{0,8},{8,0},{16,24},{24,16},{1,9},{9,1},{17,25},{25,17},{2,10},{10... | collective-permute-start | bytes 2359304 | tf_op jit(solution)/shard_map/ppermute | solution.py:600
  115.9 45.4 %copy-start.52 = (bf16[4,1,2,160,256]{4,3,2,1,0:T(8,128)(2,1)}, bf16[4,1,2,160,256]{4,3,2,1,0:T(8,128)(2,1)S(1)}, u32[]{:S(2)}) copy-start(bf16[4,1,2,160,256]{4,3,2,1,0:T(8,128)(2,1)S(1)} %get-tuple-element.263) | copy-start | bytes 1966084
  116.0 16.2 %collective-permute-start.12 = (bf16[1280,256]{1,0:T(8,128)(2,1)S(1)}, bf16[1280,256]{1,0:T(8,128)(2,1)S(1)}, u32[]{:S(2)}, u32[]{:S(2)}) collective-permute-start(bf16[1280,256]{1,0:T(8,128)(2,1)S(1)} %bitcast.431), channel_id=1, source_target_pairs={{0,4},{4,0},{1,5},{5,1},{2,6},{6,2},{3,7},{7,3},{8,12},{12,8},{9,1... | collective-permute-start | bytes 1966088 | tf_op jit(solution)/shard_map/ppermute | solution.py:482
  116.2 17.7 %collective-permute-start.11 = (bf16[1280,256]{1,0:T(8,128)(2,1)S(1)}, bf16[1280,256]{1,0:T(8,128)(2,1)S(1)}, u32[]{:S(2)}, u32[]{:S(2)}) collective-permute-start(bf16[1280,256]{1,0:T(8,128)(2,1)S(1)} %bitcast.430), channel_id=1, source_target_pairs={{0,2},{2,0},{1,3},{3,1},{4,6},{6,4},{5,7},{7,5},{8,10},{10,8},{9,1... | collective-permute-start | bytes 1966088 | tf_op jit(solution)/shard_map/ppermute | solution.py:482
  118.5 9.9 %collective-permute-start.15 = (bf16[1024,256]{1,0:T(8,128)(2,1)S(1)}, bf16[1024,256]{1,0:T(8,128)(2,1)S(1)}, u32[]{:S(2)}, u32[]{:S(2)}) collective-permute-start(bf16[1024,256]{1,0:T(8,128)(2,1)S(1)} %pad_maximum_fusion.11), channel_id=1, source_target_pairs={{0,1},{1,0},{2,3},{3,2},{4,5},{5,4},{6,7},{7,6},{8,9},{9,8},{10,11... | collective-permute-start | bytes 1572872 | tf_op jit(solution)/shard_map/ppermute | solution.py:485
  125.9 34.5 %collective-permute-start.9 = (bf16[2560,256]{1,0:T(8,128)(2,1)S(1)}, bf16[2560,256]{1,0:T(8,128)(2,1)S(1)}, u32[]{:S(2)}, u32[]{:S(2)}) collective-permute-start(bf16[2560,256]{1,0:T(8,128)(2,1)S(1)} %bitcast.412), channel_id=1, source_target_pairs={{0,2},{2,0},{1,3},{3,1},{4,6},{6,4},{5,7},{7,5},{8,10},{10,8},{9,1... | collective-permute-start | bytes 3932168 | tf_op jit(solution)/shard_map/ppermute | solution.py:482
  127.0 40.2 %copy-start.49 = (bf16[4,1,2,320,256]{4,3,2,1,0:T(8,128)(2,1)}, bf16[4,1,2,320,256]{4,3,2,1,0:T(8,128)(2,1)S(1)}, u32[]{:S(2)}) copy-start(bf16[4,1,2,320,256]{4,3,2,1,0:T(8,128)(2,1)S(1)} %get-tuple-element.255) | copy-start | bytes 3932164
  128.5 32.1 %collective-permute-start.10 = (bf16[2560,256]{1,0:T(8,128)(2,1)S(1)}, bf16[2560,256]{1,0:T(8,128)(2,1)S(1)}, u32[]{:S(2)}, u32[]{:S(2)}) collective-permute-start(bf16[2560,256]{1,0:T(8,128)(2,1)S(1)} %bitcast.413), channel_id=1, source_target_pairs={{0,4},{4,0},{1,5},{5,1},{2,6},{6,2},{3,7},{7,3},{8,12},{12,8},{9,1... | collective-permute-start | bytes 3932168 | tf_op jit(solution)/shard_map/ppermute | solution.py:482
  131.5 10.1 %copy-start.27 = (bf16[2048,256]{1,0:T(8,128)(2,1)S(1)}, bf16[2048,256]{1,0:T(8,128)(2,1)}, u32[]{:S(2)}) copy-start(bf16[2048,256]{1,0:T(8,128)(2,1)} %copy-done.26) | copy-start | bytes 3145732
  131.6 10.0 %copy-start.10 = (bf16[2048,768]{1,0:T(8,128)(2,1)S(1)}, bf16[2048,768]{1,0:T(8,128)(2,1)}, u32[]{:S(2)}) copy-start(bf16[2048,768]{1,0:T(8,128)(2,1)} %copy-done.9) | copy-start | bytes 9437188
  132.1 29.2 %copy-start.57 = (bf16[1280,256]{1,0:T(8,128)(2,1)}, bf16[1280,256]{1,0:T(8,128)(2,1)S(1)}, u32[]{:S(2)}) copy-start(bf16[1280,256]{1,0:T(8,128)(2,1)S(1)} %collective-permute-done.12) | copy-start | bytes 1966084
  133.9 24.6 %copy-start.56 = (bf16[1536,256]{1,0:T(8,128)(2,1)}, bf16[1536,256]{1,0:T(8,128)(2,1)S(1)}, u32[]{:S(2)}) copy-start(bf16[1536,256]{1,0:T(8,128)(2,1)S(1)} %collective-permute-done.13) | copy-start | bytes 2359300
  134.2 24.4 %collective-permute-start.17 = (bf16[768,256]{1,0:T(8,128)(2,1)S(1)}, bf16[768,256]{1,0:T(8,128)(2,1)S(1)}, u32[]{:S(2)}, u32[]{:S(2)}) collective-permute-start(bf16[768,256]{1,0:T(8,128)(2,1)S(1)} %bitcast.438), channel_id=1, source_target_pairs={{0,16},{8,24},{16,0},{24,8},{1,17},{9,25},{17,1},{25,9},{2,18},{10... | collective-permute-start | bytes 1179656 | tf_op jit(solution)/shard_map/ppermute | solution.py:600
  139.6 19.0 %collective-permute-start.16 = (bf16[640,256]{1,0:T(8,128)(2,1)S(1)}, bf16[640,256]{1,0:T(8,128)(2,1)S(1)}, u32[]{:S(2)}, u32[]{:S(2)}) collective-permute-start(bf16[640,256]{1,0:T(8,128)(2,1)S(1)} %bitcast.442), channel_id=1, source_target_pairs={{0,8},{8,0},{16,24},{24,16},{1,9},{9,1},{17,25},{25,17},{2,10},{10... | collective-permute-start | bytes 983048 | tf_op jit(solution)/shard_map/ppermute | solution.py:600
  158.6 9.9 %copy-start.65 = (bf16[640,256]{1,0:T(8,128)(2,1)}, bf16[640,256]{1,0:T(8,128)(2,1)S(1)}, u32[]{:S(2)}) copy-start(bf16[640,256]{1,0:T(8,128)(2,1)S(1)} %collective-permute-done.16) | copy-start | bytes 983044
  158.6 22.9 %copy-start.62 = (bf16[768,256]{1,0:T(8,128)(2,1)}, bf16[768,256]{1,0:T(8,128)(2,1)S(1)}, u32[]{:S(2)}) copy-start(bf16[768,256]{1,0:T(8,128)(2,1)S(1)} %collective-permute-done.17) | copy-start | bytes 1179652
  160.5 19.1 %copy-start.54 = (bf16[2560,256]{1,0:T(8,128)(2,1)}, bf16[2560,256]{1,0:T(8,128)(2,1)S(1)}, u32[]{:S(2)}) copy-start(bf16[2560,256]{1,0:T(8,128)(2,1)S(1)} %collective-permute-done.10) | copy-start | bytes 3932164
  162.1 32.4 %collective-permute-start.22 = (bf16[320,256]{1,0:T(8,128)(2,1)}, bf16[320,256]{1,0:T(8,128)(2,1)}, u32[]{:S(2)}, u32[]{:S(2)}) collective-permute-start(bf16[320,256]{1,0:T(8,128)(2,1)} %bitcast.70), channel_id=1, source_target_pairs={{0,16},{8,24},{16,0},{24,8},{1,17},{9,25},{17,1},{25,9},{2,18},{10... | collective-permute-start | bytes 491528 | tf_op jit(solution)/shard_map/ppermute | solution.py:600
  168.5 26.0 %collective-permute-start.21 = (bf16[1280,256]{1,0:T(8,128)(2,1)}, bf16[1280,256]{1,0:T(8,128)(2,1)}, u32[]{:S(2)}, u32[]{:S(2)}) collective-permute-start(bf16[1280,256]{1,0:T(8,128)(2,1)} %bitcast.54), channel_id=1, source_target_pairs={{0,8},{8,0},{16,24},{24,16},{1,9},{9,1},{17,25},{25,17},{2,10},{10... | collective-permute-start | bytes 1966088 | tf_op jit(solution)/shard_map/ppermute | solution.py:600
  173.5 23.9 %collective-permute-start.20 = (bf16[4,480,256]{2,1,0:T(8,128)(2,1)}, bf16[4,480,256]{2,1,0:T(8,128)(2,1)}, u32[]{:S(2)}, u32[]{:S(2)}) collective-permute-start(bf16[4,480,256]{2,1,0:T(8,128)(2,1)} %pad_maximum_fusion.8), channel_id=1, source_target_pairs={{0,4},{4,0},{1,5},{5,1},{2,6},{6,2},{3,7},{7,3},{8,12},{12,8},{9,1... | collective-permute-start | bytes 2949128 | tf_op jit(solution)/shard_map/ppermute | solution.py:482
  173.9 9.3 %collective-permute-start.18 = (bf16[1024,768]{1,0:T(8,128)(2,1)S(1)}, bf16[1024,768]{1,0:T(8,128)(2,1)S(1)}, u32[]{:S(2)}, u32[]{:S(2)}) collective-permute-start(bf16[1024,768]{1,0:T(8,128)(2,1)S(1)} %bitcast.405), channel_id=1, source_target_pairs={{0,1},{1,0},{2,3},{3,2},{4,5},{5,4},{6,7},{7,6},{8,9},{9,8},{10,11... | collective-permute-start | bytes 4718600 | tf_op jit(solution)/shard_map/ppermute | solution.py:485
  192.7 46.2 %copy-start.51 = (bf16[4,1,400,256]{3,2,1,0:T(8,128)(2,1)}, bf16[4,1,400,256]{3,2,1,0:T(8,128)(2,1)S(1)}, u32[]{:S(2)}) copy-start(bf16[4,1,400,256]{3,2,1,0:T(8,128)(2,1)S(1)} %get-tuple-element.261) | copy-start | bytes 2457604
  192.7 8.4 %copy-start.18 = (f32[512,1024]{1,0:T(8,128)S(1)}, f32[512,1024]{1,0:T(8,128)}, u32[]{:S(2)}) copy-start(f32[512,1024]{1,0:T(8,128)} %copy-done.16) | copy-start | bytes 6291460
  192.8 25.1 %collective-permute-start.19 = (bf16[1984,256]{1,0:T(8,128)(2,1)S(1)}, bf16[1984,256]{1,0:T(8,128)(2,1)S(1)}, u32[]{:S(2)}, u32[]{:S(2)}) collective-permute-start(bf16[1984,256]{1,0:T(8,128)(2,1)S(1)} %pad_maximum_fusion.7), channel_id=1, source_target_pairs={{0,4},{4,0},{1,5},{5,1},{2,6},{6,2},{3,7},{7,3},{8,12},{12,8},{9,1... | collective-permute-start | bytes 3047432 | tf_op jit(solution)/shard_map/ppermute | solution.py:482
  193.6 25.3 %collective-permute-start.25 = (bf16[512,1024]{1,0:T(8,128)(2,1)S(1)}, bf16[512,1024]{1,0:T(8,128)(2,1)S(1)}, u32[]{:S(2)}, u32[]{:S(2)}) collective-permute-start(bf16[512,1024]{1,0:T(8,128)(2,1)S(1)} %get-tuple-element.190), channel_id=1, source_target_pairs={{0,2},{2,0},{1,3},{3,1},{4,6},{6,4},{5,7},{7,5},{8,10},{10,8},{9,1... | collective-permute-start | bytes 3145736 | tf_op jit(solution)/shard_map/ppermute | solution.py:482
  198.8 16.1 %collective-permute-start.24 = (bf16[640,256]{1,0:T(8,128)(2,1)S(1)}, bf16[640,256]{1,0:T(8,128)(2,1)S(1)}, u32[]{:S(2)}, u32[]{:S(2)}) collective-permute-start(bf16[640,256]{1,0:T(8,128)(2,1)S(1)} %bitcast.448), channel_id=1, source_target_pairs={{0,16},{8,24},{16,0},{24,8},{1,17},{9,25},{17,1},{25,9},{2,18},{10... | collective-permute-start | bytes 983048 | tf_op jit(solution)/shard_map/ppermute | solution.py:600
  200.6 16.7 %collective-permute-start.23 = (bf16[960,256]{1,0:T(8,128)(2,1)S(1)}, bf16[960,256]{1,0:T(8,128)(2,1)S(1)}, u32[]{:S(2)}, u32[]{:S(2)}) collective-permute-start(bf16[960,256]{1,0:T(8,128)(2,1)S(1)} %bitcast.434), channel_id=1, source_target_pairs={{0,8},{8,0},{16,24},{24,16},{1,9},{9,1},{17,25},{25,17},{2,10},{10... | collective-permute-start | bytes 1474568 | tf_op jit(solution)/shard_map/ppermute | solution.py:600
  222.2 13.5 %collective-permute-start.28 = (bf16[672,256]{1,0:T(8,128)(2,1)S(1)}, bf16[672,256]{1,0:T(8,128)(2,1)S(1)}, u32[]{:S(2)}, u32[]{:S(2)}) collective-permute-start(bf16[672,256]{1,0:T(8,128)(2,1)S(1)} %pad_maximum_fusion.13), channel_id=1, source_target_pairs={{0,2},{2,0},{1,3},{3,1},{4,6},{6,4},{5,7},{7,5},{8,10},{10,8},{9,1... | collective-permute-start | bytes 1032200 | tf_op jit(solution)/shard_map/ppermute | solution.py:482
  223.0 12.7 %collective-permute-start.27 = (bf16[480,256]{1,0:T(8,128)(2,1)S(1)}, bf16[480,256]{1,0:T(8,128)(2,1)S(1)}, u32[]{:S(2)}, u32[]{:S(2)}) collective-permute-start(bf16[480,256]{1,0:T(8,128)(2,1)S(1)} %fusion.14), channel_id=1, source_target_pairs={{0,16},{8,24},{16,0},{24,8},{1,17},{9,25},{17,1},{25,9},{2,18},{10... | collective-permute-start | bytes 737288 | tf_op jit(solution)/shard_map/ppermute | solution.py:600
  223.1 15.8 %collective-permute-start.26 = (bf16[800,256]{1,0:T(8,128)(2,1)S(1)}, bf16[800,256]{1,0:T(8,128)(2,1)S(1)}, u32[]{:S(2)}, u32[]{:S(2)}) collective-permute-start(bf16[800,256]{1,0:T(8,128)(2,1)S(1)} %bitcast.435), channel_id=1, source_target_pairs={{0,8},{8,0},{16,24},{24,16},{1,9},{9,1},{17,25},{25,17},{2,10},{10... | collective-permute-start | bytes 1228808 | tf_op jit(solution)/shard_map/ppermute | solution.py:600
  228.2 11.0 %copy-start.67 = (bf16[160,256]{1,0:T(8,128)(2,1)S(1)}, bf16[160,256]{1,0:T(8,128)(2,1)}, u32[]{:S(2)}) copy-start(bf16[160,256]{1,0:T(8,128)(2,1)} %get-tuple-element.211) | copy-start | bytes 245764
  228.2 11.0 %copy-start.68 = (bf16[160,256]{1,0:T(8,128)(2,1)S(1)}, bf16[160,256]{1,0:T(8,128)(2,1)}, u32[]{:S(2)}) copy-start(bf16[160,256]{1,0:T(8,128)(2,1)} %get-tuple-element.210) | copy-start | bytes 245764
  228.2 11.1 %copy-start.64 = (bf16[192,256]{1,0:T(8,128)(2,1)S(1)}, bf16[192,256]{1,0:T(8,128)(2,1)}, u32[]{:S(2)}) copy-start(bf16[192,256]{1,0:T(8,128)(2,1)} %dynamic-slice_bitcast_fusion.14) | copy-start | bytes 294916
  228.3 11.1 %copy-start.58 = (bf16[320,256]{1,0:T(8,128)(2,1)S(1)}, bf16[320,256]{1,0:T(8,128)(2,1)}, u32[]{:S(2)}) copy-start(bf16[320,256]{1,0:T(8,128)(2,1)} %dynamic-slice_bitcast_fusion.10) | copy-start | bytes 491524
  228.3 11.1 %copy-start.59 = (bf16[320,256]{1,0:T(8,128)(2,1)S(1)}, bf16[320,256]{1,0:T(8,128)(2,1)}, u32[]{:S(2)}) copy-start(bf16[320,256]{1,0:T(8,128)(2,1)} %dynamic-slice_bitcast_fusion.9) | copy-start | bytes 491524
  239.7 14.7 %copy-start.61 = (bf16[800,256]{1,0:T(8,128)(2,1)S(1)}, bf16[800,256]{1,0:T(8,128)(2,1)}, u32[]{:S(2)}) copy-start(bf16[800,256]{1,0:T(8,128)(2,1)} %copy-done.60) | copy-start | bytes 1228804
  239.7 13.5 %collective-permute-start.30 = (bf16[1152,256]{1,0:T(8,128)(2,1)S(1)}, bf16[1152,256]{1,0:T(8,128)(2,1)S(1)}, u32[]{:S(2)}, u32[]{:S(2)}) collective-permute-start(bf16[1152,256]{1,0:T(8,128)(2,1)S(1)} %slice_dynamic-update-slice_fusion), channel_id=1, source_target_pairs={{0,2},{2,0},{1,3},{3,1},{4,6},{6,4},{5,7},{7,5},{8,10},{10,8},{9,1... | collective-permute-start | bytes 1769480 | tf_op jit(solution)/shard_map/ppermute | solution.py:482
  241.1 10.1 %collective-permute-start.29 = (bf16[400,256]{1,0:T(8,128)(2,1)S(1)}, bf16[400,256]{1,0:T(8,128)(2,1)S(1)}, u32[]{:S(2)}, u32[]{:S(2)}) collective-permute-start(bf16[400,256]{1,0:T(8,128)(2,1)S(1)} %fusion.18), channel_id=1, source_target_pairs={{0,16},{8,24},{16,0},{24,8},{1,17},{9,25},{17,1},{25,9},{2,18},{10... | collective-permute-start | bytes 614408 | tf_op jit(solution)/shard_map/ppermute | solution.py:600
  254.3 3.2 %collective-permute-start.32 = (bf16[2,1152,256]{2,1,0:T(8,128)(2,1)}, bf16[2,1152,256]{2,1,0:T(8,128)(2,1)}, u32[]{:S(2)}, u32[]{:S(2)}) collective-permute-start(bf16[2,1152,256]{2,1,0:T(8,128)(2,1)} %pad_maximum_fusion.3), channel_id=1, source_target_pairs={{0,1},{1,0},{2,3},{3,2},{4,5},{5,4},{6,7},{7,6},{8,9},{9,8},{10,11... | collective-permute-start | bytes 3538952 | tf_op jit(solution)/shard_map/ppermute | solution.py:485
  255.4 8.2 %collective-permute-start.31 = (bf16[400,256]{1,0:T(8,128)(2,1)S(1)}, bf16[400,256]{1,0:T(8,128)(2,1)S(1)}, u32[]{:S(2)}, u32[]{:S(2)}) collective-permute-start(bf16[400,256]{1,0:T(8,128)(2,1)S(1)} %fusion.11), channel_id=1, source_target_pairs={{0,2},{2,0},{1,3},{3,1},{4,6},{6,4},{5,7},{7,5},{8,10},{10,8},{9,1... | collective-permute-start | bytes 614408 | tf_op jit(solution)/shard_map/ppermute | solution.py:482
  263.7 1.8 collective-permute-start.33
  (43 other events, 124.4 us)

commit v3 on v2

--- a/solution.py
+++ b/solution.py
@@ -609,7 +609,7 @@
         return jnp.concatenate([v.reshape(B, -1) for v in vecs], axis=1).astype(BF).reshape(B, -1, W)
 
     hr = w_down.shape[0] // B // 2
-    pr = qr = 5 * hr // 8 // 16 * 16
+    pr = qr = 9 * hr // 16 // 16 * 16
     n_ot = D // B
     ur = hr + n_ot // 2
 

time: 268 us -> 271 us (1.011)
  starting transfers between devices: 44.2 us -> 38.2 us
  Pallas kernels: 102 us -> 107 us
    ppermute x10, starting transfers between devices: 25.5 us -> 18.5 us  [over_z(): lax.ppermute(v, 'z', [(i, i ^ bit) for i in range(Z)])]
    pallas_call x2, Pallas kernels: 26 us -> 31.5 us  [attend(): pl.pallas_call(kernel, out_shape=outs, grid_spec=pltpu.PrefetchScalarGrid...]
    ppermute x10, waiting for transfers between devices: 22.3 us -> 26.9 us  [over_z(): lax.ppermute(v, 'z', [(i, i ^ bit) for i in range(Z)])]
    ppermute x12, waiting for transfers between devices: 14.9 us -> 10.5 us  [shift(): return lax.ppermute(v, axis, [(i, (i + s) % n) for i in range(n)])]
    unnamed x185 -> x187, local copies, waits for them, and re-layouts: 20.9 us -> 22.2 us
  transfers between devices with their start and end apart: 34 -> 34, of which waited for: 17 -> 16; matrix products, arithmetic and copies ran while one was open for 15% -> 15% of each run, Pallas kernels for 25% -> 26%
where the time goes in v3:
time: 271 us; the launch traced here: 272 us
  Pallas kernels  107 us (39%)
  waiting for transfers between devices  50.7 us (19%)
  local copies, waits for them, and re-layouts  38.6 us (14%)
  starting transfers between devices  38.2 us (14%)
  other arithmetic  34.4 us (13%)
    pallas_call x17, Pallas kernels, grid_call(): pl.pallas_call(kernel, out_shape=[o for o, _, _ in outs], grid_spec=pltpu...  75.9 us
    pallas_call x2, Pallas kernels, attend(): pl.pallas_call(kernel, out_shape=outs, grid_spec=pltpu.PrefetchScalarGrid...  31.5 us
    ppermute x10, waiting for transfers between devices, over_z(): lax.ppermute(v, 'z', [(i, i ^ bit) for i in range(Z)])  26.9 us
    unnamed x187, local copies, waits for them, and re-layouts  22.2 us
    ppermute x10, starting transfers between devices, over_z(): lax.ppermute(v, 'z', [(i, i ^ bit) for i in range(Z)])  18.5 us
    ppermute x12, starting transfers between devices, shift(): return lax.ppermute(v, axis, [(i, (i + s) % n) for i in range(n)])  15.4 us
    convert_element_type x18, other arithmetic, settle(): sum((g.astype(F32) for g in terms[1:]), terms[0].astype(F32)).astype(BF)  11.6 us
    ppermute x3, waiting for transfers between devices, hop(): return lax.ppermute(v, ('y', 'c'), pairs)  11.1 us
  transfers between devices with their start and end apart: 34, of which 16 were waited for; matrix products, arithmetic and copies ran while one was open for 15% of the time, Pallas kernels for 26%

profile of v3, /device:TPU:0, one launch (start us, length us, event | category | flops | bytes accessed | tf_op | source)
XLA Modules:
  0.0 271.8 jit_solution(15994199088527074098)
XLA Ops:
  1.2 2.6 collective-permute-start
  7.6 2.1 constant_dynamic-slice_fusion.19
  9.9 1.4 copy-done.8
  11.2 2.3 shard_map.271
  13.6 1.2 pad_maximum_fusion.2.wm_ref
  14.8 2.3 shard_map.272
  17.3 6.2 %shard_map.273.dg_ref = bf16[512,4096]{1,0:T(8,128)(2,1)S(1)} custom-call(bf16[512,1024]{1,0:T(8,128)(2,1)S(1)} %bitcast.341, bf16[4096,1024]{1,0:T(8,128)(2,1)S(1)} %bitcast.346), custom_call_target="tpu_custom_call" | custom-call | flops 4294967296 | bytes 13631488 | tf_op jit(solution)/shard_map/pallas_call | solution.py:162
  23.5 4.2 %collective-permute-done.x_ref = bf16[512,1024]{1,0:T(8,128)(2,1)S(1)} collective-permute-done((bf16[512,1024]{1,0:T(8,128)(2,1)}, bf16[512,1024]{1,0:T(8,128)(2,1)S(1)}, u32[]{:S(2)}, u32[]{:S(2)}) %collective-permute-start) | collective-permute-done | bytes 1048608 | tf_op jit(solution)/shard_map/ppermute | solution.py:482
  28.3 2.3 shard_map.274
  30.7 2.3 shard_map.275
  33.0 11.9 %shard_map.276 = (bf16[2048,256]{1,0:T(8,128)(2,1)S(1)}, f32[4,2048]{1,0:T(4,128)S(1)}) custom-call(s32[8,8]{1,0:T(8,128)S(1)} %select_reduce_fusion.3.lst, s32[8]{0:T(128)S(1)} %get-tuple-element.247.cnt, s32[8]{0:T(128)S(1)} %bitcast.373, bf16[2048,768]{1,0:T(8,128)(2,1)S(1)} %get-tuple-element.133.q_ref.k_ref.v_ref, ...), custom_call_target="tpu_custom_call" | custom-call | flops 12000000000 | bytes 10534912 | tf_op jit(solution)/shard_map/pallas_call | solution.py:141
  46.5 1.8 collective-permute-start.4
  48.5 7.1 %collective-permute-done.4.refs_2_ = bf16[512,256]{1,0:T(8,128)(2,1)S(1)} collective-permute-done((bf16[512,256]{1,0:T(8,128)(2,1)S(1)}, bf16[512,256]{1,0:T(8,128)(2,1)S(1)}, u32[]{:S(2)}, u32[]{:S(2)}) %collective-permute-start.4) | collective-permute-done | bytes 262176 | tf_op jit(solution)/shard_map/ppermute | solution.py:491
  55.6 4.0 %collective-permute-done.5.refs_3_ = bf16[512,256]{1,0:T(8,128)(2,1)S(1)} collective-permute-done((bf16[512,256]{1,0:T(8,128)(2,1)S(1)}, bf16[512,256]{1,0:T(8,128)(2,1)S(1)}, u32[]{:S(2)}, u32[]{:S(2)}) %collective-permute-start.5) | collective-permute-done | bytes 262176 | tf_op jit(solution)/shard_map/ppermute | solution.py:491
  59.7 2.6 shard_map.277
  62.3 1.3 copy-done.16
  63.7 14.3 %shard_map.278 = (bf16[512,4096]{1,0:T(8,128)(2,1)S(1)}, bf16[512,4096]{1,0:T(8,128)(2,1)S(1)}, f32[512,1024]{1,0:T(8,128)S(1)}, f32[1,4096]{1,0:T(1,128)S(1)}) custom-call(bf16[512,1024]{1,0:T(8,128)(2,1)S(1)} %get-tuple-element.166.h_ref.refs_0_, bf16[1024,4096]{1,0:T(8,128)(2,1)S(1)} %bitcast.376, f32[1,4096]{1,0:T(1,128)S(1)} %bitcast.377, ...), custom_call_target="tpu_custom_call" | custom-call | flops 8589934592 | bytes 24150016 | tf_op jit(solution)/shard_map/pallas_call | solution.py:162
  78.0 1.3 copy-done.32
  79.3 5.1 %shard_map.279 = bf16[8,2,512,256]{3,2,1,0:T(8,128)(2,1)} custom-call(s32[1]{0:T(128)} %bitcast.30.half_ref, bf16[512,4096]{1,0:T(8,128)(2,1)S(1)} %get-tuple-element.191.refs_0_.a_ref, bf16[512,1024]{1,0:T(8,128)(2,1)S(1)} %bitcast.342), custom_call_target="tpu_custom_call" | custom-call | flops 2147483648 | bytes 9437184 | tf_op jit(solution)/shard_map/pallas_call | solution.py:162
  85.0 4.2 %shard_map.280 = bf16[8,2,512,256]{3,2,1,0:T(8,128)(2,1)} custom-call(s32[1]{0:T(128)} %bitcast.30.half_ref, bf16[512,1024]{1,0:T(8,128)(2,1)S(1)} %get-tuple-element.166.h_ref.refs_0_, bf16[512,4096]{1,0:T(8,128)(2,1)S(1)} %get-tuple-element.150.refs_1_), custom_call_target="tpu_custom_call" | custom-call | flops 2147483648 | bytes 9437184 | tf_op jit(solution)/shard_map/pallas_call | solution.py:162
  90.1 1.2 copy-done.14
  91.4 1.6 copy-done.17
  93.0 1.6 copy-done.33
  94.5 3.1 %shard_map.281 = (f32[512,1024]{1,0:T(8,128)S(1)}, bf16[512,1024]{1,0:T(8,128)(2,1)S(1)}, bf16[512,1024]{1,0:T(8,128)(2,1)S(1)}, f32[4,1024]{1,0:T(4,128)S(1)}) custom-call(f32[512,1024]{1,0:T(8,128)S(1)} %copy-done.33, f32[512,1024]{1,0:T(8,128)S(1)} %copy-done.17, bf16[512,1024]{1,0:T(8,128)(2,1)S(1)} %bitcast.343, f32[1,1024]{1,0:T(1,128)S(1)} %bitcast.368, ...), custom_call_target="tpu_custom_call" | custom-call | flops 1073741824 | bytes 11554816 | tf_op jit(solution)/shard_map/pallas_call | solution.py:162
  99.7 2.0 shard_map.282
  103.1 1.7 collective-permute-start.14
  105.6 2.2 copy-done.6
  107.8 5.0 %shard_map.283 = (bf16[8,2,144,256]{3,2,1,0:T(8,128)(2,1)S(1)}, bf16[8,2,144,256]{3,2,1,0:T(8,128)(2,1)S(1)}, bf16[8,2,224,256]{3,2,1,0:T(8,128)(2,1)S(1)}) custom-call(s32[1]{0:T(128)} %bitcast.4.half_ref, bf16[512,4096]{1,0:T(8,128)(2,1)S(1)} %copy-done.6, bf16[512,1024]{1,0:T(8,128)(2,1)S(1)} %bitcast.344, ...), custom_call_target="tpu_custom_call" | custom-call | flops 2147483648 | bytes 13631488 | tf_op jit(solution)/shard_map/pallas_call | solution.py:162
  113.3 1.6 collective-permute-start.12
  115.4 2.0 collective-permute-done.14
  118.8 4.6 %shard_map.284 = (bf16[8,2,320,256]{3,2,1,0:T(8,128)(2,1)S(1)}, bf16[8,2,192,256]{3,2,1,0:T(8,128)(2,1)S(1)}) custom-call(s32[1]{0:T(128)} %bitcast.4.half_ref, bf16[512,1024]{1,0:T(8,128)(2,1)S(1)} %copy-done.25, bf16[512,4096]{1,0:T(8,128)(2,1)S(1)} %copy-done.12, bf16[8,2,512,256]{3,2,1,0:T(8,128)(2,1)} %collective-permute-done.8.refs_2_), custom_call_target="tpu_custom_call" | custom-call | flops 2147483648 | bytes 13631488 | tf_op jit(solution)/shard_map/pallas_call | solution.py:162
  124.7 2.4 shard_map.285
  127.2 2.5 collective-permute-start.9
  131.1 1.5 collective-permute-start.10
  132.7 2.3 collective-permute-done.13
  135.3 7.3 %collective-permute-start.17 = (bf16[896,256]{1,0:T(8,128)(2,1)S(1)}, bf16[896,256]{1,0:T(8,128)(2,1)S(1)}, u32[]{:S(2)}, u32[]{:S(2)}) collective-permute-start(bf16[896,256]{1,0:T(8,128)(2,1)S(1)} %bitcast.438), channel_id=1, source_target_pairs={{0,16},{8,24},{16,0},{24,8},{1,17},{9,25},{17,1},{25,9},{2,18},{10... | collective-permute-start | bytes 1376264 | tf_op jit(solution)/shard_map/ppermute | solution.py:600
  142.7 1.8 collective-permute-start.16
  144.5 19.6 %shard_map.286.b_ref.dq_ref = bf16[2048,768]{1,0:T(8,128)(2,1)S(1)} custom-call(s32[8,8]{1,0:T(8,128)S(1)} %select_reduce_fusion.2.lst, s32[8]{0:T(128)S(1)} %get-tuple-element.305.cnt, s32[8]{0:T(128)S(1)} %bitcast.374, bf16[2048,768]{1,0:T(8,128)(2,1)S(1)} %copy-done.10, bf16[2048,768]{1,0:T(8,128)(2,1)S(1)} %copy-done.10, ...), custom_call_target="tpu_custom_call" | custom-call | flops 20000000000 | bytes 14729216 | tf_op jit(solution)/shard_map/pallas_call | solution.py:141
  169.5 6.1 %collective-permute-start.21 = (bf16[1280,256]{1,0:T(8,128)(2,1)}, bf16[1280,256]{1,0:T(8,128)(2,1)}, u32[]{:S(2)}, u32[]{:S(2)}) collective-permute-start(bf16[1280,256]{1,0:T(8,128)(2,1)} %bitcast.54), channel_id=1, source_target_pairs={{0,8},{8,0},{16,24},{24,16},{1,9},{9,1},{17,25},{25,17},{2,10},{10... | collective-permute-start | bytes 1966088 | tf_op jit(solution)/shard_map/ppermute | solution.py:600
  176.8 1.3 copy-done.1
  178.1 4.6 %shard_map.287 = bf16[8,384,256]{2,1,0:T(8,128)(2,1)S(1)} custom-call(bf16[2048,1024]{1,0:T(8,128)(2,1)S(1)} %copy-done.1, bf16[2048,768]{1,0:T(8,128)(2,1)S(1)} %shard_map.286.b_ref.dq_ref), custom_call_target="tpu_custom_call" | custom-call | flops 402653184 | bytes 1114112 | tf_op jit(solution)/shard_map/pallas_call | solution.py:162
  182.7 1.1 copy-done.23
  185.7 1.2 copy-done.21
  187.4 6.0 %shard_map.288 = (bf16[512,1024]{1,0:T(8,128)(2,1)S(1)}, bf16[512,1024]{1,0:T(8,128)(2,1)S(1)}, f32[2,1024]{1,0:T(2,128)S(1)}) custom-call(bf16[2048,768]{1,0:T(8,128)(2,1)S(1)} %shard_map.286.b_ref.dq_ref, bf16[1024,768]{1,0:T(8,128)(2,1)S(1)} %collective-permute-done.18.got_ref, bf16[1024,768]{1,0:T(8,128)(2,1)S(1)} %copy-done.4, ...), custom_call_target="tpu_custom_call" | custom-call | flops 402653184 | bytes 1770496 | tf_op jit(solution)/shard_map/pallas_call | solution.py:162
  194.8 1.5 pad_maximum_fusion
  198.2 1.4 add_convert_fusion.4
  200.1 1.2 add_convert_fusion.1
  201.7 3.4 %copy-done.19 = bf16[4096,1024]{1,0:T(8,128)(2,1)S(1)} copy-done((bf16[4096,1024]{1,0:T(8,128)(2,1)S(1)}, bf16[4096,1024]{1,0:T(8,128)(2,1)}, u32[]{:S(2)}) %copy-start.19) | copy-done | bytes 8388632
  205.1 6.6 %shard_map.289 = bf16[512,1024]{1,0:T(8,128)(2,1)} custom-call(bf16[512,4096]{1,0:T(8,128)(2,1)S(1)} %copy-done.7, bf16[4096,1024]{1,0:T(8,128)(2,1)S(1)} %copy-done.19, f32[512,1024]{1,0:T(8,128)S(1)} %copy-done.18, f32[1,1024]{1,0:T(1,128)S(1)} %bitcast.371), custom_call_target="tpu_custom_call" | custom-call | flops 536870912 | bytes 1966592 | tf_op jit(solution)/shard_map/pallas_call | solution.py:162
  216.6 3.9 %collective-permute-done.23 = bf16[928,256]{1,0:T(8,128)(2,1)S(1)} collective-permute-done((bf16[928,256]{1,0:T(8,128)(2,1)S(1)}, bf16[928,256]{1,0:T(8,128)(2,1)S(1)}, u32[]{:S(2)}, u32[]{:S(2)}) %collective-permute-start.23) | collective-permute-done | bytes 475168 | tf_op jit(solution)/shard_map/ppermute | solution.py:600
  221.1 1.5 collective-permute-done.25
  222.7 1.2 fusion.13
  229.6 2.2 add_bitcast_fusion
  231.9 7.0 %collective-permute-done.27 = bf16[464,256]{1,0:T(8,128)(2,1)S(1)} collective-permute-done((bf16[464,256]{1,0:T(8,128)(2,1)S(1)}, bf16[464,256]{1,0:T(8,128)(2,1)S(1)}, u32[]{:S(2)}, u32[]{:S(2)}) %collective-permute-start.27) | collective-permute-done | bytes 237600 | tf_op jit(solution)/shard_map/ppermute | solution.py:600
  238.9 3.4 %collective-permute-done.26 = bf16[800,256]{1,0:T(8,128)(2,1)S(1)} collective-permute-done((bf16[800,256]{1,0:T(8,128)(2,1)S(1)}, bf16[800,256]{1,0:T(8,128)(2,1)S(1)}, u32[]{:S(2)}, u32[]{:S(2)}) %collective-permute-start.26) | collective-permute-done | bytes 409632 | tf_op jit(solution)/shard_map/ppermute | solution.py:600
  243.1 1.6 collective-permute-start.30
  245.5 9.3 %collective-permute-done.29 = bf16[400,256]{1,0:T(8,128)(2,1)S(1)} collective-permute-done((bf16[400,256]{1,0:T(8,128)(2,1)S(1)}, bf16[400,256]{1,0:T(8,128)(2,1)S(1)}, u32[]{:S(2)}, u32[]{:S(2)}) %collective-permute-start.29) | collective-permute-done | bytes 204832 | tf_op jit(solution)/shard_map/ppermute | solution.py:600
  254.7 1.9 collective-permute-done.30
  258.8 1.6 collective-permute-start.31
  261.0 1.8 broadcast_select_fusion.3
  264.0 1.5 convert_element_type.644
  265.5 1.6 maximum_convert_fusion
  267.3 1.6 collective-permute-done.33
  269.3 1.3 convert_element_type.651
  (368 shorter events, 49.1 us)
Async XLA Ops:
  0.6 14.2 %collective-permute-start.1 = (bf16[512,1024]{1,0:T(8,128)(2,1)}, bf16[512,1024]{1,0:T(8,128)(2,1)S(1)}, u32[]{:S(2)}, u32[]{:S(2)}) collective-permute-start(bf16[512,1024]{1,0:T(8,128)(2,1)} %bitcast.333), channel_id=1, source_target_pairs={{0,1},{1,0},{2,3},{3,2},{4,5},{5,4},{6,7},{7,6},{8,9},{9,8},{10,11... | collective-permute-start | bytes 3145736 | tf_op jit(solution)/shard_map/ppermute | solution.py:485
  1.2 26.6 %collective-permute-start = (bf16[512,1024]{1,0:T(8,128)(2,1)}, bf16[512,1024]{1,0:T(8,128)(2,1)S(1)}, u32[]{:S(2)}, u32[]{:S(2)}) collective-permute-start(bf16[512,1024]{1,0:T(8,128)(2,1)} %bitcast.334), channel_id=1, source_target_pairs={{0,2},{2,0},{1,3},{3,1},{4,6},{6,4},{5,7},{7,5},{8,10},{10,8},{9,1... | collective-permute-start | bytes 3145736 | tf_op jit(solution)/shard_map/ppermute | solution.py:482
  9.7 7.4 %slice-start = ((s8[8388608]{0:T(1024)(128)(4,1)}), s8[4194304]{0:T(1024)(128)(4,1)S(1)}, s32[]{:S(2)}) async-start(s8[8388608]{0:T(1024)(128)(4,1)} %bitcast.345), calls=%async_computation | async-start | bytes 8388608
  9.9 20.8 %copy-start.3 = (bf16[1024,768]{1,0:T(8,128)(2,1)}, bf16[1024,768]{1,0:T(8,128)(2,1)S(1)}, u32[]{:S(2)}) copy-start(bf16[1024,768]{1,0:T(8,128)(2,1)S(1)} %pad_maximum_fusion.1.w_ref) | copy-start | bytes 4718596
  27.7 2.9 %collective-permute-start.2 = (bf16[512,1024]{1,0:T(8,128)(2,1)S(1)}, bf16[512,1024]{1,0:T(8,128)(2,1)S(1)}, u32[]{:S(2)}, u32[]{:S(2)}) collective-permute-start(bf16[512,1024]{1,0:T(8,128)(2,1)S(1)} %collective-permute-done.x_ref), channel_id=1, source_target_pairs={{0,1},{1,0},{2,3},{3,2},{4,5},{5,4},{6,7},{7,6},{8,9},{9,8},{10,11... | collective-permute-start | bytes 3145736 | tf_op jit(solution)/shard_map/ppermute | solution.py:485
  30.7 33.0 %slice-start.2 = ((s8[8388608]{0:T(1024)(128)(4,1)}), s8[4194304]{0:T(1024)(128)(4,1)S(1)}, s32[]{:S(2)}) async-start(s8[8388608]{0:T(1024)(128)(4,1)} %bitcast.375), calls=%async_computation.2 | async-start | bytes 8388608
  33.0 11.9 %copy-start = (bf16[2048,1024]{1,0:T(8,128)(2,1)}, bf16[2048,1024]{1,0:T(8,128)(2,1)S(1)}, u32[]{:S(2)}) copy-start(bf16[2048,1024]{1,0:T(8,128)(2,1)S(1)} %get-tuple-element.132.a_ref) | copy-start | bytes 12582916
  33.0 11.9 %copy-start.9 = (bf16[2048,768]{1,0:T(8,128)(2,1)}, bf16[2048,768]{1,0:T(8,128)(2,1)S(1)}, u32[]{:S(2)}) copy-start(bf16[2048,768]{1,0:T(8,128)(2,1)S(1)} %get-tuple-element.133.q_ref.k_ref.v_ref) | copy-start | bytes 9437188
  33.0 30.6 %slice-start.3 = ((s8[8388608]{0:T(1024)(128)(4,1)}), s8[4194304]{0:T(1024)(128)(4,1)S(1)}, s32[]{:S(2)}) async-start(s8[8388608]{0:T(1024)(128)(4,1)} %bitcast.375), calls=%async_computation.3 | async-start | bytes 8388608
  44.9 14.7 %copy-start.26 = (bf16[2048,256]{1,0:T(8,128)(2,1)}, bf16[2048,256]{1,0:T(8,128)(2,1)S(1)}, u32[]{:S(2)}) copy-start(bf16[2048,256]{1,0:T(8,128)(2,1)S(1)} %get-tuple-element.134.refs_0_.ctx_ref) | copy-start | bytes 3145732
  45.9 2.6 collective-permute-start.3
  46.5 9.2 %collective-permute-start.4 = (bf16[512,256]{1,0:T(8,128)(2,1)S(1)}, bf16[512,256]{1,0:T(8,128)(2,1)S(1)}, u32[]{:S(2)}, u32[]{:S(2)}) collective-permute-start(bf16[512,256]{1,0:T(8,128)(2,1)S(1)} %get-tuple-element.275), channel_id=1, source_target_pairs={{0,2},{1,3},{2,0},{3,1},{4,6},{5,7},{6,4},{7,5},{8,10},{9,11},{10,... | collective-permute-start | bytes 786440 | tf_op jit(solution)/shard_map/ppermute | solution.py:491
  48.2 11.4 %collective-permute-start.5 = (bf16[512,256]{1,0:T(8,128)(2,1)S(1)}, bf16[512,256]{1,0:T(8,128)(2,1)S(1)}, u32[]{:S(2)}, u32[]{:S(2)}) collective-permute-start(bf16[512,256]{1,0:T(8,128)(2,1)S(1)} %get-tuple-element.274), channel_id=1, source_target_pairs={{0,3},{1,2},{2,1},{3,0},{4,7},{5,6},{6,5},{7,4},{8,11},{9,10},{10,... | collective-permute-start | bytes 786440 | tf_op jit(solution)/shard_map/ppermute | solution.py:491
  48.3 11.3 %copy-start.2 = (bf16[1024,1024]{1,0:T(8,128)(2,1)S(1)}, bf16[1024,1024]{1,0:T(8,128)(2,1)}, u32[]{:S(2)}) copy-start(bf16[1024,1024]{1,0:T(8,128)(2,1)} %w_ref.6) | copy-start | bytes 6291460
  48.3 11.3 %copy-start.43 = (f32[1024]{0:T(1024)S(1)}, f32[1024]{0:T(1024)}, u32[]{:S(2)}) copy-start(f32[1024]{0:T(1024)} %param.24) | copy-start | bytes 12292
  48.3 11.3 %copy-start.44 = (f32[1024]{0:T(1024)S(1)}, f32[1024]{0:T(1024)}, u32[]{:S(2)}) copy-start(f32[1024]{0:T(1024)} %param.23) | copy-start | bytes 12292
  48.4 11.3 %copy-start.45 = (f32[1024]{0:T(1024)S(1)}, f32[1024]{0:T(1024)}, u32[]{:S(2)}) copy-start(f32[1024]{0:T(1024)} %param.25) | copy-start | bytes 12292
  48.5 13.8 %copy-start.20 = (bf16[2048,1024]{1,0:T(8,128)(2,1)}, bf16[2048,1024]{1,0:T(8,128)(2,1)S(1)}, u32[]{:S(2)}) copy-start(bf16[2048,1024]{1,0:T(8,128)(2,1)S(1)} %constant_dynamic-update-slice_fusion.x_ref) | copy-start | bytes 12582916
  55.6 6.7 %copy-start.37 = (bf16[512,256]{1,0:T(8,128)(2,1)}, bf16[512,256]{1,0:T(8,128)(2,1)S(1)}, u32[]{:S(2)}) copy-start(bf16[512,256]{1,0:T(8,128)(2,1)S(1)} %collective-permute-done.4.refs_2_) | copy-start | bytes 786436
  63.7 21.4 %copy-start.24 = (bf16[512,1024]{1,0:T(8,128)(2,1)}, bf16[512,1024]{1,0:T(8,128)(2,1)S(1)}, u32[]{:S(2)}) copy-start(bf16[512,1024]{1,0:T(8,128)(2,1)S(1)} %get-tuple-element.166.h_ref.refs_0_) | copy-start | bytes 3145732
  84.4 21.2 %collective-permute-start.6 = (bf16[8,2,512,256]{3,2,1,0:T(8,128)(2,1)}, bf16[8,2,512,256]{3,2,1,0:T(8,128)(2,1)}, u32[]{:S(2)}, u32[]{:S(2)}) collective-permute-start(bf16[8,2,512,256]{3,2,1,0:T(8,128)(2,1)} %shard_map.279), channel_id=1, source_target_pairs={{0,1},{1,0},{2,3},{3,2},{4,5},{5,4},{6,7},{7,6},{8,9},{9,8},{10,11... | collective-permute-start | bytes 12582920 | tf_op jit(solution)/shard_map/ppermute | solution.py:485
  89.2 29.5 %collective-permute-start.8 = (bf16[8,2,512,256]{3,2,1,0:T(8,128)(2,1)}, bf16[8,2,512,256]{3,2,1,0:T(8,128)(2,1)}, u32[]{:S(2)}, u32[]{:S(2)}) collective-permute-start(bf16[8,2,512,256]{3,2,1,0:T(8,128)(2,1)} %shard_map.280), channel_id=1, source_target_pairs={{0,1},{1,0},{2,3},{3,2},{4,5},{5,4},{6,7},{7,6},{8,9},{9,8},{10,11... | collective-permute-start | bytes 12582920 | tf_op jit(solution)/shard_map/ppermute | solution.py:485
  101.8 11.1 %collective-permute-start.7 = (bf16[8,2,128,256]{3,2,1,0:T(8,128)(2,1)}, bf16[8,2,128,256]{3,2,1,0:T(8,128)(2,1)}, u32[]{:S(2)}, u32[]{:S(2)}) collective-permute-start(bf16[8,2,128,256]{3,2,1,0:T(8,128)(2,1)} %shard_map.282), channel_id=1, source_target_pairs={{0,1},{1,0},{2,3},{3,2},{4,5},{5,4},{6,7},{7,6},{8,9},{9,8},{10,11... | collective-permute-start | bytes 3145736 | tf_op jit(solution)/shard_map/ppermute | solution.py:485
  103.1 14.4 %collective-permute-start.14 = (bf16[1024,256]{1,0:T(8,128)(2,1)}, bf16[1024,256]{1,0:T(8,128)(2,1)}, u32[]{:S(2)}, u32[]{:S(2)}) collective-permute-start(bf16[1024,256]{1,0:T(8,128)(2,1)} %pad_maximum_fusion.10), channel_id=1, source_target_pairs={{0,2},{2,0},{1,3},{3,1},{4,6},{6,4},{5,7},{7,5},{8,10},{10,8},{9,1... | collective-permute-start | bytes 1572872 | tf_op jit(solution)/shard_map/ppermute | solution.py:482
  112.8 52.7 %copy-start.36 = (bf16[8,2,224,256]{3,2,1,0:T(8,128)(2,1)}, bf16[8,2,224,256]{3,2,1,0:T(8,128)(2,1)S(1)}, u32[]{:S(2)}) copy-start(bf16[8,2,224,256]{3,2,1,0:T(8,128)(2,1)S(1)} %get-tuple-element.162) | copy-start | bytes 5505028
  113.0 22.1 %collective-permute-start.13 = (bf16[1792,256]{1,0:T(8,128)(2,1)S(1)}, bf16[1792,256]{1,0:T(8,128)(2,1)S(1)}, u32[]{:S(2)}, u32[]{:S(2)}) collective-permute-start(bf16[1792,256]{1,0:T(8,128)(2,1)S(1)} %bitcast.416), channel_id=1, source_target_pairs={{0,8},{8,0},{16,24},{24,16},{1,9},{9,1},{17,25},{25,17},{2,10},{10... | collective-permute-start | bytes 2752520 | tf_op jit(solution)/shard_map/ppermute | solution.py:600
  113.3 53.2 %copy-start.52 = (bf16[4,1,2,144,256]{4,3,2,1,0:T(8,128)(2,1)}, bf16[4,1,2,144,256]{4,3,2,1,0:T(8,128)(2,1)S(1)}, u32[]{:S(2)}) copy-start(bf16[4,1,2,144,256]{4,3,2,1,0:T(8,128)(2,1)S(1)} %get-tuple-element.263) | copy-start | bytes 1769476
  113.3 19.4 %collective-permute-start.12 = (bf16[1152,256]{1,0:T(8,128)(2,1)S(1)}, bf16[1152,256]{1,0:T(8,128)(2,1)S(1)}, u32[]{:S(2)}, u32[]{:S(2)}) collective-permute-start(bf16[1152,256]{1,0:T(8,128)(2,1)S(1)} %bitcast.431), channel_id=1, source_target_pairs={{0,4},{4,0},{1,5},{5,1},{2,6},{6,2},{3,7},{7,3},{8,12},{12,8},{9,1... | collective-permute-start | bytes 1769480 | tf_op jit(solution)/shard_map/ppermute | solution.py:482
  114.9 17.9 %collective-permute-start.11 = (bf16[1152,256]{1,0:T(8,128)(2,1)S(1)}, bf16[1152,256]{1,0:T(8,128)(2,1)S(1)}, u32[]{:S(2)}, u32[]{:S(2)}) collective-permute-start(bf16[1152,256]{1,0:T(8,128)(2,1)S(1)} %bitcast.429), channel_id=1, source_target_pairs={{0,2},{2,0},{1,3},{3,1},{4,6},{6,4},{5,7},{7,5},{8,10},{10,8},{9,1... | collective-permute-start | bytes 1769480 | tf_op jit(solution)/shard_map/ppermute | solution.py:482
  118.6 12.5 %collective-permute-start.15 = (bf16[1024,256]{1,0:T(8,128)(2,1)S(1)}, bf16[1024,256]{1,0:T(8,128)(2,1)S(1)}, u32[]{:S(2)}, u32[]{:S(2)}) collective-permute-start(bf16[1024,256]{1,0:T(8,128)(2,1)S(1)} %pad_maximum_fusion.11), channel_id=1, source_target_pairs={{0,1},{1,0},{2,3},{3,2},{4,5},{5,4},{6,7},{7,6},{8,9},{9,8},{10,11... | collective-permute-start | bytes 1572872 | tf_op jit(solution)/shard_map/ppermute | solution.py:485
  123.6 44.6 %copy-start.49 = (bf16[4,1,2,320,256]{4,3,2,1,0:T(8,128)(2,1)}, bf16[4,1,2,320,256]{4,3,2,1,0:T(8,128)(2,1)S(1)}, u32[]{:S(2)}) copy-start(bf16[4,1,2,320,256]{4,3,2,1,0:T(8,128)(2,1)S(1)} %get-tuple-element.255) | copy-start | bytes 3932164
  127.2 38.4 %collective-permute-start.9 = (bf16[2560,256]{1,0:T(8,128)(2,1)S(1)}, bf16[2560,256]{1,0:T(8,128)(2,1)S(1)}, u32[]{:S(2)}, u32[]{:S(2)}) collective-permute-start(bf16[2560,256]{1,0:T(8,128)(2,1)S(1)} %bitcast.412), channel_id=1, source_target_pairs={{0,2},{2,0},{1,3},{3,1},{4,6},{6,4},{5,7},{7,5},{8,10},{10,8},{9,1... | collective-permute-start | bytes 3932168 | tf_op jit(solution)/shard_map/ppermute | solution.py:482
  131.1 34.5 %collective-permute-start.10 = (bf16[2560,256]{1,0:T(8,128)(2,1)S(1)}, bf16[2560,256]{1,0:T(8,128)(2,1)S(1)}, u32[]{:S(2)}, u32[]{:S(2)}) collective-permute-start(bf16[2560,256]{1,0:T(8,128)(2,1)S(1)} %bitcast.413), channel_id=1, source_target_pairs={{0,4},{4,0},{1,5},{5,1},{2,6},{6,2},{3,7},{7,3},{8,12},{12,8},{9,1... | collective-permute-start | bytes 3932168 | tf_op jit(solution)/shard_map/ppermute | solution.py:482
  132.6 11.9 %copy-start.27 = (bf16[2048,256]{1,0:T(8,128)(2,1)S(1)}, bf16[2048,256]{1,0:T(8,128)(2,1)}, u32[]{:S(2)}) copy-start(bf16[2048,256]{1,0:T(8,128)(2,1)} %copy-done.26) | copy-start | bytes 3145732
  132.7 11.8 %copy-start.10 = (bf16[2048,768]{1,0:T(8,128)(2,1)S(1)}, bf16[2048,768]{1,0:T(8,128)(2,1)}, u32[]{:S(2)}) copy-start(bf16[2048,768]{1,0:T(8,128)(2,1)} %copy-done.9) | copy-start | bytes 9437188
  132.7 33.8 %copy-start.58 = (bf16[1152,256]{1,0:T(8,128)(2,1)}, bf16[1152,256]{1,0:T(8,128)(2,1)S(1)}, u32[]{:S(2)}) copy-start(bf16[1152,256]{1,0:T(8,128)(2,1)S(1)} %collective-permute-done.12) | copy-start | bytes 1769476
  135.0 30.5 %copy-start.56 = (bf16[1792,256]{1,0:T(8,128)(2,1)}, bf16[1792,256]{1,0:T(8,128)(2,1)S(1)}, u32[]{:S(2)}) copy-start(bf16[1792,256]{1,0:T(8,128)(2,1)S(1)} %collective-permute-done.13) | copy-start | bytes 2752516
  135.3 30.3 %collective-permute-start.17 = (bf16[896,256]{1,0:T(8,128)(2,1)S(1)}, bf16[896,256]{1,0:T(8,128)(2,1)S(1)}, u32[]{:S(2)}, u32[]{:S(2)}) collective-permute-start(bf16[896,256]{1,0:T(8,128)(2,1)S(1)} %bitcast.438), channel_id=1, source_target_pairs={{0,16},{8,24},{16,0},{24,8},{1,17},{9,25},{17,1},{25,9},{2,18},{10... | collective-permute-start | bytes 1376264 | tf_op jit(solution)/shard_map/ppermute | solution.py:600
  142.7 22.8 %collective-permute-start.16 = (bf16[576,256]{1,0:T(8,128)(2,1)S(1)}, bf16[576,256]{1,0:T(8,128)(2,1)S(1)}, u32[]{:S(2)}, u32[]{:S(2)}) collective-permute-start(bf16[576,256]{1,0:T(8,128)(2,1)S(1)} %bitcast.445), channel_id=1, source_target_pairs={{0,8},{8,0},{16,24},{24,16},{1,9},{9,1},{17,25},{25,17},{2,10},{10... | collective-permute-start | bytes 884744 | tf_op jit(solution)/shard_map/ppermute | solution.py:600
  165.6 17.1 %copy-start.54 = (bf16[2560,256]{1,0:T(8,128)(2,1)}, bf16[2560,256]{1,0:T(8,128)(2,1)S(1)}, u32[]{:S(2)}) copy-start(bf16[2560,256]{1,0:T(8,128)(2,1)S(1)} %collective-permute-done.10) | copy-start | bytes 3932164
  165.6 18.3 %copy-start.59 = (bf16[896,256]{1,0:T(8,128)(2,1)}, bf16[896,256]{1,0:T(8,128)(2,1)S(1)}, u32[]{:S(2)}) copy-start(bf16[896,256]{1,0:T(8,128)(2,1)S(1)} %collective-permute-done.17) | copy-start | bytes 1376260
  167.2 30.8 %collective-permute-start.22 = (bf16[288,256]{1,0:T(8,128)(2,1)}, bf16[288,256]{1,0:T(8,128)(2,1)}, u32[]{:S(2)}, u32[]{:S(2)}) collective-permute-start(bf16[288,256]{1,0:T(8,128)(2,1)} %bitcast.70), channel_id=1, source_target_pairs={{0,16},{8,24},{16,0},{24,8},{1,17},{9,25},{17,1},{25,9},{2,18},{10... | collective-permute-start | bytes 442376 | tf_op jit(solution)/shard_map/ppermute | solution.py:600
  169.5 28.6 %collective-permute-start.21 = (bf16[1280,256]{1,0:T(8,128)(2,1)}, bf16[1280,256]{1,0:T(8,128)(2,1)}, u32[]{:S(2)}, u32[]{:S(2)}) collective-permute-start(bf16[1280,256]{1,0:T(8,128)(2,1)} %bitcast.54), channel_id=1, source_target_pairs={{0,8},{8,0},{16,24},{24,16},{1,9},{9,1},{17,25},{25,17},{2,10},{10... | collective-permute-start | bytes 1966088 | tf_op jit(solution)/shard_map/ppermute | solution.py:600
  176.6 21.6 %collective-permute-start.20 = (bf16[4,464,256]{2,1,0:T(8,128)(2,1)}, bf16[4,464,256]{2,1,0:T(8,128)(2,1)}, u32[]{:S(2)}, u32[]{:S(2)}) collective-permute-start(bf16[4,464,256]{2,1,0:T(8,128)(2,1)} %pad_maximum_fusion.8), channel_id=1, source_target_pairs={{0,4},{4,0},{1,5},{5,1},{2,6},{6,2},{3,7},{7,3},{8,12},{12,8},{9,1... | collective-permute-start | bytes 2850824 | tf_op jit(solution)/shard_map/ppermute | solution.py:482
  176.7 9.0 %collective-permute-start.18 = (bf16[1024,768]{1,0:T(8,128)(2,1)S(1)}, bf16[1024,768]{1,0:T(8,128)(2,1)S(1)}, u32[]{:S(2)}, u32[]{:S(2)}) collective-permute-start(bf16[1024,768]{1,0:T(8,128)(2,1)S(1)} %bitcast.405), channel_id=1, source_target_pairs={{0,1},{1,0},{2,3},{3,2},{4,5},{5,4},{6,7},{7,6},{8,9},{9,8},{10,11... | collective-permute-start | bytes 4718600 | tf_op jit(solution)/shard_map/ppermute | solution.py:485
  196.5 45.9 %copy-start.51 = (bf16[4,1,400,256]{3,2,1,0:T(8,128)(2,1)}, bf16[4,1,400,256]{3,2,1,0:T(8,128)(2,1)S(1)}, u32[]{:S(2)}) copy-start(bf16[4,1,400,256]{3,2,1,0:T(8,128)(2,1)S(1)} %get-tuple-element.261) | copy-start | bytes 2457604
  196.6 24.6 %collective-permute-start.19 = (bf16[2048,256]{1,0:T(8,128)(2,1)S(1)}, bf16[2048,256]{1,0:T(8,128)(2,1)S(1)}, u32[]{:S(2)}, u32[]{:S(2)}) collective-permute-start(bf16[2048,256]{1,0:T(8,128)(2,1)S(1)} %pad_maximum_fusion.7), channel_id=1, source_target_pairs={{0,4},{4,0},{1,5},{5,1},{2,6},{6,2},{3,7},{7,3},{8,12},{12,8},{9,1... | collective-permute-start | bytes 3145736 | tf_op jit(solution)/shard_map/ppermute | solution.py:482
  197.4 25.3 %collective-permute-start.25 = (bf16[512,1024]{1,0:T(8,128)(2,1)S(1)}, bf16[512,1024]{1,0:T(8,128)(2,1)S(1)}, u32[]{:S(2)}, u32[]{:S(2)}) collective-permute-start(bf16[512,1024]{1,0:T(8,128)(2,1)S(1)} %get-tuple-element.190), channel_id=1, source_target_pairs={{0,2},{2,0},{1,3},{3,1},{4,6},{6,4},{5,7},{7,5},{8,10},{10,8},{9,1... | collective-permute-start | bytes 3145736 | tf_op jit(solution)/shard_map/ppermute | solution.py:482
  199.7 16.9 %collective-permute-start.24 = (bf16[640,256]{1,0:T(8,128)(2,1)S(1)}, bf16[640,256]{1,0:T(8,128)(2,1)S(1)}, u32[]{:S(2)}, u32[]{:S(2)}) collective-permute-start(bf16[640,256]{1,0:T(8,128)(2,1)S(1)} %bitcast.444), channel_id=1, source_target_pairs={{0,16},{8,24},{16,0},{24,8},{1,17},{9,25},{17,1},{25,9},{2,18},{10... | collective-permute-start | bytes 983048 | tf_op jit(solution)/shard_map/ppermute | solution.py:600
  201.2 19.3 %collective-permute-start.23 = (bf16[928,256]{1,0:T(8,128)(2,1)S(1)}, bf16[928,256]{1,0:T(8,128)(2,1)S(1)}, u32[]{:S(2)}, u32[]{:S(2)}) collective-permute-start(bf16[928,256]{1,0:T(8,128)(2,1)S(1)} %bitcast.432), channel_id=1, source_target_pairs={{0,8},{8,0},{16,24},{24,16},{1,9},{9,1},{17,25},{25,17},{2,10},{10... | collective-permute-start | bytes 1425416 | tf_op jit(solution)/shard_map/ppermute | solution.py:600
  226.0 12.9 %collective-permute-start.28 = (bf16[688,256]{1,0:T(8,128)(2,1)S(1)}, bf16[688,256]{1,0:T(8,128)(2,1)S(1)}, u32[]{:S(2)}, u32[]{:S(2)}) collective-permute-start(bf16[688,256]{1,0:T(8,128)(2,1)S(1)} %pad_maximum_fusion.13), channel_id=1, source_target_pairs={{0,2},{2,0},{1,3},{3,1},{4,6},{6,4},{5,7},{7,5},{8,10},{10,8},{9,1... | collective-permute-start | bytes 1056776 | tf_op jit(solution)/shard_map/ppermute | solution.py:482
  226.6 12.3 %collective-permute-start.27 = (bf16[464,256]{1,0:T(8,128)(2,1)S(1)}, bf16[464,256]{1,0:T(8,128)(2,1)S(1)}, u32[]{:S(2)}, u32[]{:S(2)}) collective-permute-start(bf16[464,256]{1,0:T(8,128)(2,1)S(1)} %fusion.14), channel_id=1, source_target_pairs={{0,16},{8,24},{16,0},{24,8},{1,17},{9,25},{17,1},{25,9},{2,18},{10... | collective-permute-start | bytes 712712 | tf_op jit(solution)/shard_map/ppermute | solution.py:600
  226.7 15.6 %collective-permute-start.26 = (bf16[800,256]{1,0:T(8,128)(2,1)S(1)}, bf16[800,256]{1,0:T(8,128)(2,1)S(1)}, u32[]{:S(2)}, u32[]{:S(2)}) collective-permute-start(bf16[800,256]{1,0:T(8,128)(2,1)S(1)} %bitcast.439), channel_id=1, source_target_pairs={{0,8},{8,0},{16,24},{24,16},{1,9},{9,1},{17,25},{25,17},{2,10},{10... | collective-permute-start | bytes 1228808 | tf_op jit(solution)/shard_map/ppermute | solution.py:600
  231.8 10.8 %copy-start.65 = (bf16[144,256]{1,0:T(8,128)(2,1)S(1)}, bf16[144,256]{1,0:T(8,128)(2,1)}, u32[]{:S(2)}) copy-start(bf16[144,256]{1,0:T(8,128)(2,1)} %get-tuple-element.211) | copy-start | bytes 221188
  231.8 10.8 %copy-start.66 = (bf16[144,256]{1,0:T(8,128)(2,1)S(1)}, bf16[144,256]{1,0:T(8,128)(2,1)}, u32[]{:S(2)}) copy-start(bf16[144,256]{1,0:T(8,128)(2,1)} %get-tuple-element.210) | copy-start | bytes 221188
  231.8 10.9 %copy-start.61 = (bf16[224,256]{1,0:T(8,128)(2,1)S(1)}, bf16[224,256]{1,0:T(8,128)(2,1)}, u32[]{:S(2)}) copy-start(bf16[224,256]{1,0:T(8,128)(2,1)} %dynamic-slice_bitcast_fusion.14) | copy-start | bytes 344068
  231.8 10.9 %copy-start.62 = (bf16[224,256]{1,0:T(8,128)(2,1)S(1)}, bf16[224,256]{1,0:T(8,128)(2,1)}, u32[]{:S(2)}) copy-start(bf16[224,256]{1,0:T(8,128)(2,1)} %dynamic-slice_bitcast_fusion.13) | copy-start | bytes 344068
  231.9 10.9 %copy-start.57 = (bf16[320,256]{1,0:T(8,128)(2,1)S(1)}, bf16[320,256]{1,0:T(8,128)(2,1)}, u32[]{:S(2)}) copy-start(bf16[320,256]{1,0:T(8,128)(2,1)} %dynamic-slice_bitcast_fusion.10) | copy-start | bytes 491524
  243.1 14.7 %copy-start.64 = (bf16[800,256]{1,0:T(8,128)(2,1)S(1)}, bf16[800,256]{1,0:T(8,128)(2,1)}, u32[]{:S(2)}) copy-start(bf16[800,256]{1,0:T(8,128)(2,1)} %copy-done.63) | copy-start | bytes 1228804
  243.1 13.6 %collective-permute-start.30 = (bf16[1152,256]{1,0:T(8,128)(2,1)S(1)}, bf16[1152,256]{1,0:T(8,128)(2,1)S(1)}, u32[]{:S(2)}, u32[]{:S(2)}) collective-permute-start(bf16[1152,256]{1,0:T(8,128)(2,1)S(1)} %slice_dynamic-update-slice_fusion), channel_id=1, source_target_pairs={{0,2},{2,0},{1,3},{3,1},{4,6},{6,4},{5,7},{7,5},{8,10},{10,8},{9,1... | collective-permute-start | bytes 1769480 | tf_op jit(solution)/shard_map/ppermute | solution.py:482
  244.7 10.1 %collective-permute-start.29 = (bf16[400,256]{1,0:T(8,128)(2,1)S(1)}, bf16[400,256]{1,0:T(8,128)(2,1)S(1)}, u32[]{:S(2)}, u32[]{:S(2)}) collective-permute-start(bf16[400,256]{1,0:T(8,128)(2,1)S(1)} %fusion.19), channel_id=1, source_target_pairs={{0,16},{8,24},{16,0},{24,8},{1,17},{9,25},{17,1},{25,9},{2,18},{10... | collective-permute-start | bytes 614408 | tf_op jit(solution)/shard_map/ppermute | solution.py:600
  257.8 3.2 %collective-permute-start.32 = (bf16[2,1152,256]{2,1,0:T(8,128)(2,1)}, bf16[2,1152,256]{2,1,0:T(8,128)(2,1)}, u32[]{:S(2)}, u32[]{:S(2)}) collective-permute-start(bf16[2,1152,256]{2,1,0:T(8,128)(2,1)} %pad_maximum_fusion.3), channel_id=1, source_target_pairs={{0,1},{1,0},{2,3},{3,2},{4,5},{5,4},{6,7},{7,6},{8,9},{9,8},{10,11... | collective-permute-start | bytes 3538952 | tf_op jit(solution)/shard_map/ppermute | solution.py:485
  258.8 8.3 %collective-permute-start.31 = (bf16[400,256]{1,0:T(8,128)(2,1)S(1)}, bf16[400,256]{1,0:T(8,128)(2,1)S(1)}, u32[]{:S(2)}, u32[]{:S(2)}) collective-permute-start(bf16[400,256]{1,0:T(8,128)(2,1)S(1)} %fusion.12), channel_id=1, source_target_pairs={{0,2},{2,0},{1,3},{3,1},{4,6},{6,4},{5,7},{7,5},{8,10},{10,8},{9,1... | collective-permute-start | bytes 614408 | tf_op jit(solution)/shard_map/ppermute | solution.py:482
  267.1 1.8 collective-permute-start.33
  (44 other events, 114.0 us)

commit v4 on v3

--- a/solution.py
+++ b/solution.py
@@ -609,7 +609,7 @@
         return jnp.concatenate([v.reshape(B, -1) for v in vecs], axis=1).astype(BF).reshape(B, -1, W)
 
     hr = w_down.shape[0] // B // 2
-    pr = qr = 9 * hr // 16 // 16 * 16
+    pr = qr = 11 * hr // 16 // 16 * 16
     n_ot = D // B
     ur = hr + n_ot // 2
 

time: 271 us -> 272 us (level)
  waiting for transfers between devices: 50.7 us -> 56.1 us
    ppermute x12, waiting for transfers between devices: 10.5 us -> 18.5 us  [shift(): return lax.ppermute(v, axis, [(i, (i + s) % n) for i in range(n)])]
    ppermute x10, waiting for transfers between devices: 26.9 us -> 23.1 us  [over_z(): lax.ppermute(v, 'z', [(i, i ^ bit) for i in range(Z)])]
    ppermute x12, starting transfers between devices: 15.4 us -> 11.6 us  [shift(): return lax.ppermute(v, axis, [(i, (i + s) % n) for i in range(n)])]
    unnamed x187 -> x185, local copies, waits for them, and re-layouts: 22.2 us -> 21.9 us
  transfers between devices with their start and end apart: 34 -> 34, of which waited for: 16 -> 14; matrix products, arithmetic and copies ran while one was open for 15% -> 14% of each run, Pallas kernels for 26% -> 26%
where the time goes in v4:
time: 272 us; the launch traced here: 270 us
  Pallas kernels  105 us (39%)
  waiting for transfers between devices  56.1 us (21%)
  local copies, waits for them, and re-layouts  38.5 us (14%)
  starting transfers between devices  35.5 us (13%)
  other arithmetic  32.8 us (12%)
    pallas_call x17, Pallas kernels, grid_call(): pl.pallas_call(kernel, out_shape=[o for o, _, _ in outs], grid_spec=pltpu...  75.8 us
    pallas_call x2, Pallas kernels, attend(): pl.pallas_call(kernel, out_shape=outs, grid_spec=pltpu.PrefetchScalarGrid...  29.2 us
    ppermute x10, waiting for transfers between devices, over_z(): lax.ppermute(v, 'z', [(i, i ^ bit) for i in range(Z)])  23.1 us
    unnamed x185, local copies, waits for them, and re-layouts  21.9 us
    ppermute x10, starting transfers between devices, over_z(): lax.ppermute(v, 'z', [(i, i ^ bit) for i in range(Z)])  19.6 us
    ppermute x12, waiting for transfers between devices, shift(): return lax.ppermute(v, axis, [(i, (i + s) % n) for i in range(n)])  18.5 us
    ppermute x12, starting transfers between devices, shift(): return lax.ppermute(v, axis, [(i, (i + s) % n) for i in range(n)])  11.6 us
    convert_element_type x18, other arithmetic, settle(): sum((g.astype(F32) for g in terms[1:]), terms[0].astype(F32)).astype(BF)  11.6 us
  transfers between devices with their start and end apart: 34, of which 14 were waited for; matrix products, arithmetic and copies ran while one was open for 14% of the time, Pallas kernels for 26%

profile of v4, /device:TPU:0, one launch (start us, length us, event | category | flops | bytes accessed | tf_op | source)
XLA Modules:
  0.0 270.2 jit_solution(6844895424610284603)
XLA Ops:
  1.2 2.6 collective-permute-start
  7.6 2.1 constant_dynamic-slice_fusion.19
  9.9 1.4 copy-done.8
  11.2 2.4 shard_map.271
  13.6 1.2 pad_maximum_fusion.2.wm_ref
  14.9 2.4 shard_map.272
  17.4 6.2 %shard_map.273.dg_ref = bf16[512,4096]{1,0:T(8,128)(2,1)S(1)} custom-call(bf16[512,1024]{1,0:T(8,128)(2,1)S(1)} %bitcast.341, bf16[4096,1024]{1,0:T(8,128)(2,1)S(1)} %bitcast.346), custom_call_target="tpu_custom_call" | custom-call | flops 4294967296 | bytes 13631488 | tf_op jit(solution)/shard_map/pallas_call | solution.py:162
  23.6 4.1 %collective-permute-done.x_ref = bf16[512,1024]{1,0:T(8,128)(2,1)S(1)} collective-permute-done((bf16[512,1024]{1,0:T(8,128)(2,1)}, bf16[512,1024]{1,0:T(8,128)(2,1)S(1)}, u32[]{:S(2)}, u32[]{:S(2)}) %collective-permute-start) | collective-permute-done | bytes 1048608 | tf_op jit(solution)/shard_map/ppermute | solution.py:482
  28.3 2.4 shard_map.274
  30.8 2.4 shard_map.275
  33.2 11.1 %shard_map.276 = (bf16[2048,256]{1,0:T(8,128)(2,1)S(1)}, f32[4,2048]{1,0:T(4,128)S(1)}) custom-call(s32[8,8]{1,0:T(8,128)S(1)} %select_reduce_fusion.3.lst, s32[8]{0:T(128)S(1)} %get-tuple-element.247.cnt, s32[8]{0:T(128)S(1)} %bitcast.373, bf16[2048,768]{1,0:T(8,128)(2,1)S(1)} %get-tuple-element.133.q_ref.k_ref.v_ref, ...), custom_call_target="tpu_custom_call" | custom-call | flops 12000000000 | bytes 10534912 | tf_op jit(solution)/shard_map/pallas_call | solution.py:141
  45.9 1.8 collective-permute-start.4
  48.0 7.1 %collective-permute-done.4.refs_2_ = bf16[512,256]{1,0:T(8,128)(2,1)S(1)} collective-permute-done((bf16[512,256]{1,0:T(8,128)(2,1)S(1)}, bf16[512,256]{1,0:T(8,128)(2,1)S(1)}, u32[]{:S(2)}, u32[]{:S(2)}) %collective-permute-start.4) | collective-permute-done | bytes 262176 | tf_op jit(solution)/shard_map/ppermute | solution.py:491
  55.1 4.0 %collective-permute-done.5.refs_3_ = bf16[512,256]{1,0:T(8,128)(2,1)S(1)} collective-permute-done((bf16[512,256]{1,0:T(8,128)(2,1)S(1)}, bf16[512,256]{1,0:T(8,128)(2,1)S(1)}, u32[]{:S(2)}, u32[]{:S(2)}) %collective-permute-start.5) | collective-permute-done | bytes 262176 | tf_op jit(solution)/shard_map/ppermute | solution.py:491
  59.1 2.6 shard_map.277
  61.8 1.3 copy-done.16
  63.1 14.1 %shard_map.278 = (bf16[512,4096]{1,0:T(8,128)(2,1)S(1)}, bf16[512,4096]{1,0:T(8,128)(2,1)S(1)}, f32[512,1024]{1,0:T(8,128)S(1)}, f32[1,4096]{1,0:T(1,128)S(1)}) custom-call(bf16[512,1024]{1,0:T(8,128)(2,1)S(1)} %get-tuple-element.166.h_ref.refs_0_, bf16[1024,4096]{1,0:T(8,128)(2,1)S(1)} %bitcast.376, f32[1,4096]{1,0:T(1,128)S(1)} %bitcast.377, ...), custom_call_target="tpu_custom_call" | custom-call | flops 8589934592 | bytes 24150016 | tf_op jit(solution)/shard_map/pallas_call | solution.py:162
  77.2 1.3 copy-done.32
  78.6 5.1 %shard_map.279 = bf16[8,2,512,256]{3,2,1,0:T(8,128)(2,1)} custom-call(s32[1]{0:T(128)} %bitcast.30.half_ref, bf16[512,4096]{1,0:T(8,128)(2,1)S(1)} %get-tuple-element.191.refs_0_.a_ref, bf16[512,1024]{1,0:T(8,128)(2,1)S(1)} %bitcast.342), custom_call_target="tpu_custom_call" | custom-call | flops 2147483648 | bytes 9437184 | tf_op jit(solution)/shard_map/pallas_call | solution.py:162
  84.2 4.1 %shard_map.280 = bf16[8,2,512,256]{3,2,1,0:T(8,128)(2,1)} custom-call(s32[1]{0:T(128)} %bitcast.30.half_ref, bf16[512,1024]{1,0:T(8,128)(2,1)S(1)} %get-tuple-element.166.h_ref.refs_0_, bf16[512,4096]{1,0:T(8,128)(2,1)S(1)} %get-tuple-element.150.refs_1_), custom_call_target="tpu_custom_call" | custom-call | flops 2147483648 | bytes 9437184 | tf_op jit(solution)/shard_map/pallas_call | solution.py:162
  88.7 1.2 copy-done.14
  89.9 1.6 copy-done.17
  91.5 1.6 copy-done.33
  93.1 2.9 %shard_map.281 = (f32[512,1024]{1,0:T(8,128)S(1)}, bf16[512,1024]{1,0:T(8,128)(2,1)S(1)}, bf16[512,1024]{1,0:T(8,128)(2,1)S(1)}, f32[4,1024]{1,0:T(4,128)S(1)}) custom-call(f32[512,1024]{1,0:T(8,128)S(1)} %copy-done.33, f32[512,1024]{1,0:T(8,128)S(1)} %copy-done.17, bf16[512,1024]{1,0:T(8,128)(2,1)S(1)} %bitcast.343, f32[1,1024]{1,0:T(1,128)S(1)} %bitcast.368, ...), custom_call_target="tpu_custom_call" | custom-call | flops 1073741824 | bytes 11554816 | tf_op jit(solution)/shard_map/pallas_call | solution.py:162
  98.2 2.0 shard_map.282
  101.4 1.7 collective-permute-start.14
  103.4 2.2 copy-done.6
  105.6 5.0 %shard_map.283 = (bf16[8,2,176,256]{3,2,1,0:T(8,128)(2,1)S(1)}, bf16[8,2,176,256]{3,2,1,0:T(8,128)(2,1)S(1)}, bf16[8,2,160,256]{3,2,1,0:T(8,128)(2,1)S(1)}) custom-call(s32[1]{0:T(128)} %bitcast.4.half_ref, bf16[512,4096]{1,0:T(8,128)(2,1)S(1)} %copy-done.6, bf16[512,1024]{1,0:T(8,128)(2,1)S(1)} %bitcast.344, ...), custom_call_target="tpu_custom_call" | custom-call | flops 2147483648 | bytes 13631488 | tf_op jit(solution)/shard_map/pallas_call | solution.py:162
  110.7 7.9 %collective-permute-start.13 = (bf16[1280,256]{1,0:T(8,128)(2,1)S(1)}, bf16[1280,256]{1,0:T(8,128)(2,1)S(1)}, u32[]{:S(2)}, u32[]{:S(2)}) collective-permute-start(bf16[1280,256]{1,0:T(8,128)(2,1)S(1)} %bitcast.425), channel_id=1, source_target_pairs={{0,8},{8,0},{16,24},{24,16},{1,9},{9,1},{17,25},{25,17},{2,10},{10... | collective-permute-start | bytes 1966088 | tf_op jit(solution)/shard_map/ppermute | solution.py:600
  119.8 1.8 fusion.47
  121.8 4.7 %shard_map.284 = (bf16[8,2,320,256]{3,2,1,0:T(8,128)(2,1)S(1)}, bf16[8,2,192,256]{3,2,1,0:T(8,128)(2,1)S(1)}) custom-call(s32[1]{0:T(128)} %bitcast.4.half_ref, bf16[512,1024]{1,0:T(8,128)(2,1)S(1)} %copy-done.25, bf16[512,4096]{1,0:T(8,128)(2,1)S(1)} %copy-done.12, bf16[8,2,512,256]{3,2,1,0:T(8,128)(2,1)} %collective-permute-done.8.refs_2_), custom_call_target="tpu_custom_call" | custom-call | flops 2147483648 | bytes 13631488 | tf_op jit(solution)/shard_map/pallas_call | solution.py:162
  126.4 2.4 shard_map.285
  131.2 2.0 collective-permute-start.10
  133.4 4.5 %collective-permute-done.12 = bf16[1408,256]{1,0:T(8,128)(2,1)S(1)} collective-permute-done((bf16[1408,256]{1,0:T(8,128)(2,1)S(1)}, bf16[1408,256]{1,0:T(8,128)(2,1)S(1)}, u32[]{:S(2)}, u32[]{:S(2)}) %collective-permute-start.12) | collective-permute-done | bytes 720928 | tf_op jit(solution)/shard_map/ppermute | solution.py:482
  138.5 2.0 collective-permute-start.16
  140.4 18.0 %shard_map.286.b_ref.dq_ref = bf16[2048,768]{1,0:T(8,128)(2,1)S(1)} custom-call(s32[8,8]{1,0:T(8,128)S(1)} %select_reduce_fusion.2.lst, s32[8]{0:T(128)S(1)} %get-tuple-element.305.cnt, s32[8]{0:T(128)S(1)} %bitcast.374, bf16[2048,768]{1,0:T(8,128)(2,1)S(1)} %copy-done.10, bf16[2048,768]{1,0:T(8,128)(2,1)S(1)} %copy-done.10, ...), custom_call_target="tpu_custom_call" | custom-call | flops 20000000000 | bytes 14729216 | tf_op jit(solution)/shard_map/pallas_call | solution.py:141
  159.9 4.6 %collective-permute-done.9 = bf16[2560,256]{1,0:T(8,128)(2,1)S(1)} collective-permute-done((bf16[2560,256]{1,0:T(8,128)(2,1)S(1)}, bf16[2560,256]{1,0:T(8,128)(2,1)S(1)}, u32[]{:S(2)}, u32[]{:S(2)}) %collective-permute-start.9) | collective-permute-done | bytes 1310752 | tf_op jit(solution)/shard_map/ppermute | solution.py:482
  164.5 1.1 add_convert_fusion
  168.0 5.4 %collective-permute-start.21 = (bf16[1280,256]{1,0:T(8,128)(2,1)}, bf16[1280,256]{1,0:T(8,128)(2,1)}, u32[]{:S(2)}, u32[]{:S(2)}) collective-permute-start(bf16[1280,256]{1,0:T(8,128)(2,1)} %bitcast.54), channel_id=1, source_target_pairs={{0,8},{8,0},{16,24},{24,16},{1,9},{9,1},{17,25},{25,17},{2,10},{10... | collective-permute-start | bytes 1966088 | tf_op jit(solution)/shard_map/ppermute | solution.py:600
  174.7 1.3 copy-done.1
  176.0 4.6 %shard_map.287 = bf16[8,384,256]{2,1,0:T(8,128)(2,1)S(1)} custom-call(bf16[2048,1024]{1,0:T(8,128)(2,1)S(1)} %copy-done.1, bf16[2048,768]{1,0:T(8,128)(2,1)S(1)} %shard_map.286.b_ref.dq_ref), custom_call_target="tpu_custom_call" | custom-call | flops 402653184 | bytes 1114112 | tf_op jit(solution)/shard_map/pallas_call | solution.py:162
  183.5 1.2 copy-done.21
  185.3 6.0 %shard_map.288 = (bf16[512,1024]{1,0:T(8,128)(2,1)S(1)}, bf16[512,1024]{1,0:T(8,128)(2,1)S(1)}, f32[2,1024]{1,0:T(2,128)S(1)}) custom-call(bf16[2048,768]{1,0:T(8,128)(2,1)S(1)} %shard_map.286.b_ref.dq_ref, bf16[1024,768]{1,0:T(8,128)(2,1)S(1)} %collective-permute-done.18.got_ref, bf16[1024,768]{1,0:T(8,128)(2,1)S(1)} %copy-done.4, ...), custom_call_target="tpu_custom_call" | custom-call | flops 402653184 | bytes 1770496 | tf_op jit(solution)/shard_map/pallas_call | solution.py:162
  191.3 1.5 pad_maximum_fusion
  192.9 1.6 collective-permute-start.25
  196.1 1.5 collective-permute-done.20
  197.6 1.3 add_convert_fusion.4
  198.9 2.7 collective-permute-start.24
  201.5 1.2 add_convert_fusion.1
  203.2 3.4 %copy-done.19 = bf16[4096,1024]{1,0:T(8,128)(2,1)S(1)} copy-done((bf16[4096,1024]{1,0:T(8,128)(2,1)S(1)}, bf16[4096,1024]{1,0:T(8,128)(2,1)}, u32[]{:S(2)}) %copy-start.19) | copy-done | bytes 8388632
  206.5 6.6 %shard_map.289 = bf16[512,1024]{1,0:T(8,128)(2,1)} custom-call(bf16[512,4096]{1,0:T(8,128)(2,1)S(1)} %copy-done.7, bf16[4096,1024]{1,0:T(8,128)(2,1)S(1)} %copy-done.19, f32[512,1024]{1,0:T(8,128)S(1)} %copy-done.18, f32[1,1024]{1,0:T(1,128)S(1)} %bitcast.371), custom_call_target="tpu_custom_call" | custom-call | flops 536870912 | bytes 1966592 | tf_op jit(solution)/shard_map/pallas_call | solution.py:162
  217.0 4.3 %collective-permute-done.23 = bf16[992,256]{1,0:T(8,128)(2,1)S(1)} collective-permute-done((bf16[992,256]{1,0:T(8,128)(2,1)S(1)}, bf16[992,256]{1,0:T(8,128)(2,1)S(1)}, u32[]{:S(2)}, u32[]{:S(2)}) %collective-permute-start.23) | collective-permute-done | bytes 507936 | tf_op jit(solution)/shard_map/ppermute | solution.py:600
  221.4 1.2 fusion.12
  228.6 2.2 add_bitcast_fusion
  230.9 5.7 %collective-permute-done.27 = bf16[496,256]{1,0:T(8,128)(2,1)S(1)} collective-permute-done((bf16[496,256]{1,0:T(8,128)(2,1)S(1)}, bf16[496,256]{1,0:T(8,128)(2,1)S(1)}, u32[]{:S(2)}, u32[]{:S(2)}) %collective-permute-start.27) | collective-permute-done | bytes 253984 | tf_op jit(solution)/shard_map/ppermute | solution.py:600
  236.6 4.4 %collective-permute-done.26 = bf16[800,256]{1,0:T(8,128)(2,1)S(1)} collective-permute-done((bf16[800,256]{1,0:T(8,128)(2,1)S(1)}, bf16[800,256]{1,0:T(8,128)(2,1)S(1)}, u32[]{:S(2)}, u32[]{:S(2)}) %collective-permute-start.26) | collective-permute-done | bytes 409632 | tf_op jit(solution)/shard_map/ppermute | solution.py:600
  242.8 8.7 %collective-permute-done.29 = bf16[400,256]{1,0:T(8,128)(2,1)S(1)} collective-permute-done((bf16[400,256]{1,0:T(8,128)(2,1)S(1)}, bf16[400,256]{1,0:T(8,128)(2,1)S(1)}, u32[]{:S(2)}, u32[]{:S(2)}) %collective-permute-start.29) | collective-permute-done | bytes 204832 | tf_op jit(solution)/shard_map/ppermute | solution.py:600
  251.5 3.6 %collective-permute-done.30 = bf16[1152,256]{1,0:T(8,128)(2,1)S(1)} collective-permute-done((bf16[1152,256]{1,0:T(8,128)(2,1)S(1)}, bf16[1152,256]{1,0:T(8,128)(2,1)S(1)}, u32[]{:S(2)}, u32[]{:S(2)}) %collective-permute-start.30) | collective-permute-done | bytes 589856 | tf_op jit(solution)/shard_map/ppermute | solution.py:482
  257.7 1.8 collective-permute-done.32
  259.4 1.7 broadcast_select_fusion.3
  262.4 1.5 convert_element_type.644
  264.0 1.6 maximum_convert_fusion
  265.8 1.6 collective-permute-done.33
  267.8 1.3 convert_element_type.651
  (366 shorter events, 43.1 us)
Async XLA Ops:
  0.6 14.2 %collective-permute-start.1 = (bf16[512,1024]{1,0:T(8,128)(2,1)}, bf16[512,1024]{1,0:T(8,128)(2,1)S(1)}, u32[]{:S(2)}, u32[]{:S(2)}) collective-permute-start(bf16[512,1024]{1,0:T(8,128)(2,1)} %bitcast.333), channel_id=1, source_target_pairs={{0,1},{1,0},{2,3},{3,2},{4,5},{5,4},{6,7},{7,6},{8,9},{9,8},{10,11... | collective-permute-start | bytes 3145736 | tf_op jit(solution)/shard_map/ppermute | solution.py:485
  1.2 26.6 %collective-permute-start = (bf16[512,1024]{1,0:T(8,128)(2,1)}, bf16[512,1024]{1,0:T(8,128)(2,1)S(1)}, u32[]{:S(2)}, u32[]{:S(2)}) collective-permute-start(bf16[512,1024]{1,0:T(8,128)(2,1)} %bitcast.334), channel_id=1, source_target_pairs={{0,2},{2,0},{1,3},{3,1},{4,6},{6,4},{5,7},{7,5},{8,10},{10,8},{9,1... | collective-permute-start | bytes 3145736 | tf_op jit(solution)/shard_map/ppermute | solution.py:482
  9.7 7.5 %slice-start = ((s8[8388608]{0:T(1024)(128)(4,1)}), s8[4194304]{0:T(1024)(128)(4,1)S(1)}, s32[]{:S(2)}) async-start(s8[8388608]{0:T(1024)(128)(4,1)} %bitcast.345), calls=%async_computation | async-start | bytes 8388608
  9.9 20.9 %copy-start.3 = (bf16[1024,768]{1,0:T(8,128)(2,1)}, bf16[1024,768]{1,0:T(8,128)(2,1)S(1)}, u32[]{:S(2)}) copy-start(bf16[1024,768]{1,0:T(8,128)(2,1)S(1)} %pad_maximum_fusion.1.w_ref) | copy-start | bytes 4718596
  27.7 3.0 %collective-permute-start.2 = (bf16[512,1024]{1,0:T(8,128)(2,1)S(1)}, bf16[512,1024]{1,0:T(8,128)(2,1)S(1)}, u32[]{:S(2)}, u32[]{:S(2)}) collective-permute-start(bf16[512,1024]{1,0:T(8,128)(2,1)S(1)} %collective-permute-done.x_ref), channel_id=1, source_target_pairs={{0,1},{1,0},{2,3},{3,2},{4,5},{5,4},{6,7},{7,6},{8,9},{9,8},{10,11... | collective-permute-start | bytes 3145736 | tf_op jit(solution)/shard_map/ppermute | solution.py:485
  30.7 32.3 %slice-start.2 = ((s8[8388608]{0:T(1024)(128)(4,1)}), s8[4194304]{0:T(1024)(128)(4,1)S(1)}, s32[]{:S(2)}) async-start(s8[8388608]{0:T(1024)(128)(4,1)} %bitcast.375), calls=%async_computation.2 | async-start | bytes 8388608
  33.2 11.2 %copy-start = (bf16[2048,1024]{1,0:T(8,128)(2,1)}, bf16[2048,1024]{1,0:T(8,128)(2,1)S(1)}, u32[]{:S(2)}) copy-start(bf16[2048,1024]{1,0:T(8,128)(2,1)S(1)} %get-tuple-element.132.a_ref) | copy-start | bytes 12582916
  33.2 11.2 %copy-start.9 = (bf16[2048,768]{1,0:T(8,128)(2,1)}, bf16[2048,768]{1,0:T(8,128)(2,1)S(1)}, u32[]{:S(2)}) copy-start(bf16[2048,768]{1,0:T(8,128)(2,1)S(1)} %get-tuple-element.133.q_ref.k_ref.v_ref) | copy-start | bytes 9437188
  33.2 29.9 %slice-start.3 = ((s8[8388608]{0:T(1024)(128)(4,1)}), s8[4194304]{0:T(1024)(128)(4,1)S(1)}, s32[]{:S(2)}) async-start(s8[8388608]{0:T(1024)(128)(4,1)} %bitcast.375), calls=%async_computation.3 | async-start | bytes 8388608
  44.4 14.7 %copy-start.26 = (bf16[2048,256]{1,0:T(8,128)(2,1)}, bf16[2048,256]{1,0:T(8,128)(2,1)S(1)}, u32[]{:S(2)}) copy-start(bf16[2048,256]{1,0:T(8,128)(2,1)S(1)} %get-tuple-element.134.refs_0_.ctx_ref) | copy-start | bytes 3145732
  45.3 2.6 collective-permute-start.3
  45.9 9.2 %collective-permute-start.4 = (bf16[512,256]{1,0:T(8,128)(2,1)S(1)}, bf16[512,256]{1,0:T(8,128)(2,1)S(1)}, u32[]{:S(2)}, u32[]{:S(2)}) collective-permute-start(bf16[512,256]{1,0:T(8,128)(2,1)S(1)} %get-tuple-element.275), channel_id=1, source_target_pairs={{0,2},{1,3},{2,0},{3,1},{4,6},{5,7},{6,4},{7,5},{8,10},{9,11},{10,... | collective-permute-start | bytes 786440 | tf_op jit(solution)/shard_map/ppermute | solution.py:491
  47.7 11.4 %collective-permute-start.5 = (bf16[512,256]{1,0:T(8,128)(2,1)S(1)}, bf16[512,256]{1,0:T(8,128)(2,1)S(1)}, u32[]{:S(2)}, u32[]{:S(2)}) collective-permute-start(bf16[512,256]{1,0:T(8,128)(2,1)S(1)} %get-tuple-element.274), channel_id=1, source_target_pairs={{0,3},{1,2},{2,1},{3,0},{4,7},{5,6},{6,5},{7,4},{8,11},{9,10},{10,... | collective-permute-start | bytes 786440 | tf_op jit(solution)/shard_map/ppermute | solution.py:491
  47.7 11.3 %copy-start.2 = (bf16[1024,1024]{1,0:T(8,128)(2,1)S(1)}, bf16[1024,1024]{1,0:T(8,128)(2,1)}, u32[]{:S(2)}) copy-start(bf16[1024,1024]{1,0:T(8,128)(2,1)} %w_ref.6) | copy-start | bytes 6291460
  47.8 11.3 %copy-start.43 = (f32[1024]{0:T(1024)S(1)}, f32[1024]{0:T(1024)}, u32[]{:S(2)}) copy-start(f32[1024]{0:T(1024)} %param.24) | copy-start | bytes 12292
  47.8 11.3 %copy-start.44 = (f32[1024]{0:T(1024)S(1)}, f32[1024]{0:T(1024)}, u32[]{:S(2)}) copy-start(f32[1024]{0:T(1024)} %param.23) | copy-start | bytes 12292
  47.8 11.3 %copy-start.45 = (f32[1024]{0:T(1024)S(1)}, f32[1024]{0:T(1024)}, u32[]{:S(2)}) copy-start(f32[1024]{0:T(1024)} %param.25) | copy-start | bytes 12292
  47.9 13.8 %copy-start.20 = (bf16[2048,1024]{1,0:T(8,128)(2,1)}, bf16[2048,1024]{1,0:T(8,128)(2,1)S(1)}, u32[]{:S(2)}) copy-start(bf16[2048,1024]{1,0:T(8,128)(2,1)S(1)} %constant_dynamic-update-slice_fusion.x_ref) | copy-start | bytes 12582916
  63.1 21.1 %copy-start.24 = (bf16[512,1024]{1,0:T(8,128)(2,1)}, bf16[512,1024]{1,0:T(8,128)(2,1)S(1)}, u32[]{:S(2)}) copy-start(bf16[512,1024]{1,0:T(8,128)(2,1)S(1)} %get-tuple-element.166.h_ref.refs_0_) | copy-start | bytes 3145732
  83.6 19.8 %collective-permute-start.6 = (bf16[8,2,512,256]{3,2,1,0:T(8,128)(2,1)}, bf16[8,2,512,256]{3,2,1,0:T(8,128)(2,1)}, u32[]{:S(2)}, u32[]{:S(2)}) collective-permute-start(bf16[8,2,512,256]{3,2,1,0:T(8,128)(2,1)} %shard_map.279), channel_id=1, source_target_pairs={{0,1},{1,0},{2,3},{3,2},{4,5},{5,4},{6,7},{7,6},{8,9},{9,8},{10,11... | collective-permute-start | bytes 12582920 | tf_op jit(solution)/shard_map/ppermute | solution.py:485
  88.3 33.4 %collective-permute-start.8 = (bf16[8,2,512,256]{3,2,1,0:T(8,128)(2,1)}, bf16[8,2,512,256]{3,2,1,0:T(8,128)(2,1)}, u32[]{:S(2)}, u32[]{:S(2)}) collective-permute-start(bf16[8,2,512,256]{3,2,1,0:T(8,128)(2,1)} %shard_map.280), channel_id=1, source_target_pairs={{0,1},{1,0},{2,3},{3,2},{4,5},{5,4},{6,7},{7,6},{8,9},{9,8},{10,11... | collective-permute-start | bytes 12582920 | tf_op jit(solution)/shard_map/ppermute | solution.py:485
  100.1 10.5 %collective-permute-start.7 = (bf16[8,2,128,256]{3,2,1,0:T(8,128)(2,1)}, bf16[8,2,128,256]{3,2,1,0:T(8,128)(2,1)}, u32[]{:S(2)}, u32[]{:S(2)}) collective-permute-start(bf16[8,2,128,256]{3,2,1,0:T(8,128)(2,1)} %shard_map.282), channel_id=1, source_target_pairs={{0,1},{1,0},{2,3},{3,2},{4,5},{5,4},{6,7},{7,6},{8,9},{9,8},{10,11... | collective-permute-start | bytes 3145736 | tf_op jit(solution)/shard_map/ppermute | solution.py:485
  101.4 18.0 %collective-permute-start.14 = (bf16[1024,256]{1,0:T(8,128)(2,1)}, bf16[1024,256]{1,0:T(8,128)(2,1)}, u32[]{:S(2)}, u32[]{:S(2)}) collective-permute-start(bf16[1024,256]{1,0:T(8,128)(2,1)} %pad_maximum_fusion.10), channel_id=1, source_target_pairs={{0,2},{2,0},{1,3},{3,1},{4,6},{6,4},{5,7},{7,5},{8,10},{10,8},{9,1... | collective-permute-start | bytes 1572872 | tf_op jit(solution)/shard_map/ppermute | solution.py:482
  110.6 49.2 %copy-start.36 = (bf16[8,2,160,256]{3,2,1,0:T(8,128)(2,1)}, bf16[8,2,160,256]{3,2,1,0:T(8,128)(2,1)S(1)}, u32[]{:S(2)}) copy-start(bf16[8,2,160,256]{3,2,1,0:T(8,128)(2,1)S(1)} %get-tuple-element.162) | copy-start | bytes 3932164
  110.7 22.6 %collective-permute-start.13 = (bf16[1280,256]{1,0:T(8,128)(2,1)S(1)}, bf16[1280,256]{1,0:T(8,128)(2,1)S(1)}, u32[]{:S(2)}, u32[]{:S(2)}) collective-permute-start(bf16[1280,256]{1,0:T(8,128)(2,1)S(1)} %bitcast.425), channel_id=1, source_target_pairs={{0,8},{8,0},{16,24},{24,16},{1,9},{9,1},{17,25},{25,17},{2,10},{10... | collective-permute-start | bytes 1966088 | tf_op jit(solution)/shard_map/ppermute | solution.py:600
  118.7 48.4 %copy-start.52 = (bf16[4,1,2,176,256]{4,3,2,1,0:T(8,128)(2,1)}, bf16[4,1,2,176,256]{4,3,2,1,0:T(8,128)(2,1)S(1)}, u32[]{:S(2)}) copy-start(bf16[4,1,2,176,256]{4,3,2,1,0:T(8,128)(2,1)S(1)} %get-tuple-element.263) | copy-start | bytes 2162692
  118.7 19.1 %collective-permute-start.12 = (bf16[1408,256]{1,0:T(8,128)(2,1)S(1)}, bf16[1408,256]{1,0:T(8,128)(2,1)S(1)}, u32[]{:S(2)}, u32[]{:S(2)}) collective-permute-start(bf16[1408,256]{1,0:T(8,128)(2,1)S(1)} %bitcast.423), channel_id=1, source_target_pairs={{0,4},{4,0},{1,5},{5,1},{2,6},{6,2},{3,7},{7,3},{8,12},{12,8},{9,1... | collective-permute-start | bytes 2162696 | tf_op jit(solution)/shard_map/ppermute | solution.py:482
  118.9 19.1 %collective-permute-start.11 = (bf16[1408,256]{1,0:T(8,128)(2,1)S(1)}, bf16[1408,256]{1,0:T(8,128)(2,1)S(1)}, u32[]{:S(2)}, u32[]{:S(2)}) collective-permute-start(bf16[1408,256]{1,0:T(8,128)(2,1)S(1)} %bitcast.424), channel_id=1, source_target_pairs={{0,2},{2,0},{1,3},{3,1},{4,6},{6,4},{5,7},{7,5},{8,10},{10,8},{9,1... | collective-permute-start | bytes 2162696 | tf_op jit(solution)/shard_map/ppermute | solution.py:482
  121.7 9.6 %collective-permute-start.15 = (bf16[1024,256]{1,0:T(8,128)(2,1)S(1)}, bf16[1024,256]{1,0:T(8,128)(2,1)S(1)}, u32[]{:S(2)}, u32[]{:S(2)}) collective-permute-start(bf16[1024,256]{1,0:T(8,128)(2,1)S(1)} %pad_maximum_fusion.11), channel_id=1, source_target_pairs={{0,1},{1,0},{2,3},{3,2},{4,5},{5,4},{6,7},{7,6},{8,9},{9,8},{10,11... | collective-permute-start | bytes 1572872 | tf_op jit(solution)/shard_map/ppermute | solution.py:485
  129.0 35.5 %collective-permute-start.9 = (bf16[2560,256]{1,0:T(8,128)(2,1)S(1)}, bf16[2560,256]{1,0:T(8,128)(2,1)S(1)}, u32[]{:S(2)}, u32[]{:S(2)}) collective-permute-start(bf16[2560,256]{1,0:T(8,128)(2,1)S(1)} %bitcast.412), channel_id=1, source_target_pairs={{0,2},{2,0},{1,3},{3,1},{4,6},{6,4},{5,7},{7,5},{8,10},{10,8},{9,1... | collective-permute-start | bytes 3932168 | tf_op jit(solution)/shard_map/ppermute | solution.py:482
  129.8 34.7 %copy-start.50 = (bf16[4,1,2,320,256]{4,3,2,1,0:T(8,128)(2,1)}, bf16[4,1,2,320,256]{4,3,2,1,0:T(8,128)(2,1)S(1)}, u32[]{:S(2)}) copy-start(bf16[4,1,2,320,256]{4,3,2,1,0:T(8,128)(2,1)S(1)} %get-tuple-element.255) | copy-start | bytes 3932164
  131.2 33.3 %collective-permute-start.10 = (bf16[2560,256]{1,0:T(8,128)(2,1)S(1)}, bf16[2560,256]{1,0:T(8,128)(2,1)S(1)}, u32[]{:S(2)}, u32[]{:S(2)}) collective-permute-start(bf16[2560,256]{1,0:T(8,128)(2,1)S(1)} %bitcast.413), channel_id=1, source_target_pairs={{0,4},{4,0},{1,5},{5,1},{2,6},{6,2},{3,7},{7,3},{8,12},{12,8},{9,1... | collective-permute-start | bytes 3932168 | tf_op jit(solution)/shard_map/ppermute | solution.py:482
  133.4 26.5 %copy-start.57 = (bf16[1280,256]{1,0:T(8,128)(2,1)}, bf16[1280,256]{1,0:T(8,128)(2,1)S(1)}, u32[]{:S(2)}) copy-start(bf16[1280,256]{1,0:T(8,128)(2,1)S(1)} %collective-permute-done.13) | copy-start | bytes 1966084
  137.8 29.3 %copy-start.56 = (bf16[1408,256]{1,0:T(8,128)(2,1)}, bf16[1408,256]{1,0:T(8,128)(2,1)S(1)}, u32[]{:S(2)}) copy-start(bf16[1408,256]{1,0:T(8,128)(2,1)S(1)} %collective-permute-done.12) | copy-start | bytes 2162692
  138.3 21.6 %collective-permute-start.17 = (bf16[640,256]{1,0:T(8,128)(2,1)S(1)}, bf16[640,256]{1,0:T(8,128)(2,1)S(1)}, u32[]{:S(2)}, u32[]{:S(2)}) collective-permute-start(bf16[640,256]{1,0:T(8,128)(2,1)S(1)} %bitcast.445), channel_id=1, source_target_pairs={{0,16},{8,24},{16,0},{24,8},{1,17},{9,25},{17,1},{25,9},{2,18},{10... | collective-permute-start | bytes 983048 | tf_op jit(solution)/shard_map/ppermute | solution.py:600
  138.5 21.4 %collective-permute-start.16 = (bf16[704,256]{1,0:T(8,128)(2,1)S(1)}, bf16[704,256]{1,0:T(8,128)(2,1)S(1)}, u32[]{:S(2)}, u32[]{:S(2)}) collective-permute-start(bf16[704,256]{1,0:T(8,128)(2,1)S(1)} %bitcast.441), channel_id=1, source_target_pairs={{0,8},{8,0},{16,24},{24,16},{1,9},{9,1},{17,25},{25,17},{2,10},{10... | collective-permute-start | bytes 1081352 | tf_op jit(solution)/shard_map/ppermute | solution.py:600
  159.9 21.9 %copy-start.65 = (bf16[640,256]{1,0:T(8,128)(2,1)}, bf16[640,256]{1,0:T(8,128)(2,1)S(1)}, u32[]{:S(2)}) copy-start(bf16[640,256]{1,0:T(8,128)(2,1)S(1)} %collective-permute-done.17) | copy-start | bytes 983044
  159.9 20.7 %copy-start.62 = (bf16[704,256]{1,0:T(8,128)(2,1)}, bf16[704,256]{1,0:T(8,128)(2,1)S(1)}, u32[]{:S(2)}) copy-start(bf16[704,256]{1,0:T(8,128)(2,1)S(1)} %collective-permute-done.16) | copy-start | bytes 1081348
  167.9 28.2 %collective-permute-start.22 = (bf16[352,256]{1,0:T(8,128)(2,1)}, bf16[352,256]{1,0:T(8,128)(2,1)}, u32[]{:S(2)}, u32[]{:S(2)}) collective-permute-start(bf16[352,256]{1,0:T(8,128)(2,1)} %bitcast.70), channel_id=1, source_target_pairs={{0,16},{8,24},{16,0},{24,8},{1,17},{9,25},{17,1},{25,9},{2,18},{10... | collective-permute-start | bytes 540680 | tf_op jit(solution)/shard_map/ppermute | solution.py:600
  168.0 28.1 %collective-permute-start.21 = (bf16[1280,256]{1,0:T(8,128)(2,1)}, bf16[1280,256]{1,0:T(8,128)(2,1)}, u32[]{:S(2)}, u32[]{:S(2)}) collective-permute-start(bf16[1280,256]{1,0:T(8,128)(2,1)} %bitcast.54), channel_id=1, source_target_pairs={{0,8},{8,0},{16,24},{24,16},{1,9},{9,1},{17,25},{25,17},{2,10},{10... | collective-permute-start | bytes 1966088 | tf_op jit(solution)/shard_map/ppermute | solution.py:600
  174.5 23.1 %collective-permute-start.20 = (bf16[4,496,256]{2,1,0:T(8,128)(2,1)}, bf16[4,496,256]{2,1,0:T(8,128)(2,1)}, u32[]{:S(2)}, u32[]{:S(2)}) collective-permute-start(bf16[4,496,256]{2,1,0:T(8,128)(2,1)} %pad_maximum_fusion.7), channel_id=1, source_target_pairs={{0,4},{4,0},{1,5},{5,1},{2,6},{6,2},{3,7},{7,3},{8,12},{12,8},{9,1... | collective-permute-start | bytes 3047432 | tf_op jit(solution)/shard_map/ppermute | solution.py:482
  174.6 8.9 %collective-permute-start.18 = (bf16[1024,768]{1,0:T(8,128)(2,1)S(1)}, bf16[1024,768]{1,0:T(8,128)(2,1)S(1)}, u32[]{:S(2)}, u32[]{:S(2)}) collective-permute-start(bf16[1024,768]{1,0:T(8,128)(2,1)S(1)} %bitcast.405), channel_id=1, source_target_pairs={{0,1},{1,0},{2,3},{3,2},{4,5},{5,4},{6,7},{7,6},{8,9},{9,8},{10,11... | collective-permute-start | bytes 4718600 | tf_op jit(solution)/shard_map/ppermute | solution.py:485
  192.9 28.4 %collective-permute-start.25 = (bf16[512,1024]{1,0:T(8,128)(2,1)S(1)}, bf16[512,1024]{1,0:T(8,128)(2,1)S(1)}, u32[]{:S(2)}, u32[]{:S(2)}) collective-permute-start(bf16[512,1024]{1,0:T(8,128)(2,1)S(1)} %get-tuple-element.190), channel_id=1, source_target_pairs={{0,2},{2,0},{1,3},{3,1},{4,6},{6,4},{5,7},{7,5},{8,10},{10,8},{9,1... | collective-permute-start | bytes 3145736 | tf_op jit(solution)/shard_map/ppermute | solution.py:482
  194.6 46.5 %copy-start.51 = (bf16[4,1,400,256]{3,2,1,0:T(8,128)(2,1)}, bf16[4,1,400,256]{3,2,1,0:T(8,128)(2,1)S(1)}, u32[]{:S(2)}) copy-start(bf16[4,1,400,256]{3,2,1,0:T(8,128)(2,1)S(1)} %get-tuple-element.261) | copy-start | bytes 2457604
  194.6 8.5 %copy-start.18 = (f32[512,1024]{1,0:T(8,128)S(1)}, f32[512,1024]{1,0:T(8,128)}, u32[]{:S(2)}) copy-start(f32[512,1024]{1,0:T(8,128)} %copy-done.16) | copy-start | bytes 6291460
  194.7 26.6 %collective-permute-start.19 = (bf16[1920,256]{1,0:T(8,128)(2,1)S(1)}, bf16[1920,256]{1,0:T(8,128)(2,1)S(1)}, u32[]{:S(2)}, u32[]{:S(2)}) collective-permute-start(bf16[1920,256]{1,0:T(8,128)(2,1)S(1)} %pad_maximum_fusion.8), channel_id=1, source_target_pairs={{0,4},{4,0},{1,5},{5,1},{2,6},{6,2},{3,7},{7,3},{8,12},{12,8},{9,1... | collective-permute-start | bytes 2949128 | tf_op jit(solution)/shard_map/ppermute | solution.py:482
  196.1 7.1 %copy-start.46 = (f32[1024]{0:T(1024)S(1)}, f32[1024]{0:T(1024)}, u32[]{:S(2)}) copy-start(f32[1024]{0:T(1024)} %param.29) | copy-start | bytes 12292
  198.9 18.1 %collective-permute-start.24 = (bf16[640,256]{1,0:T(8,128)(2,1)S(1)}, bf16[640,256]{1,0:T(8,128)(2,1)S(1)}, u32[]{:S(2)}, u32[]{:S(2)}) collective-permute-start(bf16[640,256]{1,0:T(8,128)(2,1)S(1)} %bitcast.448), channel_id=1, source_target_pairs={{0,16},{8,24},{16,0},{24,8},{1,17},{9,25},{17,1},{25,9},{2,18},{10... | collective-permute-start | bytes 983048 | tf_op jit(solution)/shard_map/ppermute | solution.py:600
  202.7 18.6 %collective-permute-start.23 = (bf16[992,256]{1,0:T(8,128)(2,1)S(1)}, bf16[992,256]{1,0:T(8,128)(2,1)S(1)}, u32[]{:S(2)}, u32[]{:S(2)}) collective-permute-start(bf16[992,256]{1,0:T(8,128)(2,1)S(1)} %bitcast.434), channel_id=1, source_target_pairs={{0,8},{8,0},{16,24},{24,16},{1,9},{9,1},{17,25},{25,17},{2,10},{10... | collective-permute-start | bytes 1523720 | tf_op jit(solution)/shard_map/ppermute | solution.py:600
  224.6 12.0 %collective-permute-start.28 = (bf16[656,256]{1,0:T(8,128)(2,1)S(1)}, bf16[656,256]{1,0:T(8,128)(2,1)S(1)}, u32[]{:S(2)}, u32[]{:S(2)}) collective-permute-start(bf16[656,256]{1,0:T(8,128)(2,1)S(1)} %pad_maximum_fusion.13), channel_id=1, source_target_pairs={{0,2},{2,0},{1,3},{3,1},{4,6},{6,4},{5,7},{7,5},{8,10},{10,8},{9,1... | collective-permute-start | bytes 1007624 | tf_op jit(solution)/shard_map/ppermute | solution.py:482
  225.2 11.4 %collective-permute-start.27 = (bf16[496,256]{1,0:T(8,128)(2,1)S(1)}, bf16[496,256]{1,0:T(8,128)(2,1)S(1)}, u32[]{:S(2)}, u32[]{:S(2)}) collective-permute-start(bf16[496,256]{1,0:T(8,128)(2,1)S(1)} %fusion.14), channel_id=1, source_target_pairs={{0,16},{8,24},{16,0},{24,8},{1,17},{9,25},{17,1},{25,9},{2,18},{10... | collective-permute-start | bytes 761864 | tf_op jit(solution)/shard_map/ppermute | solution.py:600
  225.8 15.2 %collective-permute-start.26 = (bf16[800,256]{1,0:T(8,128)(2,1)S(1)}, bf16[800,256]{1,0:T(8,128)(2,1)S(1)}, u32[]{:S(2)}, u32[]{:S(2)}) collective-permute-start(bf16[800,256]{1,0:T(8,128)(2,1)S(1)} %bitcast.435), channel_id=1, source_target_pairs={{0,8},{8,0},{16,24},{24,16},{1,9},{9,1},{17,25},{25,17},{2,10},{10... | collective-permute-start | bytes 1228808 | tf_op jit(solution)/shard_map/ppermute | solution.py:600
  230.8 10.5 %copy-start.63 = (bf16[176,256]{1,0:T(8,128)(2,1)S(1)}, bf16[176,256]{1,0:T(8,128)(2,1)}, u32[]{:S(2)}) copy-start(bf16[176,256]{1,0:T(8,128)(2,1)} %get-tuple-element.211) | copy-start | bytes 270340
  230.8 10.5 %copy-start.64 = (bf16[176,256]{1,0:T(8,128)(2,1)S(1)}, bf16[176,256]{1,0:T(8,128)(2,1)}, u32[]{:S(2)}) copy-start(bf16[176,256]{1,0:T(8,128)(2,1)} %get-tuple-element.210) | copy-start | bytes 270340
  230.8 10.6 %copy-start.67 = (bf16[160,256]{1,0:T(8,128)(2,1)S(1)}, bf16[160,256]{1,0:T(8,128)(2,1)}, u32[]{:S(2)}) copy-start(bf16[160,256]{1,0:T(8,128)(2,1)} %dynamic-slice_bitcast_fusion.17) | copy-start | bytes 245764
  230.8 10.6 %copy-start.68 = (bf16[160,256]{1,0:T(8,128)(2,1)S(1)}, bf16[160,256]{1,0:T(8,128)(2,1)}, u32[]{:S(2)}) copy-start(bf16[160,256]{1,0:T(8,128)(2,1)} %dynamic-slice_bitcast_fusion.18) | copy-start | bytes 245764
  230.9 10.6 %copy-start.58 = (bf16[320,256]{1,0:T(8,128)(2,1)S(1)}, bf16[320,256]{1,0:T(8,128)(2,1)}, u32[]{:S(2)}) copy-start(bf16[320,256]{1,0:T(8,128)(2,1)} %dynamic-slice_bitcast_fusion.10) | copy-start | bytes 491524
  230.9 10.6 %copy-start.59 = (bf16[320,256]{1,0:T(8,128)(2,1)S(1)}, bf16[320,256]{1,0:T(8,128)(2,1)}, u32[]{:S(2)}) copy-start(bf16[320,256]{1,0:T(8,128)(2,1)} %dynamic-slice_bitcast_fusion.9) | copy-start | bytes 491524
  241.8 14.5 %copy-start.61 = (bf16[800,256]{1,0:T(8,128)(2,1)S(1)}, bf16[800,256]{1,0:T(8,128)(2,1)}, u32[]{:S(2)}) copy-start(bf16[800,256]{1,0:T(8,128)(2,1)} %copy-done.60) | copy-start | bytes 1228804
  241.8 13.4 %collective-permute-start.30 = (bf16[1152,256]{1,0:T(8,128)(2,1)S(1)}, bf16[1152,256]{1,0:T(8,128)(2,1)S(1)}, u32[]{:S(2)}, u32[]{:S(2)}) collective-permute-start(bf16[1152,256]{1,0:T(8,128)(2,1)S(1)} %slice_dynamic-update-slice_fusion), channel_id=1, source_target_pairs={{0,2},{2,0},{1,3},{3,1},{4,6},{6,4},{5,7},{7,5},{8,10},{10,8},{9,1... | collective-permute-start | bytes 1769480 | tf_op jit(solution)/shard_map/ppermute | solution.py:482
  242.5 9.0 %collective-permute-start.29 = (bf16[400,256]{1,0:T(8,128)(2,1)S(1)}, bf16[400,256]{1,0:T(8,128)(2,1)S(1)}, u32[]{:S(2)}, u32[]{:S(2)}) collective-permute-start(bf16[400,256]{1,0:T(8,128)(2,1)S(1)} %fusion.18), channel_id=1, source_target_pairs={{0,16},{8,24},{16,0},{24,8},{1,17},{9,25},{17,1},{25,9},{2,18},{10... | collective-permute-start | bytes 614408 | tf_op jit(solution)/shard_map/ppermute | solution.py:600
  256.3 3.2 %collective-permute-start.32 = (bf16[2,1152,256]{2,1,0:T(8,128)(2,1)}, bf16[2,1152,256]{2,1,0:T(8,128)(2,1)}, u32[]{:S(2)}, u32[]{:S(2)}) collective-permute-start(bf16[2,1152,256]{2,1,0:T(8,128)(2,1)} %pad_maximum_fusion.3), channel_id=1, source_target_pairs={{0,1},{1,0},{2,3},{3,2},{4,5},{5,4},{6,7},{7,6},{8,9},{9,8},{10,11... | collective-permute-start | bytes 3538952 | tf_op jit(solution)/shard_map/ppermute | solution.py:485
  257.3 8.2 %collective-permute-start.31 = (bf16[400,256]{1,0:T(8,128)(2,1)S(1)}, bf16[400,256]{1,0:T(8,128)(2,1)S(1)}, u32[]{:S(2)}, u32[]{:S(2)}) collective-permute-start(bf16[400,256]{1,0:T(8,128)(2,1)S(1)} %fusion.11), channel_id=1, source_target_pairs={{0,2},{2,0},{1,3},{3,1},{4,6},{6,4},{5,7},{7,5},{8,10},{10,8},{9,1... | collective-permute-start | bytes 614408 | tf_op jit(solution)/shard_map/ppermute | solution.py:482
  265.6 1.8 collective-permute-start.33
  (43 other events, 110.1 us)
